TPU v7x, 32 devices: a whole 2x2x4 slice. The times are simulated.
32 devices in a mesh: shard: 4 (over y, core), seq: 8 (over z, x).
Axes of the slice: x: 2, y: 2, z: 4, core: 2. Of those that a mesh axis runs over, the one named last changes fastest.
Arguments:
- tokens: bfloat16 [2, 4, 4096, 1024], P(None, 'shard', 'seq'), may hold values from -6 to 6
- cotangent: bfloat16 [2, 4, 4096, 1024], P(None, 'shard', 'seq'), may hold values from -6 to 6
- lengths: int32 [2, 4], P(None, 'shard'), may hold values from 1024 to 4096
- variates: int32 [2, 4, 4096], P(None, 'shard', 'seq'), may hold values from 0 to 7
- positions: int32 [2, 4, 4096], P(None, 'shard', 'seq'), may hold values from 0 to 4095
- attn_gain: float32 [1024], replicated, may hold values from 0.5 to 1.5
- w_query: bfloat16 [1024, 1024], P('shard'), may hold values from -0.1875 to 0.1875
- w_key: bfloat16 [1024, 1024], P('shard'), may hold values from -0.1875 to 0.1875
- w_value: bfloat16 [1024, 1024], P('shard'), may hold values from -0.1875 to 0.1875
- w_out: bfloat16 [1024, 1024], P('shard'), may hold values from -2 to 2
- bias_table: float32 [16, 2], replicated, may hold values from -3 to 3
- ffn_gain: float32 [1024], replicated, may hold values from 0.5 to 1.5
- w_gate: bfloat16 [1024, 4096], P('shard'), may hold values from -0.1875 to 0.1875
- w_up: bfloat16 [1024, 4096], P('shard'), may hold values from -0.1875 to 0.1875
- w_down: bfloat16 [4096, 1024], P('shard'), may hold values from -0.09375 to 0.09375
Outputs:
- output: bfloat16 [2, 4, 4096, 1024], P(None, 'shard', 'seq')
- grad_tokens: bfloat16 [2, 4, 4096, 1024], P(None, 'shard', 'seq')
- grad_attn_gain: float32 [1024], replicated
- grad_query: float32 [1024, 1024], P(('shard', 'seq'))
- grad_key: float32 [1024, 1024], P(('shard', 'seq'))
- grad_value: float32 [1024, 1024], P(('shard', 'seq'))
- grad_out: float32 [1024, 1024], P(('shard', 'seq'))
- grad_bias: float32 [16, 2], replicated
- grad_ffn_gain: float32 [1024], replicated
- grad_gate: float32 [1024, 4096], P(('shard', 'seq'))
- grad_up: float32 [1024, 4096], P(('shard', 'seq'))
- grad_down: float32 [4096, 1024], P(('shard', 'seq'))
All inputs are finite; a program needn't handle non-finite values.
Results may differ from a plain program's by a relative error of at most 0.015.
Values may be sent and summed in bfloat16 or wider, within the bound.
A program may use at most 448 MiB of HBM per device.

v0:
```python
import functools
import math

import jax
import jax.numpy as jnp
from jax import lax
from jax.experimental import pallas as pl
from jax.experimental.pallas import tpu as pltpu
from jax.sharding import PartitionSpec as P

EPSILON = 1e-06
ROTARY_BASE = 10000.0
LOG2E = 1.4426950408889634
LN2 = 0.6931471805599453
CLASSES = 8
AUX = 16
COVER = 16
EXTRA = 32
MASKED = -1.5e9
FAR = 1e30
F32 = jnp.float32
BF16 = jnp.bfloat16


def dot(a, b):
    return jnp.dot(a, b, preferred_element_type=F32)


def contract(a, b, da, db):
    return lax.dot_general(a, b, (((da,), (db,)), ((), ())), preferred_element_type=F32)


def pieces(x):
    high = x.astype(BF16).astype(F32)
    rest = x - high
    mid = rest.astype(BF16).astype(F32)
    low = (rest - mid).astype(BF16).astype(F32)
    return high, mid, low


def one_hot(row):
    classes = lax.broadcasted_iota(jnp.int32, (CLASSES, row.shape[1]), 0).astype(F32)
    return jnp.where(classes == row, 1.0, 0.0)


def rows_of(values, width):
    index = lax.broadcasted_iota(jnp.int32, (8, width), 0)
    out = jnp.zeros((8, width), F32)
    for at, value in enumerate(values):
        out = jnp.where(index == at, value, out)
    return out


def key_extra(row, start, length, other, same):
    width = row.shape[1]
    hot = one_hot(row)
    step = pieces(jnp.full((1, width), same - other, F32))
    base = pieces(jnp.full((1, width), other, F32))
    index = start + lax.broadcasted_iota(jnp.int32, (1, width), 1)
    mask = jnp.where(index < length, 0.0, MASKED)
    tail = rows_of(base + (mask, 1.0, 1.0, 1.0), width)
    return jnp.concatenate([hot * step[0], hot * step[1], hot * step[2], tail], axis=0).astype(BF16)


def query_extra(row, shift):
    hot = one_hot(row)
    tail = rows_of((1.0, 1.0, 1.0, 1.0) + shift, row.shape[1])
    return jnp.concatenate([hot, hot, hot, tail], axis=0).astype(BF16)


def forward_kernel(
    shape, len_ref, bias_ref, x_ref, ids_ref, *rest
):
    local, head_dim, block, aliased = shape
    if aliased:
        rest = rest[1:]
    mixed_ref, lse_ref, keys, vals, query, score, peak, total = rest
    count, _, width = x_ref.shape
    sub = block // width
    step = pl.program_id(0)
    length = len_ref[0]
    other = bias_ref[local, 0] * LOG2E
    same = bias_ref[local, 1] * LOG2E

    @pl.when(step == 0)
    def _():
        for b in range(count):
            at = pl.ds(b * width, width)
            row = ids_ref[b, 0:1, :].astype(F32)
            extra = key_extra(row, b * width, length, other, same)
            full = jnp.concatenate([x_ref[b, head_dim : 2 * head_dim, :], extra], axis=0)
            keys[at, :] = full.T
            vals[0:head_dim, at] = x_ref[b, 2 * head_dim : 3 * head_dim, :]
        vals[head_dim:, :] = jnp.ones((16, vals.shape[1]), BF16)

    used = pl.cdiv(length, block)
    inside = step * block < length

    @pl.when(jnp.logical_not(inside))
    def _():
        mixed_ref[...] = jnp.zeros_like(mixed_ref)
        lse_ref[...] = jnp.full(lse_ref.shape, FAR, F32)

    @pl.when(inside)
    def _():
        for b in range(sub):
            at = slice(b * width, (b + 1) * width)
            row = ids_ref[step * sub + b, 0:1, :].astype(F32)
            query[0:head_dim, at] = x_ref[step * sub + b, 0:head_dim, :]
            query[head_dim:, at] = query_extra(row, (0.0, 0.0, 0.0))
        peak[...] = jnp.full(peak.shape, -FAR, F32)
        total[...] = jnp.zeros_like(total)

        def span(j):
            return pl.ds(pl.multiple_of(j * block, block), block)

        def scores_of(j):
            return dot(keys[span(j), :], query[...])

        def one(j, now, ahead):
            if ahead:
                score[1 - now] = scores_of(j + 1)
            current = score[now]
            before = peak[...]
            top = jnp.maximum(before, jnp.max(current, axis=0, keepdims=True))
            weight = jnp.exp2(current - top).astype(BF16)
            peak[...] = top
            total[...] = total[...] * jnp.exp2(before - top) + dot(vals[:, span(j)], weight)

        score[0] = scores_of(0)
        pairs = (used - 1) // 2

        def pair(j, carry):
            one(2 * j, 0, True)
            one(2 * j + 1, 1, True)
            return carry

        lax.fori_loop(0, pairs, pair, 0)
        last = 2 * pairs

        @pl.when(used - last == 1)
        def _():
            one(last, 0, False)

        @pl.when(used - last == 2)
        def _():
            one(last, 0, True)
            one(last + 1, 1, False)

        mass = total[head_dim : head_dim + 1, :]
        mixed = (total[0:head_dim, :] / mass).astype(BF16)
        for b in range(sub):
            mixed_ref[b] = mixed[:, b * width : (b + 1) * width]
        lse_ref[0] = peak[...] + jnp.log2(mass)


def attend_forward(x, ids, length, bias, mixed, local, heads_here, head_dim):
    count, rows, width = x.shape
    block = max(width, 512)
    seq_len = count * width
    blocks = seq_len // block
    depth = head_dim + EXTRA
    whole = pl.BlockSpec((count, rows, width), lambda i, *_: (0, 0, 0))
    operands = [length, bias, x, ids]
    in_specs = [whole, pl.BlockSpec((count, AUX, width), lambda i, *_: (0, 3 * head_dim // AUX, 0))]
    aliases = {}
    if mixed is not None:
        operands.append(mixed)
        in_specs.append(pl.BlockSpec(memory_space=pl.ANY))
        aliases = {4: 0}
    return pl.pallas_call(
        functools.partial(forward_kernel, (local, head_dim, block, mixed is not None)),
        grid_spec=pltpu.PrefetchScalarGridSpec(
            num_scalar_prefetch=2,
            grid=(blocks,),
            in_specs=in_specs,
            out_specs=[
                pl.BlockSpec((block // width, head_dim, width), lambda i, *_: (i, local, 0)),
                pl.BlockSpec((1, 1, block), lambda i, *_: (i, 0, 0)),
            ],
            scratch_shapes=[
                pltpu.VMEM((seq_len, depth), BF16),
                pltpu.VMEM((head_dim + 16, seq_len), BF16),
                pltpu.VMEM((depth, block), BF16),
                pltpu.VMEM((2, block, block), F32),
                pltpu.VMEM((1, block), F32),
                pltpu.VMEM((head_dim + 16, block), F32),
            ],
        ),
        out_shape=[
            jax.ShapeDtypeStruct((count, heads_here * head_dim, width), BF16),
            jax.ShapeDtypeStruct((blocks, 1, block), F32),
        ],
        input_output_aliases=aliases,
        compiler_params=pltpu.CompilerParams(vmem_limit_bytes=62 << 20),
        cost_estimate=pl.CostEstimate(
            flops=8 * seq_len * seq_len * 256 // COVER,
            bytes_accessed=x.size * 4,
            transcendentals=0,
        ),
        name="attend_forward",
    )(*operands)


def backward_kernel(
    shape, len_ref, bias_ref, x_ref, ids_ref, grad_ref, mixed_ref, lse_ref, out_ref, bias_out_ref,
    keys, keys_flat, vals, query, grads, query_rows, grad_rows, acc_keys, acc_vals, acc_query,
):
    local, head_dim, block = shape
    count, _, width = x_ref.shape
    sub = block // width
    step = pl.program_id(0)
    length = len_ref[0]
    other = bias_ref[local, 0] * LOG2E
    same = bias_ref[local, 1] * LOG2E

    @pl.when(step == 0)
    def _():
        ones = jnp.ones((16, width), BF16)
        for b in range(count):
            at = pl.ds(b * width, width)
            row = ids_ref[b, 0:1, :].astype(F32)
            extra = key_extra(row, b * width, length, other, same)
            here = x_ref[b, head_dim : 2 * head_dim, :]
            keys[at, :] = jnp.concatenate([here, extra], axis=0).T
            keys_flat[:, at] = here
            vals[at, :] = jnp.concatenate([x_ref[b, 2 * head_dim : 3 * head_dim, :], ones], axis=0).T
        acc_keys[...] = jnp.zeros_like(acc_keys)
        acc_vals[...] = jnp.zeros_like(acc_vals)

    used = pl.cdiv(length, block)
    inside = step * block < length

    @pl.when(jnp.logical_not(inside))
    def _():
        for b in range(sub):
            out_ref[step * sub + b, 0:head_dim, :] = jnp.zeros((head_dim, width), BF16)

    @pl.when(inside)
    def _():
        for b in range(sub):
            at = slice(b * width, (b + 1) * width)
            here = step * sub + b
            row = ids_ref[here, 0:1, :].astype(F32)
            shift = pieces(-lse_ref[step][:, at])
            grad = grad_ref[here]
            delta = jnp.sum(grad.astype(F32) * mixed_ref[here].astype(F32), axis=0, keepdims=True)
            query[0:head_dim, at] = x_ref[here, 0:head_dim, :]
            query[head_dim:, at] = query_extra(row, shift)
            grads[0:head_dim, at] = grad
            tail = rows_of(pieces(-delta), width)
            grads[head_dim:, at] = jnp.concatenate([tail, jnp.zeros_like(tail)], axis=0).astype(BF16)
        query_rows[...] = query[...].T
        grad_rows[...] = grads[...].T
        acc_query[...] = jnp.zeros_like(acc_query)

        def one(j):
            at = pl.ds(pl.multiple_of(j * block, block), block)
            probs = jnp.exp2(dot(keys[at, :], query[...]))
            grad_probs = dot(vals[at, :], grads[...])
            grad_scores = (probs * grad_probs).astype(BF16)
            acc_vals[at, :] += dot(probs.astype(BF16), grad_rows[...])
            acc_keys[at, :] += dot(grad_scores, query_rows[...])
            acc_query[...] += dot(keys_flat[:, at], grad_scores)

        def pair(j, carry):
            one(2 * j)
            one(2 * j + 1)
            return carry

        lax.fori_loop(0, used // 2, pair, 0)

        @pl.when(used % 2 == 1)
        def _():
            one(used - 1)

        grad_query = (acc_query[...] * (1.0 / math.sqrt(head_dim))).astype(BF16)
        for b in range(sub):
            out_ref[step * sub + b, 0:head_dim, :] = grad_query[:, b * width : (b + 1) * width]

    @pl.when(step == pl.num_programs(0) - 1)
    def _():
        same_total = jnp.zeros((CLASSES, width), F32)
        all_total = jnp.zeros((CLASSES, width), F32)
        for b in range(count):
            at = pl.ds(b * width, width)
            row = ids_ref[b, 0:1, :].astype(F32)
            flat = acc_keys[at, :].T
            out_ref[b, head_dim : 2 * head_dim, :] = (flat[0:head_dim] * LN2).astype(BF16)
            out_ref[b, 2 * head_dim : 3 * head_dim, :] = acc_vals[at, :].T[0:head_dim].astype(BF16)
            by_class = flat[head_dim : head_dim + CLASSES]
            all_total += by_class
            same_total += by_class * one_hot(row)
        same_sum = jnp.sum(same_total, keepdims=True)
        other_sum = jnp.sum(all_total, keepdims=True) - same_sum
        lane = lax.broadcasted_iota(jnp.int32, (8, 128), 1)
        bias_out_ref[...] = jnp.where(lane == 0, other_sum, jnp.where(lane == 1, same_sum, 0.0))


def attend_backward(x, ids, grad, mixed, lse, length, bias, local, head_dim):
    count, rows, width = x.shape
    blocks, _, block = lse.shape
    seq_len = count * width
    depth = head_dim + EXTRA

    def whole(a):
        return pl.BlockSpec(a.shape, lambda i, *_: (0,) * a.ndim)

    head_spec = pl.BlockSpec((count, head_dim, width), lambda i, *_: (0, local, 0))
    return pl.pallas_call(
        functools.partial(backward_kernel, (local, head_dim, block)),
        grid_spec=pltpu.PrefetchScalarGridSpec(
            num_scalar_prefetch=2,
            grid=(blocks,),
            in_specs=[
                whole(x),
                pl.BlockSpec((count, AUX, width), lambda i, *_: (0, 3 * head_dim // AUX, 0)),
                head_spec, head_spec, whole(lse),
            ],
            out_specs=[
                pl.BlockSpec((count, 3 * head_dim, width), lambda i, *_: (0, 0, 0)),
                pl.BlockSpec((8, 128), lambda i, *_: (0, 0)),
            ],
            scratch_shapes=[
                pltpu.VMEM((seq_len, depth), BF16),
                pltpu.VMEM((head_dim, seq_len), BF16),
                pltpu.VMEM((seq_len, head_dim + 16), BF16),
                pltpu.VMEM((depth, block), BF16),
                pltpu.VMEM((head_dim + 16, block), BF16),
                pltpu.VMEM((block, depth), BF16),
                pltpu.VMEM((block, head_dim + 16), BF16),
                pltpu.VMEM((seq_len, depth), F32),
                pltpu.VMEM((seq_len, head_dim + 16), F32),
                pltpu.VMEM((head_dim, block), F32),
            ],
        ),
        out_shape=[
            jax.ShapeDtypeStruct((count, 3 * head_dim, width), BF16),
            jax.ShapeDtypeStruct((8, 128), F32),
        ],
        compiler_params=pltpu.CompilerParams(vmem_limit_bytes=62 << 20),
        cost_estimate=pl.CostEstimate(
            flops=20 * seq_len * seq_len * 256 // COVER,
            bytes_accessed=x.size * 6,
            transcendentals=0,
        ),
        name="attend_backward",
    )(length, bias, x, ids, grad, mixed, lse)


def rotary_tables(places, half_dim):
    frequency = jnp.exp(-math.log(ROTARY_BASE) * jnp.arange(half_dim, dtype=F32) / half_dim)
    angles = places.astype(F32)[None, :] * frequency[:, None]
    return jnp.cos(angles), jnp.sin(angles)


def sigmoid_of(x):
    return 1.0 / (1.0 + jnp.exp2(x * -LOG2E))


def project_kernel(
    shape, core_ref, tokens_ref, gain_ref, query_ref, key_ref, value_ref, cos_ref, sin_ref, ids_ref, flat_ref, *rest
):
    here, head_dim, extras, swap = shape
    outs, flat_weights = rest[:-1], rest[-1]
    pair = pl.program_id(0)

    @pl.when(pair == 0)
    def _():
        inputs = tokens_ref[0, 0].astype(F32)
        inverse = lax.rsqrt(jnp.mean(inputs * inputs, axis=-1, keepdims=True) + EPSILON)
        flat_ref[...] = (inputs * inverse * gain_ref[...]).astype(BF16).T

    flat_weights[0:128, :] = query_ref[...].T
    flat_weights[128:256, :] = key_ref[...].T
    flat_weights[256:384, :] = value_ref[...].T
    made = dot(flat_weights[...], flat_ref[...])
    cosine, sine = cos_ref[...], sin_ref[...]
    half = head_dim // 2

    def turned(start, scale):
        first = made[start : start + half]
        second = made[start + half : start + head_dim]
        both = [first * cosine - second * sine, second * cosine + first * sine]
        return (jnp.concatenate(both, axis=0) * scale).astype(BF16)

    def put(at, slot, place):
        spot = at * head_dim
        target = outs[slot]
        target[place, 0:head_dim, :] = turned(spot, LOG2E / math.sqrt(head_dim))
        target[place, head_dim : 2 * head_dim, :] = turned(128 + spot, 1.0)
        target[place, 2 * head_dim : 3 * head_dim, :] = made[256 + spot : 256 + spot + head_dim].astype(BF16)
        if extras[slot]:
            target[place, 3 * head_dim :, :] = jnp.broadcast_to(ids_ref[...], (AUX, ids_ref.shape[1])).astype(BF16)

    if swap:
        for core in range(2):

            @pl.when(core_ref[0] == core)
            def _():
                put(core, 0, 0)
                put(1 - core, 1, 0)

    else:
        for at in range(128 // head_dim):
            put(at, at % here, 0 if here > 1 else at)


def project(core, tokens, unit, gain, weights, cosine, sine, ids, count, here, head_dim, swap):
    width, model = tokens.shape[2:]
    heads = count * here
    pairs = heads * head_dim // 128
    per = 128 // head_dim // here
    extras = [h == (1 if swap else 0) for h in range(here)]

    def fixed(a):
        return pl.BlockSpec(a.shape, lambda p: (0,) * a.ndim)

    weight_specs = [pl.BlockSpec((model, 128), lambda p, i=i: (0, i * pairs + p)) for i in range(3)]
    return pl.pallas_call(
        functools.partial(project_kernel, (here, head_dim, extras, swap)),
        grid=(pairs,),
        in_specs=[
            pl.BlockSpec(memory_space=pltpu.SMEM),
            pl.BlockSpec((1, 1, width, model), lambda p: unit + (0, 0)),
            fixed(gain), *weight_specs, fixed(cosine), fixed(sine), fixed(ids),
        ],
        out_specs=[pl.BlockSpec((model, width), lambda p: (0, 0))]
        + [pl.BlockSpec((per, 3 * head_dim + AUX * e, width), lambda p: (p, 0, 0)) for e in extras],
        out_shape=[jax.ShapeDtypeStruct((model, width), BF16)]
        + [jax.ShapeDtypeStruct((count, 3 * head_dim + AUX * e, width), BF16) for e in extras],
        scratch_shapes=[pltpu.VMEM((384, model), BF16)],
        compiler_params=pltpu.CompilerParams(vmem_limit_bytes=62 << 20),
        cost_estimate=pl.CostEstimate(
            flops=6 * width * model * model // COVER, bytes_accessed=12 * model * model, transcendentals=0
        ),
        name="project",
    )(core, tokens, gain, weights, weights, weights, cosine, sine, ids)


def middle_kernel(
    shape, info_ref, mixed_ref, tokens_ref, cot_ref, out_w_ref, gain_ref, gate_w_ref, up_w_ref, down_w_ref, *rest
):
    head_dim, aliased = shape
    if aliased:
        rest = rest[1:]
    (
        output_ref, ordered_ref, flat_ref, hidden_ref, grad_gate_ref, grad_up_ref, grad_ffn_ref, grad_res_ref,
        grad_attn_ref, grad_mixed_ref, gain_out_ref, normed, residual, ffn_out, grad_normed, slots,
    ) = rest
    core = info_ref[2]
    step = pl.program_id(0)
    width = normed.shape[0]

    def valid():
        index = info_ref[1] + lax.broadcasted_iota(jnp.int32, (width, 1), 0)
        return jnp.where(index < info_ref[0], 1.0, 0.0)

    def inverse_of(x):
        return lax.rsqrt(jnp.mean(x * x, axis=-1, keepdims=True) + EPSILON)

    def head_rows(pair, slot):
        head = 2 * pair + (core if slot == 0 else 1 - core)
        return pl.ds(pl.multiple_of(head * head_dim, head_dim), head_dim)

    def slot_rows(pair, slot):
        return slice((2 * pair + slot) * head_dim, (2 * pair + slot + 1) * head_dim)

    spots = [(pair, slot) for pair in range(mixed_ref.shape[0] // head_dim // 2) for slot in range(2)]

    @pl.when(step == 0)
    def _():
        for spot in spots:
            ordered_ref[head_rows(*spot), :] = mixed_ref[slot_rows(*spot), :]
        inputs = tokens_ref[0, 0].astype(F32) + dot(ordered_ref[...].T, out_w_ref[...])
        residual[...] = inputs
        made = (inputs * inverse_of(inputs) * gain_ref[...]).astype(BF16)
        normed[...] = made
        flat_ref[...] = made.T
        grad_ffn_ref[...] = (cot_ref[0, 0].astype(F32) * valid()).astype(BF16)
        ffn_out[...] = jnp.zeros_like(ffn_out)
        grad_normed[...] = jnp.zeros_like(grad_normed)

    gate = dot(normed[...], gate_w_ref[...])
    up = dot(normed[...], up_w_ref[...])
    grad_hidden = contract(grad_ffn_ref[...], down_w_ref[...], 1, 1)
    sigmoid = sigmoid_of(gate)
    silu = gate * sigmoid
    hidden = (silu * up).astype(BF16)
    grad_gate = (grad_hidden * up * (sigmoid + silu * (1.0 - sigmoid))).astype(BF16)
    grad_up = (grad_hidden * silu).astype(BF16)
    hidden_ref[...] = hidden.T
    grad_gate_ref[...] = grad_gate
    grad_up_ref[...] = grad_up
    ffn_out[...] += dot(hidden, down_w_ref[...])
    grad_normed[...] += contract(grad_gate, gate_w_ref[...], 1, 1) + contract(grad_up, up_w_ref[...], 1, 1)

    @pl.when(step == pl.num_programs(0) - 1)
    def _():
        keep = valid()
        kept = residual[...]
        output_ref[0, 0] = ((kept + ffn_out[...]) * keep).astype(BF16)
        inverse = inverse_of(kept)
        scaled = grad_normed[...] * gain_ref[...]
        mean = jnp.mean(scaled * kept, axis=-1, keepdims=True)
        grad = cot_ref[0, 0].astype(F32) * keep
        grad = grad + (inverse * scaled - kept * (inverse * inverse * inverse) * mean)
        gain_out_ref[...] = jnp.sum(grad_normed[...] * kept * inverse, axis=0, keepdims=True)
        grad_res_ref[...] = grad
        low = grad.astype(BF16)
        grad_attn_ref[...] = low
        slots[...] = contract(out_w_ref[...], low, 1, 1).astype(BF16)
        for spot in spots:
            grad_mixed_ref[slot_rows(*spot), :] = slots[head_rows(*spot), :]


def middle_part(info, mixed, tokens, cotangent, unit, weights, gain, head_dim, output):
    width, model = tokens.shape[2:]
    out_w, gate_w, up_w, down_w = weights
    ffn = gate_w.shape[1]
    block = 512

    def fixed(a):
        return pl.BlockSpec(a.shape, lambda f, *_: (0,) * a.ndim)

    def one(*shape):
        return pl.BlockSpec(shape, lambda f, *_: (0,) * len(shape))

    token_spec = pl.BlockSpec((1, 1, width, model), lambda f, *_: unit + (0, 0))
    operands = [info, mixed, tokens, cotangent, out_w, gain, gate_w, up_w, down_w]
    in_specs = [
        fixed(mixed), token_spec, token_spec, fixed(out_w), fixed(gain),
        pl.BlockSpec((model, block), lambda f, *_: (0, f)),
        pl.BlockSpec((model, block), lambda f, *_: (0, f)),
        pl.BlockSpec((block, model), lambda f, *_: (f, 0)),
    ]
    aliases = {}
    if output is not None:
        aliases = {len(operands): 0}
        operands.append(output)
        in_specs.append(pl.BlockSpec(memory_space=pl.ANY))
    struct = jax.ShapeDtypeStruct
    return pl.pallas_call(
        functools.partial(middle_kernel, (head_dim, output is not None)),
        grid_spec=pltpu.PrefetchScalarGridSpec(
            num_scalar_prefetch=1,
            grid=(ffn // block,),
            in_specs=in_specs,
            out_specs=[
                token_spec, one(model, width), one(model, width),
                pl.BlockSpec((block, width), lambda f, *_: (f, 0)),
                pl.BlockSpec((width, block), lambda f, *_: (0, f)),
                pl.BlockSpec((width, block), lambda f, *_: (0, f)),
                one(width, model), one(width, model), one(width, model), one(model, width), one(1, model),
            ],
            scratch_shapes=[
                pltpu.VMEM((width, model), BF16),
                pltpu.VMEM((width, model), F32),
                pltpu.VMEM((width, model), F32),
                pltpu.VMEM((width, model), F32),
                pltpu.VMEM((model, width), BF16),
            ],
        ),
        out_shape=[
            struct(tokens.shape, BF16), struct((model, width), BF16), struct((model, width), BF16),
            struct((ffn, width), BF16),
            struct((width, ffn), BF16), struct((width, ffn), BF16), struct((width, model), BF16),
            struct((width, model), F32), struct((width, model), BF16), struct((model, width), BF16),
            struct((1, model), F32),
        ],
        input_output_aliases=aliases,
        compiler_params=pltpu.CompilerParams(vmem_limit_bytes=62 << 20),
        cost_estimate=pl.CostEstimate(
            flops=12 * width * model * ffn // COVER, bytes_accessed=8 * model * ffn, transcendentals=0
        ),
        name="middle_part",
    )(*operands)


def final_kernel(
    shape, core_ref, tokens_ref, grad_res_ref, gain_ref, query_ref, key_ref, value_ref, cos_ref, sin_ref, *rest
):
    here, head_dim, aliased = shape
    back = rest[:here]
    rest = rest[here:]
    if aliased:
        rest = rest[1:]
    out_ref, grad_q_ref, grad_k_ref, grad_v_ref, gain_out_ref, total = rest
    step = pl.program_id(0)
    cosine, sine = cos_ref[...], sin_ref[...]
    half = head_dim // 2

    def turned(x):
        first, second = x[:half].astype(F32), x[half:].astype(F32)
        return jnp.concatenate(
            [first * cosine + second * sine, second * cosine - first * sine], axis=0
        ).astype(BF16)

    for at in range(256 // head_dim):
        head = at
        if here == 2:
            head = at // 2 * 2 + (core_ref[0] if at % 2 == 0 else 1 - core_ref[0])
        place = pl.ds(pl.multiple_of(head * head_dim, head_dim), head_dim)
        part = back[at % here]
        grad_q_ref[place, :] = turned(part[at // here, 0:head_dim, :])
        grad_k_ref[place, :] = turned(part[at // here, head_dim : 2 * head_dim, :])
        grad_v_ref[place, :] = part[at // here, 2 * head_dim : 3 * head_dim, :]
    made = (
        contract(grad_q_ref[...].T, query_ref[...], 1, 1)
        + contract(grad_k_ref[...].T, key_ref[...], 1, 1)
        + contract(grad_v_ref[...].T, value_ref[...], 1, 1)
    )

    @pl.when(step == 0)
    def _():
        total[...] = made

    @pl.when(step > 0)
    def _():
        total[...] += made

    @pl.when(step == pl.num_programs(0) - 1)
    def _():
        inputs = tokens_ref[0, 0].astype(F32)
        inverse = lax.rsqrt(jnp.mean(inputs * inputs, axis=-1, keepdims=True) + EPSILON)
        scaled = total[...] * gain_ref[...]
        mean = jnp.mean(scaled * inputs, axis=-1, keepdims=True)
        grad = inverse * scaled - inputs * (inverse * inverse * inverse) * mean
        out_ref[0, 0] = (grad_res_ref[...] + grad).astype(BF16)
        gain_out_ref[...] = jnp.sum(total[...] * inputs * inverse, axis=0, keepdims=True)


def final_part(core, tokens, unit, grad_res, gain, weights, cosine, sine, back, head_dim, output):
    width, model = tokens.shape[2:]
    here = len(back)
    steps = model // 256

    def fixed(a):
        return pl.BlockSpec(a.shape, lambda c: (0,) * a.ndim)

    token_spec = pl.BlockSpec((1, 1, width, model), lambda c: unit + (0, 0))
    weight_specs = [pl.BlockSpec((model, 256), lambda c, i=i: (0, i * steps + c)) for i in range(3)]
    row_spec = pl.BlockSpec((256, width), lambda c: (c, 0))
    operands = [core, tokens, grad_res, gain, weights, weights, weights, cosine, sine, *back]
    in_specs = [
        pl.BlockSpec(memory_space=pltpu.SMEM), token_spec, fixed(grad_res), fixed(gain), *weight_specs,
        fixed(cosine), fixed(sine),
    ] + [
        pl.BlockSpec((256 // head_dim // here, 3 * head_dim, width), lambda c: (c, 0, 0)) for _ in back
    ]
    aliases = {}
    if output is not None:
        aliases = {len(operands): 0}
        operands.append(output)
        in_specs.append(pl.BlockSpec(memory_space=pl.ANY))
    struct = jax.ShapeDtypeStruct
    return pl.pallas_call(
        functools.partial(final_kernel, (here, head_dim, output is not None)),
        grid=(steps,),
        in_specs=in_specs,
        out_specs=[token_spec, row_spec, row_spec, row_spec, pl.BlockSpec((1, model), lambda c: (0, 0))],
        out_shape=[
            struct(tokens.shape, BF16), struct((model, width), BF16), struct((model, width), BF16),
            struct((model, width), BF16), struct((1, model), F32),
        ],
        scratch_shapes=[pltpu.VMEM((width, model), F32)],
        input_output_aliases=aliases,
        compiler_params=pltpu.CompilerParams(vmem_limit_bytes=62 << 20),
        cost_estimate=pl.CostEstimate(
            flops=6 * width * model * model // COVER, bytes_accessed=12 * model * model, transcendentals=0
        ),
        name="final_part",
    )(*operands)


def picked_kernel(units, rows, places, flipped, split, table_ref, *refs):
    weights = len(places)
    lefts = refs[0:units]
    rights = refs[units : units * (1 + weights)]
    outs = refs[units * (1 + weights) : units * (1 + weights) + weights * split]
    picked = refs[units * (1 + weights) + weights * split :]

    @pl.when(pl.program_id(0) == 0)
    def _():
        for w, (start, size) in enumerate(places):
            for p in range(size):
                at = pl.ds(pl.multiple_of(table_ref[start + p] * rows, rows), rows)
                for u in range(units):
                    picked[w * units + u][p * rows : (p + 1) * rows, :] = lefts[u][at, :]

    for w in range(weights):
        total = None
        for u in range(units):
            right = rights[w * units + u][...]
            left = picked[w * units + u][...]
            made = contract(left, right, 1, 1) if flipped else dot(left, right)
            total = made if total is None else total + made
        height = total.shape[0] // split
        for i in range(split):
            outs[w * split + i][...] = total[i * height : (i + 1) * height].astype(BF16)


def picked_grads(table, places, lefts, rights, rows, flipped, split, block, name):
    units = len(lefts)
    width = lefts[0].shape[1]
    columns = rights[0].shape[0 if flipped else 1]
    in_specs = [pl.BlockSpec(a.shape, lambda n, *_: (0, 0)) for a in lefts]
    for a in rights:
        if flipped:
            in_specs.append(pl.BlockSpec((block, width), lambda n, *_: (n, 0)))
        else:
            in_specs.append(pl.BlockSpec((width, block), lambda n, *_: (0, n)))
    heights = [size * rows for _, size in places]
    return pl.pallas_call(
        functools.partial(picked_kernel, units, rows, places, flipped, split),
        grid_spec=pltpu.PrefetchScalarGridSpec(
            num_scalar_prefetch=1,
            grid=(columns // block,),
            in_specs=in_specs,
            out_specs=[
                pl.BlockSpec((height // split, block), lambda n, *_: (0, n)) for height in heights for _ in range(split)
            ],
            scratch_shapes=[pltpu.VMEM((height, width), BF16) for height in heights for _ in lefts],
        ),
        out_shape=[
            jax.ShapeDtypeStruct((height // split, columns), BF16) for height in heights for _ in range(split)
        ],
        compiler_params=pltpu.CompilerParams(vmem_limit_bytes=62 << 20),
        cost_estimate=pl.CostEstimate(
            flops=2 * units * sum(heights) * width * columns // COVER,
            bytes_accessed=4 * sum(heights) * columns,
            transcendentals=0,
        ),
        name=name,
    )(table, *lefts, *rights)


def tall_kernel(units, pieces_here, table_ref, *refs):
    keep_ref, send_ref = refs[-2:]
    total = None
    for u in range(units):
        left = [refs[u * pieces_here + i][...] for i in range(pieces_here)]
        made = dot(jnp.concatenate(left, axis=0), refs[units * pieces_here + u][...])
        total = made if total is None else total + made
    kept = pl.program_id(0) < pl.num_programs(0) // 2

    @pl.when(kept)
    def _():
        keep_ref[...] = total.astype(BF16)

    @pl.when(jnp.logical_not(kept))
    def _():
        send_ref[...] = total.astype(BF16)


def tall_grads(table, lefts, rights, rows, name):
    units = len(lefts)
    width = lefts[0].shape[1]
    columns = rights[0].shape[1]
    places = table.shape[0]
    each = 4
    middle = places // each // 2
    in_specs = []
    for _ in lefts:
        for i in range(each):
            in_specs.append(pl.BlockSpec((rows, width), lambda n, table, i=i: (table[n * each + i], 0)))
    in_specs += [pl.BlockSpec(a.shape, lambda n, *_: (0, 0)) for a in rights]
    return pl.pallas_call(
        functools.partial(tall_kernel, units, each),
        grid_spec=pltpu.PrefetchScalarGridSpec(
            num_scalar_prefetch=1,
            grid=(places // each,),
            in_specs=in_specs,
            out_specs=[
                pl.BlockSpec((each * rows, columns), lambda n, *_: (jnp.minimum(n, middle - 1), 0)),
                pl.BlockSpec((each * rows, columns), lambda n, *_: (jnp.maximum(n - middle, 0), 0)),
            ],
        ),
        out_shape=[jax.ShapeDtypeStruct((places // 2 * rows, columns), BF16)] * 2,
        compiler_params=pltpu.CompilerParams(vmem_limit_bytes=62 << 20),
        cost_estimate=pl.CostEstimate(
            flops=2 * units * places * rows * width * columns // COVER,
            bytes_accessed=2 * places * rows * columns,
            transcendentals=0,
        ),
        name=name,
    )(table, *[a for a in lefts for _ in range(each)], *rights)


def reduce_kernel(orders, count, *refs):
    streams = len(orders)
    rounds = len(orders[0])
    ins, vec_ref = refs[:streams], refs[streams]
    outs, vec_out = refs[streams + 1 : 2 * streams + 1], refs[2 * streams + 1]
    rest = refs[2 * streams + 2 :]
    works, arrivals = rest[:streams], rest[streams : 2 * streams]
    vec_work, vec_arrival, send_sem, recv_sem, vec_send, vec_recv = rest[2 * streams :]
    shard, seq = lax.axis_index("shard"), lax.axis_index("seq")

    def partner(mask):
        if mask >= count:
            step = mask // count
            return (shard + step * (1 - 2 * (shard // step % 2)), seq)
        return (shard, seq + mask * (1 - 2 * (seq // mask % 2)))

    barrier = pltpu.get_barrier_semaphore()
    for mask in orders[0]:
        pl.semaphore_signal(
            barrier, inc=1, device_id=partner(mask), device_id_type=pl.DeviceIdType.MESH
        )
    pl.semaphore_wait(barrier, rounds)

    height = ins[0].shape[0]
    halves = [height >> (r + 1) for r in range(rounds)]
    starts = [sum(halves[:r]) for r in range(rounds)]

    def copy_of(s, r):
        source = ins[s] if r == 0 else works[s]
        return pltpu.make_async_remote_copy(
            src_ref=source.at[pl.ds(halves[r], halves[r])],
            dst_ref=arrivals[s].at[pl.ds(starts[r], halves[r])],
            send_sem=send_sem.at[s, r],
            recv_sem=recv_sem.at[s, r],
            device_id=partner(orders[s][r]),
            device_id_type=pl.DeviceIdType.MESH,
        )

    def vec_copy(r):
        return pltpu.make_async_remote_copy(
            src_ref=vec_ref if r == 0 else vec_work.at[r - 1],
            dst_ref=vec_arrival.at[r],
            send_sem=vec_send.at[r],
            recv_sem=vec_recv.at[r],
            device_id=partner(orders[0][r]),
            device_id_type=pl.DeviceIdType.MESH,
        )

    for s in range(streams):
        copy_of(s, 0).start()
    vec_copy(0).start()
    for r in range(rounds):
        for s in range(streams):
            copy_of(s, r).wait_recv()
            source = ins[s] if r == 0 else works[s]
            size = halves[r]

            def added(low, high):
                mine = source[low:high].astype(F32)
                return mine + arrivals[s][starts[r] + low : starts[r] + high].astype(F32)

            if r == rounds - 1:
                outs[s][...] = added(0, size)
            else:
                works[s][size // 2 : size] = added(size // 2, size).astype(BF16)
                copy_of(s, r + 1).start()
                works[s][0 : size // 2] = added(0, size // 2).astype(BF16)
        vec_copy(r).wait_recv()
        before = vec_ref[...] if r == 0 else vec_work[r - 1]
        if r == rounds - 1:
            vec_out[...] = before + vec_arrival[r]
        else:
            vec_work[r] = before + vec_arrival[r]
            vec_copy(r + 1).start()
    for r in range(rounds):
        for s in range(streams):
            copy_of(s, r).wait_send()
        vec_copy(r).wait_send()


def reduce_rows(parts, vector, orders, count):
    streams = len(parts)
    rounds = len(orders[0])
    height, columns = parts[0].shape
    rows = height >> rounds
    vmem = pl.BlockSpec(memory_space=pltpu.VMEM)
    return pl.pallas_call(
        functools.partial(reduce_kernel, orders, count),
        in_specs=[vmem] * (streams + 1),
        out_specs=[vmem] * (streams + 1),
        out_shape=[jax.ShapeDtypeStruct((rows, columns), F32)] * streams
        + [jax.ShapeDtypeStruct(vector.shape, F32)],
        scratch_shapes=[pltpu.VMEM((height // 2, columns), BF16) for _ in parts]
        + [pltpu.VMEM((height - rows, columns), BF16) for _ in parts]
        + [
            pltpu.VMEM((rounds - 1,) + vector.shape, F32),
            pltpu.VMEM((rounds,) + vector.shape, F32),
            pltpu.SemaphoreType.DMA((streams, rounds)),
            pltpu.SemaphoreType.DMA((streams, rounds)),
            pltpu.SemaphoreType.DMA((rounds,)),
            pltpu.SemaphoreType.DMA((rounds,)),
        ],
        compiler_params=pltpu.CompilerParams(
            collective_id=0, has_side_effects=True, vmem_limit_bytes=62 << 20
        ),
        name="reduce_rows",
    )(*parts, vector)


def on_device(
    tokens, cotangent, lengths, variates, positions, attn_gain, w_query, w_key, w_value, w_out,
    bias_table, ffn_gain, w_gate, w_up, w_down,
):
    micro, seqs, width, model = tokens.shape
    heads = bias_table.shape[0]
    head_dim = model // heads
    count = lax.axis_size("seq")
    here = heads // count
    ffn = w_gate.shape[1]
    devices = lax.axis_size("shard") * count
    seq_index = lax.axis_index("seq")
    units = [(m, s) for m in range(micro) for s in range(seqs)]
    swap = here == 2 and len(units) == 2 and lax.axis_size("shard") % 2 == 0
    core = (lax.axis_index("shard") % 2 if swap else jnp.int32(0)).astype(jnp.int32).reshape(1)
    heads_here = 1 if swap else here
    first_head = seq_index * here + core[0]
    bias_here = lax.dynamic_slice_in_dim(bias_table, first_head, heads_here, 0)
    attn_row, ffn_row = attn_gain[None, :], ffn_gain[None, :]

    def gather(weight):
        return lax.all_gather(weight, "shard", axis=0, tiled=True)

    def exchange(values):
        return lax.all_to_all(values, "seq", split_axis=0, concat_axis=0, tiled=True)

    def after(value, *before):
        return lax.optimization_barrier((value,) + before)[0]

    attn_joined = gather(jnp.concatenate([w_query, w_key, w_value], axis=1))
    ffn_weights = [gather(w_out), gather(w_gate), gather(w_up), gather(w_down)]

    def permute(value, mask):
        return lax.ppermute(value, ("shard", "seq"), [(i, i ^ mask) for i in range(devices)])

    def cross(value):
        return permute(value, count)

    lengths_of = [lengths, cross(lengths)] if swap else [lengths] * here
    packed_list, flats, tables = [], [], []

    def run_project(u, token):
        m, s = units[u]
        cosine, sine = rotary_tables(positions[m, s], head_dim // 2)
        ids = after(variates[m, s].astype(F32)[None, :], *token)
        flat, *packed = project(
            core, tokens, (m, s), attn_row, attn_joined, cosine, sine, ids, count, here, head_dim, swap
        )
        flats.append(flat)
        tables.append((cosine, sine))
        packed_list.append(packed)

    sent = {}
    mixed_now = [None] * len(units)
    sums = {}
    mixed_tok = {}
    crossed, mixed_part, mixed_cross, heads_cross, back_cross = {}, {}, {}, {}, {}
    middle = [None] * len(units)
    grad_heads = {}
    state = {"output": None, "grads": None}
    packed_grads = {}
    returned = {}
    bias_terms = {}
    finals = [None] * len(units)

    def length_of(u, h, token):
        m, s = units[u]
        return after(lengths_of[h][m, s].reshape(1), *token)

    def inputs_of(u, h):
        if not swap:
            return sent[u, h], sent[u, 0]
        return (sent[u, 0], sent[u, 1]) if h == 0 else (crossed[u], crossed[u])

    def run_forward(u, h, token):
        made, sums[u, h] = attend_forward(
            *inputs_of(u, h), length_of(u, h, token), bias_here, None if swap else mixed_now[u],
            0 if swap else h, heads_here, head_dim,
        )
        if swap:
            mixed_part[u, h] = made
            if h == 1:
                mixed_cross[u] = cross(made)
        else:
            mixed_now[u] = made
        return sums[u, h]

    def run_middle(u, token):
        m, s = units[u]
        info = jnp.stack([lengths[m, s], seq_index * width, core[0]]).astype(jnp.int32)
        state["output"], mixed_tok[u], *middle[u] = middle_part(
            after(info, *token), mixed_tok[u], tokens, cotangent, (m, s), ffn_weights, ffn_row, head_dim,
            state["output"],
        )
        return middle[u][8]

    def run_backward(u, h, token):
        if swap:
            grad = grad_heads[u] if h == 0 else heads_cross[u]
            mixed = mixed_part[u, h]
        else:
            grad, mixed = grad_heads[u], mixed_now[u]
        packed_grads[u, h], both = attend_backward(
            *inputs_of(u, h), grad, mixed, sums[u, h], length_of(u, h, token), bias_here,
            0 if swap else h, head_dim,
        )
        if swap and h == 1:
            back_cross[u] = cross(packed_grads[u, h])
        bias_terms[u, h] = both
        return both

    def run_final(u, token):
        m, s = units[u]
        cosine, sine = tables[u]
        state["grads"], *finals[u] = final_part(
            core, tokens, (m, s), middle[u][5], after(attn_row, *token), attn_joined, cosine, sine,
            [returned[u, h] for h in range(here)], head_dim, state["grads"],
        )
        return finals[u][3]

    rows = model // devices
    fold = ffn // model
    tall = ffn // devices
    seq_masks = [1 << i for i in range(count.bit_length() - 1)]
    shard_masks = [count << i for i in range((devices // count).bit_length() - 1)]
    spread = shard_masks[1:]
    orders = (
        shard_masks[:1] + spread + seq_masks,
        shard_masks[:1] + seq_masks[:1] + spread + seq_masks[1:],
        shard_masks[:1] + seq_masks[1:2] + seq_masks[:1] + spread + seq_masks[2:],
    )
    direct = rows % 16 == 0 and devices == 1 << len(orders[0])

    def places_of(order):
        marks = []
        for p in range(devices):
            bits = [p >> (len(order) - 1 - i) & 1 for i in range(len(order))]
            marks.append(sum(mask for bit, mask in zip(bits, order) if bit))
        me = lax.axis_index("shard") * count + seq_index
        return me.astype(jnp.int32) ^ jnp.array(marks, jnp.int32)

    def column(index):
        return [item[index] for item in middle]

    def run_weights(token):
        if not direct:
            return [
                sum(dot(left, right) for left, right in zip(lefts, rights)).astype(BF16)
                for lefts, rights in (
                    (column(0), column(2)), (column(0), column(3)), (column(1), column(4)),
                    ([mixed_tok[u] for u in range(len(units))], column(6)),
                )
            ]
        tables = [after(places_of(order), *token) for order in orders]
        span = [(0, devices)]
        down = tall_grads(tables[2], column(1), column(4), tall, "down_grad")
        came = [permute(down[1], orders[2][0])]
        table = after(tables[0], down[0])
        gate = picked_grads(table, span, column(0), column(2), rows, False, 2, 1024, "gate_grad")
        came.append(permute(gate[1], orders[0][0]))
        table = after(tables[1], gate[0], *holder["flying"])
        up = picked_grads(table, span, column(0), column(3), rows, False, 2, 1024, "up_grad")
        came.append(permute(up[1], orders[1][0]))
        table = after(tables[2], up[0], *came[:2])
        mixed_all = [mixed_tok[u] for u in range(len(units))]
        out = picked_grads(table, span, mixed_all, column(6), rows, False, 2, 512, "out_grad")
        came.append(permute(out[1], orders[2][0]))
        kept = [down[0], gate[0], up[0], out[0]]
        masks = [orders[2], orders[0], orders[1], orders[2]]
        streams = [[keep, got, mask[1:]] for keep, got, mask in zip(kept, came, masks)]
        holder["streams"] = streams
        return out[0]

    def wide_sum(a, b):
        return a.astype(F32) + b.astype(F32)

    def advance(token):
        out = ()
        if not direct:
            return out
        for stream in holder["streams"]:
            keep, came, masks = stream
            if not masks:
                continue
            keep = after(keep, *token)
            half = keep.shape[0] // 2
            send = wide_sum(keep[half:], came[half:]).astype(BF16)
            stream[0] = wide_sum(keep[:half], came[:half]).astype(BF16)
            stream[1] = permute(send, masks[0])
            stream[2] = masks[1:]
            out = out + (send, stream[0])
        return out

    holder = {}

    def weights_work(token):
        holder["terms"] = run_weights(token)
        return holder["terms"]

    def send_packed(u, h):
        def keep(moved):
            sent[u, h] = moved
            if swap and h == 1:
                crossed[u] = cross(moved)

        return lambda: packed_list[u][h], keep

    def send_mixed(u):
        def keep(moved):
            mixed_tok[u] = moved.reshape(model, width)

        if not swap:
            return lambda: mixed_now[u], keep
        return lambda: jnp.concatenate([mixed_part[u, 0], mixed_cross[u]], axis=1), keep

    def send_heads(u):
        def keep(moved):
            grad_heads[u] = moved
            if swap:
                heads_cross[u] = cross(moved[:, head_dim:])
                pending.append(heads_cross[u])

        return lambda: middle[u][7].reshape(count, here * head_dim, width), keep

    def send_back(u, h):
        def keep(moved):
            returned[u, h] = moved

        return lambda: back_cross[u] if swap and h == 1 else packed_grads[u, h], keep

    def work_project(u):
        def work(token):
            run_project(u, token)
            return flats[u]

        return work

    def work(function, *args):
        return lambda token: function(*args, token)

    total = len(units)
    order = [(u, h) for u in range(total) for h in range(here)]
    if swap:
        steps = [
            (work_project(0), None),
            (work_project(1), send_packed(0, 1)),
            (work(run_forward, 0, 1), send_packed(0, 0)),
            (work(run_forward, 0, 0), send_packed(1, 1)),
            (work(run_forward, 1, 1), send_packed(1, 0)),
            (work(run_forward, 1, 0), send_mixed(0)),
            (work(run_middle, 0), send_mixed(1)),
            (work(run_middle, 1), send_heads(0)),
            (weights_work, send_heads(1)),
            (work(run_backward, 0, 0), None),
            (work(run_backward, 0, 1), send_back(0, 0)),
            (work(run_backward, 1, 0), send_back(0, 1)),
            (work(run_backward, 1, 1), send_back(1, 0)),
            (work(run_final, 0), send_back(1, 1)),
            (work(run_final, 1), None),
        ]
    else:
        steps = [(work_project(u), None) for u in range(total)]
        steps += [(None, send_packed(*at)) for at in order]
        for u in range(total):
            steps += [(work(run_forward, u, h), None) for h in range(here)]
            steps += [(None, send_mixed(u))]
        for u in range(total):
            steps += [(work(run_middle, u), None), (None, send_heads(u))]
        steps += [(weights_work, None)]
        for at in order:
            steps += [(work(run_backward, *at), None), (None, send_back(*at))]
        steps += [(work(run_final, u), None) for u in range(total)]

    late = [task for task, _ in steps[-2:]]
    token = ()
    pending = []
    for task, send in steps:
        done = ()
        moved = None
        waited = tuple(pending)
        pending.clear()
        if "streams" in holder:
            leaving = advance(token)
            token = token if task in late else token + leaving
        if send is not None:
            moved = exchange(after(send[0](), *token))
            done = (moved,)
        holder["flying"] = done
        if task is not None:
            done = done + (task(token),)
        if send is not None:
            send[1](after(moved, *done[1:]))
        token = done + waited
    acc_bias = jnp.concatenate(
        [sum(bias_terms[u, h] for u in range(total))[0:1, 0:2] for h in range(here)], axis=0
    )
    if swap:
        acc_bias = acc_bias[0:1] + acc_bias[1:2]
    bias_full = lax.dynamic_update_slice(
        jnp.zeros((heads, 2), F32), acc_bias, (first_head, jnp.int32(0))
    )
    gain_attn = sum(item[3][0] for item in finals)
    gain_ffn = sum(item[8][0] for item in middle)
    if direct:
        while holder["streams"][0][2]:
            advance(token)
        down_own, gate_own, up_own, out_own = [
            wide_sum(after(keep, *token), came) for keep, came, _ in holder["streams"]
        ]
        table = jnp.concatenate([places_of(order) for order in orders])
        attn_terms = picked_grads(
            table, [(i * devices, devices) for i in range(3)], flats,
            [item[i] for i in range(3) for item in finals], rows, True, 1, 256, "attn_grads",
        )
        flat = jnp.concatenate([gain_attn, gain_ffn, bias_full.reshape(-1)])
        tiles = -(-flat.shape[0] // 1024) * 8
        flat = jnp.pad(flat, (0, tiles * 128 - flat.shape[0])).reshape(tiles, 128)
        query_own, key_own, value_own, flat = reduce_rows(list(attn_terms), flat, orders, count)
        flat = flat.reshape(-1)
        gain_attn, gain_ffn = flat[:model], flat[model : 2 * model]
        bias_full = flat[2 * model : 2 * model + 2 * heads].reshape(heads, 2)
    else:

        def scatter(value):
            owned = lax.psum_scatter(value, ("shard", "seq"), scatter_dimension=0, tiled=True)
            return owned.astype(F32)

        gate_own, up_own, down_own, out_own = [scatter(value) for value in holder["terms"]]
        query_own, key_own, value_own = [
            scatter(
                sum(contract(flat, item[i], 1, 1) for flat, item in zip(flats, finals)).astype(BF16)
            )
            for i in range(3)
        ]
        gain_attn, gain_ffn, bias_full = lax.psum(
            (gain_attn, gain_ffn, bias_full), ("shard", "seq")
        )
    return (
        state["output"], state["grads"], gain_attn, query_own, key_own, value_own, out_own,
        bias_full, gain_ffn, gate_own, up_own, down_own,
    )


def solution(mesh):
    token_spec = P(None, "shard", "seq", None)
    row_spec = P("shard", None)
    in_specs = (
        token_spec, token_spec, P(None, "shard"), P(None, "shard", "seq"), P(None, "shard", "seq"),
        P(), row_spec, row_spec, row_spec, row_spec, P(), P(), row_spec, row_spec, row_spec,
    )
    owned = P(("shard", "seq"), None)
    out_specs = (
        token_spec, token_spec, P(), owned, owned, owned, owned, P(), P(), owned, owned, owned,
    )
    return jax.shard_map(
        on_device, mesh=mesh, in_specs=in_specs, out_specs=out_specs, check_vma=False
    )
```

profile of v0, /device:TPU:0, one launch (start us, length us, event | category | flops | bytes accessed | tf_op | source)
XLA Modules:
  0.0 858.4 jit_solution(11318976501493234607)
XLA Ops:
  7.2 2.6 pad_maximum_fusion
  13.8 45.5 %all-gather.6.cloned.1.call-done.query_ref.key_ref.value_ref = bf16[1024,3072]{1,0:T(8,128)(2,1)} async-done(((bf16[256,3072]{1,0:T(8,128)(2,1)}), bf16[1024,3072]{1,0:T(8,128)(2,1)}) %all-gather.6.cloned.1.call-update) | async-done | bytes 6291472 | tf_op jit(solution)/shard_map/all_gather | solution.py:920
  59.3 10.9 %project.2 = (bf16[1024,512]{1,0:T(8,128)(2,1)}, bf16[8,192,512]{2,1,0:T(8,128)(2,1)}, bf16[8,208,512]{2,1,0:T(8,128)(2,1)}) custom-call(s32[1]{0:T(128)} %bitcast.2.core_ref, bf16[2,1,512,1024]{3,2,1,0:T(8,128)(2,1)} %tokens_ref.11, f32[1,1024]{1,0:T(1,128)} %bitcast.30, bf16[1024,3072]{1,0:T(8,128)(2,1)} %all-gather.6.cloned.1.call-done.query_ref.key_ref.value_ref, ...), custom_call_target="tpu_custom_call" | custom-call | flops 201326592 | bytes 12582912 | tf_op jit(solution)/shard_map/project/pallas_call | solution.py:420
  70.2 5.5 all-to-all-start
  76.3 10.9 %project.3 = (bf16[1024,512]{1,0:T(8,128)(2,1)}, bf16[8,192,512]{2,1,0:T(8,128)(2,1)}, bf16[8,208,512]{2,1,0:T(8,128)(2,1)}) custom-call(s32[1]{0:T(128)} %bitcast.2.core_ref, bf16[2,1,512,1024]{3,2,1,0:T(8,128)(2,1)} %tokens_ref.11, f32[1,1024]{1,0:T(1,128)} %bitcast.31, bf16[1024,3072]{1,0:T(8,128)(2,1)} %all-gather.6.cloned.1.call-done.query_ref.key_ref.value_ref, ...), custom_call_target="tpu_custom_call" | custom-call | flops 201326592 | bytes 12582912 | tf_op jit(solution)/shard_map/project/pallas_call | solution.py:420
  87.3 28.7 %all-to-all-done.ids_ref = bf16[8,208,512]{2,1,0:T(8,128)(2,1)S(1)} async-done(((bf16[8,208,512]{2,1,0:T(8,128)(2,1)}), bf16[8,208,512]{2,1,0:T(8,128)(2,1)S(1)}, u32[]{:S(2)}, u32[]{:S(2)}) %all-to-all-start) | async-done | bytes 1703968 | tf_op jit(solution)/shard_map/all_to_all | solution.py:923
  115.9 4.3 all-to-all-start.1
  124.1 11.7 %attend_forward.4 = (bf16[8,64,512]{2,1,0:T(8,128)(2,1)}, f32[8,1,512]{2,1,0:T(1,128)}) custom-call(s32[1]{0:T(128)} %bitcast.8.len_ref, f32[1,2]{1,0:T(1,128)} %copy.39.bias_ref, bf16[8,208,512]{2,1,0:T(8,128)(2,1)} %collective-permute-done.1.x_ref.ids_ref, bf16[8,208,512]{2,1,0:T(8,128)(2,1)} %collective-permute-done.1.x_ref.ids_ref), custom_call_target="tpu_custom_call" | custom-call | flops 2147483648 | bytes 3407872 | tf_op jit(solution)/shard_map/attend_forward/pallas_call | solution.py:171
  135.8 21.1 %all-to-all-done.1.x_ref = bf16[8,192,512]{2,1,0:T(8,128)(2,1)} async-done(((bf16[8,192,512]{2,1,0:T(8,128)(2,1)}), bf16[8,192,512]{2,1,0:T(8,128)(2,1)}, u32[]{:S(2)}, u32[]{:S(2)}) %all-to-all-start.1) | async-done | bytes 1572896 | tf_op jit(solution)/shard_map/all_to_all | solution.py:923
  156.9 3.6 all-to-all-start.2
  161.1 18.2 %attend_forward.5 = (bf16[8,64,512]{2,1,0:T(8,128)(2,1)}, f32[8,1,512]{2,1,0:T(1,128)}) custom-call(s32[1]{0:T(128)} %bitcast.9.len_ref, f32[1,2]{1,0:T(1,128)} %copy.39.bias_ref, bf16[8,192,512]{2,1,0:T(8,128)(2,1)} %all-to-all-done.1.x_ref, bf16[8,208,512]{2,1,0:T(8,128)(2,1)} %copy-done.16), custom_call_target="tpu_custom_call" | custom-call | flops 2147483648 | bytes 3145728 | tf_op jit(solution)/shard_map/attend_forward/pallas_call | solution.py:171
  179.2 21.2 %all-to-all-done.2.ids_ref = bf16[8,208,512]{2,1,0:T(8,128)(2,1)S(1)} async-done(((bf16[8,208,512]{2,1,0:T(8,128)(2,1)}), bf16[8,208,512]{2,1,0:T(8,128)(2,1)S(1)}, u32[]{:S(2)}, u32[]{:S(2)}) %all-to-all-start.2) | async-done | bytes 1703968 | tf_op jit(solution)/shard_map/all_to_all | solution.py:923
  200.5 4.3 all-to-all-start.3
  205.4 3.7 collective-permute-done.4
  210.2 11.7 %attend_forward.6 = (bf16[8,64,512]{2,1,0:T(8,128)(2,1)}, f32[8,1,512]{2,1,0:T(1,128)}) custom-call(s32[1]{0:T(128)} %bitcast.10.len_ref, f32[1,2]{1,0:T(1,128)} %copy.39.bias_ref, bf16[8,208,512]{2,1,0:T(8,128)(2,1)} %collective-permute-done.2.x_ref.ids_ref, bf16[8,208,512]{2,1,0:T(8,128)(2,1)} %collective-permute-done.2.x_ref.ids_ref), custom_call_target="tpu_custom_call" | custom-call | flops 2147483648 | bytes 3407872 | tf_op jit(solution)/shard_map/attend_forward/pallas_call | solution.py:171
  221.9 19.5 %all-to-all-done.3.x_ref = bf16[8,192,512]{2,1,0:T(8,128)(2,1)} async-done(((bf16[8,192,512]{2,1,0:T(8,128)(2,1)}), bf16[8,192,512]{2,1,0:T(8,128)(2,1)}, u32[]{:S(2)}, u32[]{:S(2)}) %all-to-all-start.3) | async-done | bytes 1572896 | tf_op jit(solution)/shard_map/all_to_all | solution.py:923
  241.4 4.1 all-to-all-start.4
  245.6 22.5 %attend_forward.7 = (bf16[8,64,512]{2,1,0:T(8,128)(2,1)}, f32[8,1,512]{2,1,0:T(1,128)}) custom-call(s32[1]{0:T(128)} %bitcast.len_ref, f32[1,2]{1,0:T(1,128)} %copy.39.bias_ref, bf16[8,192,512]{2,1,0:T(8,128)(2,1)} %all-to-all-done.3.x_ref, bf16[8,208,512]{2,1,0:T(8,128)(2,1)} %copy-done.15), custom_call_target="tpu_custom_call" | custom-call | flops 2147483648 | bytes 3145728 | tf_op jit(solution)/shard_map/attend_forward/pallas_call | solution.py:171
  268.2 2.1 pad_maximum_fusion.1
  272.4 4.8 all-to-all-start.5
  278.5 42.3 %middle_part.2 = (bf16[2,1,512,1024]{3,2,1,0:T(8,128)(2,1)}, bf16[1024,512]{1,0:T(8,128)(2,1)}, bf16[1024,512]{1,0:T(8,128)(2,1)}, bf16[4096,512]{1,0:T(8,128)(2...) custom-call(s32[3]{0:T(128)} %add_add_fusion.1.info_ref, ...), custom_call_target="tpu_custom_call" | custom-call | flops 1610612736 | bytes 33554432 | tf_op jit(solution)/shard_map/middle_part/pallas_call | solution.py:543
  320.9 6.2 all-to-all-start.6
  329.4 42.3 %middle_part.3 = (bf16[2,1,512,1024]{3,2,1,0:T(8,128)(2,1)}, bf16[1024,512]{1,0:T(8,128)(2,1)}, bf16[1024,512]{1,0:T(8,128)(2,1)}, bf16[4096,512]{1,0:T(8,128)(2...) custom-call(s32[3]{0:T(128)} %add_add_fusion.info_ref, ...), custom_call_target="tpu_custom_call", output_to_operand_aliasing={{0}: (9, {})} | custom-call | flops 1610612736 | bytes 33554432 | tf_op jit(solution)/shard_map/middle_part/pallas_call | solution.py:543
  371.8 16.3 %down_grad.1 = (bf16[2048,1024]{1,0:T(8,128)(2,1)}, bf16[2048,1024]{1,0:T(8,128)(2,1)}) custom-call(s32[32]{0:T(128)} %broadcast_xor_fusion.2.table_ref, bf16[4096,512]{1,0:T(8,128)(2,1)} %get-tuple-element.189.refs_0_.refs_1_.refs_2_.refs_3_, bf16[4096,512]{1,0:T(8,128)(2,1)} %get-tuple-element.189.refs_0_.refs_1_.refs_2_.refs_3_, ...), custom_call_target="tpu_custom_call" | custom-call | flops 536870912 | bytes 8388608 | tf_op jit(solution)/shard_map/down_grad/pallas_call | solution.py:768
  388.1 6.2 all-to-all-start.7
  394.3 13.7 %gate_grad.1 = (bf16[512,4096]{1,0:T(8,128)(2,1)}, bf16[512,4096]{1,0:T(8,128)(2,1)}) custom-call(s32[32]{0:T(128)} %get-tuple-element.194.table_ref, bf16[1024,512]{1,0:T(8,128)(2,1)} %get-tuple-element.195.refs_0_, bf16[1024,512]{1,0:T(8,128)(2,1)} %get-tuple-element.196.refs_1_, bf16[512,4096]{1,0:T(8,128)(2,1)} %get-tuple-element.197.refs_2_, ...), custom_call_target="tpu_custom_call" | custom-call | flops 536870912 | bytes 16777216 | tf_op jit(solution)/shard_map/gate_grad/pallas_call | solution.py:714
  408.5 9.7 %all-to-all-done.7.grad_ref = bf16[8,128,512]{2,1,0:T(8,128)(2,1)S(1)} async-done(((bf16[8,128,512]{2,1,0:T(8,128)(2,1)}), bf16[8,128,512]{2,1,0:T(8,128)(2,1)S(1)}, u32[]{:S(2)}, u32[]{:S(2)}) %all-to-all-start.7) | async-done | bytes 1048608 | tf_op jit(solution)/shard_map/all_to_all | solution.py:923
  418.2 13.8 %up_grad.1 = (bf16[512,4096]{1,0:T(8,128)(2,1)}, bf16[512,4096]{1,0:T(8,128)(2,1)}) custom-call(s32[32]{0:T(128)} %get-tuple-element.200.table_ref, bf16[1024,512]{1,0:T(8,128)(2,1)} %get-tuple-element.195.refs_0_, bf16[1024,512]{1,0:T(8,128)(2,1)} %get-tuple-element.196.refs_1_, bf16[512,4096]{1,0:T(8,128)(2,1)} %get-tuple-element.201.refs_2_, ...), custom_call_target="tpu_custom_call" | custom-call | flops 536870912 | bytes 16777216 | tf_op jit(solution)/shard_map/up_grad/pallas_call | solution.py:714
  434.4 6.1 out_grad.1
  441.0 5.7 add_convert_fusion.2
  447.3 4.4 add_convert_fusion.4
  454.9 4.2 add_convert_fusion
  460.3 32.5 %attend_backward.4 = (bf16[8,192,512]{2,1,0:T(8,128)(2,1)}, f32[8,128]{1,0:T(8,128)}) custom-call(s32[1]{0:T(128)} %bitcast.9.len_ref, f32[1,2]{1,0:T(1,128)} %copy.39.bias_ref, bf16[8,192,512]{2,1,0:T(8,128)(2,1)} %all-to-all-done.1.x_ref, bf16[8,208,512]{2,1,0:T(8,128)(2,1)} %copy-done.16, bf16[8,128,512]{2,1,0:T(8,128)(2,1)} %all-to-all-done.6.grad_ref, ...), custom_call_target="tpu_custom_call" | custom-call | flops 5368709120 | bytes 4718592 | tf_op jit(solution)/shard_map/attend_backward/pallas_call | solution.py:310
  492.8 17.6 %collective-permute-done.14 = bf16[256,1024]{1,0:T(8,128)(2,1)S(1)} collective-permute-done((bf16[256,1024]{1,0:T(8,128)(2,1)}, bf16[256,1024]{1,0:T(8,128)(2,1)S(1)}, u32[]{:S(2)}, u32[]{:S(2)}) %collective-permute-start.14) | collective-permute-done | bytes 524320 | tf_op jit(solution)/shard_map/ppermute | solution.py:932
  511.3 4.6 add_convert_fusion.10
  515.9 3.6 add_convert_fusion.8
  519.5 3.5 add_convert_fusion.6
  523.1 3.6 all-to-all-start.8
  532.1 18.0 %attend_backward.5 = (bf16[8,192,512]{2,1,0:T(8,128)(2,1)}, f32[8,128]{1,0:T(8,128)}) custom-call(s32[1]{0:T(128)} %bitcast.8.len_ref, f32[1,2]{1,0:T(1,128)} %copy.39.bias_ref, bf16[8,208,512]{2,1,0:T(8,128)(2,1)} %collective-permute-done.1.x_ref.ids_ref, bf16[8,208,512]{2,1,0:T(8,128)(2,1)} %collective-permute-done.1.x_ref.ids_ref, ...), custom_call_target="tpu_custom_call" | custom-call | flops 5368709120 | bytes 5111808 | tf_op jit(solution)/shard_map/attend_backward/pallas_call | solution.py:310
  550.1 13.4 %collective-permute-start.15 = (bf16[8,192,512]{2,1,0:T(8,128)(2,1)}, bf16[8,192,512]{2,1,0:T(8,128)(2,1)}, u32[]{:S(2)}, u32[]{:S(2)}) collective-permute-start(bf16[8,192,512]{2,1,0:T(8,128)(2,1)} %get-tuple-element.227), channel_id=1, source_target_pairs={{0,8},{1,9},{2,10},{3,11},{4,12},{5,13},{6,14},{7,15},{8,0},{9,1},... | collective-permute-start | bytes 4718600 | tf_op jit(solution)/shard_map/ppermute | solution.py:932
  563.5 6.2 collective-permute-done.16
  569.7 2.9 add_convert_fusion.16
  572.6 2.7 collective-permute-done.19
  577.0 2.5 add_convert_fusion.12
  579.6 16.2 %collective-permute-done.17 = bf16[128,4096]{1,0:T(8,128)(2,1)} collective-permute-done((bf16[128,4096]{1,0:T(8,128)(2,1)}, bf16[128,4096]{1,0:T(8,128)(2,1)}, u32[]{:S(2)}, u32[]{:S(2)}) %collective-permute-start.17) | collective-permute-done | bytes 1048608 | tf_op jit(solution)/shard_map/ppermute | solution.py:932
  595.8 2.4 add_convert_fusion.14
  598.2 4.6 all-to-all-start.9
  604.8 3.4 collective-permute-start.23
  608.3 41.3 %attend_backward.6 = (bf16[8,192,512]{2,1,0:T(8,128)(2,1)}, f32[8,128]{1,0:T(8,128)}) custom-call(s32[1]{0:T(128)} %bitcast.len_ref, f32[1,2]{1,0:T(1,128)} %copy.39.bias_ref, bf16[8,192,512]{2,1,0:T(8,128)(2,1)} %all-to-all-done.3.x_ref, bf16[8,208,512]{2,1,0:T(8,128)(2,1)} %copy-done.15, bf16[8,128,512]{2,1,0:T(8,128)(2,1)} %copy-done.13, ...), custom_call_target="tpu_custom_call" | custom-call | flops 5368709120 | bytes 4718592 | tf_op jit(solution)/shard_map/attend_backward/pallas_call | solution.py:310
  649.6 2.7 add_convert_fusion.20
  653.0 2.0 add_convert_fusion.22
  656.6 2.0 add_convert_fusion.24
  658.6 5.3 all-to-all-start.10
  663.9 17.9 %attend_backward.7 = (bf16[8,192,512]{2,1,0:T(8,128)(2,1)}, f32[8,128]{1,0:T(8,128)}) custom-call(s32[1]{0:T(128)} %bitcast.10.len_ref, f32[1,2]{1,0:T(1,128)} %copy.39.bias_ref, bf16[8,208,512]{2,1,0:T(8,128)(2,1)} %collective-permute-done.2.x_ref.ids_ref, bf16[8,208,512]{2,1,0:T(8,128)(2,1)} %collective-permute-done.2.x_ref.ids_ref, ...), custom_call_target="tpu_custom_call" | custom-call | flops 5368709120 | bytes 5111808 | tf_op jit(solution)/shard_map/attend_backward/pallas_call | solution.py:310
  681.9 21.3 %collective-permute-start.24 = (bf16[8,192,512]{2,1,0:T(8,128)(2,1)}, bf16[8,192,512]{2,1,0:T(8,128)(2,1)}, u32[]{:S(2)}, u32[]{:S(2)}) collective-permute-start(bf16[8,192,512]{2,1,0:T(8,128)(2,1)} %get-tuple-element.243), channel_id=1, source_target_pairs={{0,8},{1,9},{2,10},{3,11},{4,12},{5,13},{6,14},{7,15},{8,0},{9,1},... | collective-permute-start | bytes 4718600 | tf_op jit(solution)/shard_map/ppermute | solution.py:932
  703.2 3.4 collective-permute-done.24
  706.5 5.7 all-to-all-start.11
  712.9 3.0 collective-permute-start.28
  716.0 2.8 collective-permute-start.26
  719.3 11.5 %final_part.2 = (bf16[2,1,512,1024]{3,2,1,0:T(8,128)(2,1)}, bf16[1024,512]{1,0:T(8,128)(2,1)}, bf16[1024,512]{1,0:T(8,128)(2,1)}, bf16[1024,512]{1,0:T(8,128)(2,1)}, f32[1,1024]{1,0:T(1,128)}) custom-call(s32[1]{0:T(128)} %bitcast.2.core_ref, bf16[2,1,512,1024]{3,2,1,0:T(8,128)(2,1)} %tokens_ref.11, f32[512,1024]{1,0:T(8,128)} %get-tuple-element.248.grad_res_ref, ...), custom_call_target="tpu_custom_call" | custom-call | flops 201326592 | bytes 12582912 | tf_op jit(solution)/shard_map/final_part/pallas_call | solution.py:657
  730.8 38.3 %all-to-all-done.11.rest_1_ = bf16[8,192,512]{2,1,0:T(8,128)(2,1)} async-done(((bf16[8,192,512]{2,1,0:T(8,128)(2,1)}), bf16[8,192,512]{2,1,0:T(8,128)(2,1)}, u32[]{:S(2)}, u32[]{:S(2)}) %all-to-all-start.11) | async-done | bytes 1572896 | tf_op jit(solution)/shard_map/all_to_all | solution.py:923
  769.0 11.5 %final_part.3 = (bf16[2,1,512,1024]{3,2,1,0:T(8,128)(2,1)}, bf16[1024,512]{1,0:T(8,128)(2,1)}, bf16[1024,512]{1,0:T(8,128)(2,1)}, bf16[1024,512]{1,0:T(8,128)(2,1)}, f32[1,1024]{1,0:T(1,128)}) custom-call(s32[1]{0:T(128)} %bitcast.2.core_ref, bf16[2,1,512,1024]{3,2,1,0:T(8,128)(2,1)} %tokens_ref.11, ...), custom_call_target="tpu_custom_call", output_to_operand_aliasing={{0}: (11, {})} | custom-call | flops 201326592 | bytes 12582912 | tf_op jit(solution)/shard_map/final_part/pallas_call | solution.py:657
  783.7 11.9 %attn_grads.1 = (bf16[1024,1024]{1,0:T(8,128)(2,1)}, bf16[1024,1024]{1,0:T(8,128)(2,1)}, bf16[1024,1024]{1,0:T(8,128)(2,1)}) custom-call(s32[96]{0:T(128)} %pad_add_fusion.table_ref, bf16[1024,512]{1,0:T(8,128)(2,1)} %get-tuple-element.144.refs_0_, bf16[1024,512]{1,0:T(8,128)(2,1)} %get-tuple-element.151.refs_1_, ...), custom_call_target="tpu_custom_call" | custom-call | flops 402653184 | bytes 12582912 | tf_op jit(solution)/shard_map/attn_grads/pallas_call | solution.py:714
  795.6 47.6 %reduce_rows.1 = (f32[32,1024]{1,0:T(8,128)}, f32[32,1024]{1,0:T(8,128)}, f32[32,1024]{1,0:T(8,128)}, f32[24,128]{1,0:T(8,128)}) custom-call(bf16[1024,1024]{1,0:T(8,128)(2,1)} %get-tuple-element.264.refs_0_, bf16[1024,1024]{1,0:T(8,128)(2,1)} %get-tuple-element.265.refs_1_, bf16[1024,1024]{1,0:T(8,128)(2,1)} %get-tuple-element.266.refs_2_, ...), custom_call_target="tpu_custom_call" | custom-call | tf_op jit(solution)/shard_map/reduce_rows/pallas_call | solution.py:876
  (193 shorter events, 50.1 us)
Async XLA Ops:
  7.2 113.6 %copy-start = (f32[16,2]{0,1:T(2,128)S(1)}, f32[16,2]{0,1:T(2,128)}, u32[]{:S(2)}) copy-start(f32[16,2]{0,1:T(2,128)} %param.31) | copy-start | bytes 388
  7.2 52.1 %all-gather.6.cloned.1.call-start = ((), (), s32[]{:S(2)}) async-start(), calls=%async_computation.12 | async-start | bytes 7864320 | tf_op jit(solution)/shard_map/all_gather | solution.py:920
  9.9 268.6 %all-gather.8.cloned.1.call-start = ((), (), s32[]{:S(2)}) async-start(), calls=%async_computation.13 | async-start | bytes 2621440 | tf_op jit(solution)/shard_map/all_gather | solution.py:920
  10.7 267.8 %all-gather.10.cloned.1.call-start = ((), (), s32[]{:S(2)}) async-start(), calls=%async_computation.14 | async-start | bytes 10485760 | tf_op jit(solution)/shard_map/all_gather | solution.py:920
  11.4 267.1 %all-gather.12.cloned.1.call-start = ((), (), s32[]{:S(2)}) async-start(), calls=%async_computation.15 | async-start | bytes 10485760 | tf_op jit(solution)/shard_map/all_gather | solution.py:920
  70.2 45.7 %all-to-all-start = ((bf16[8,208,512]{2,1,0:T(8,128)(2,1)}), bf16[8,208,512]{2,1,0:T(8,128)(2,1)S(1)}, u32[]{:S(2)}, u32[]{:S(2)}) async-start(bf16[8,208,512]{2,1,0:T(8,128)(2,1)} %get-tuple-element.150), calls=%async_computation | async-start | bytes 3407872 | tf_op jit(solution)/shard_map/all_to_all | solution.py:923
  75.7 202.8 %all-gather.14.cloned.1.call-start = ((), (), s32[]{:S(2)}) async-start(), calls=%async_computation.16 | async-start | bytes 10485760 | tf_op jit(solution)/shard_map/all_gather | solution.py:920
  87.3 33.0 %copy-start.39 = (s32[2,1]{0,1:T(1,128)S(1)}, s32[2,1]{0,1:T(1,128)}, u32[]{:S(2)}) copy-start(s32[2,1]{0,1:T(1,128)} %param.23) | copy-start | bytes 28
  115.9 40.9 %all-to-all-start.1 = ((bf16[8,192,512]{2,1,0:T(8,128)(2,1)}), bf16[8,192,512]{2,1,0:T(8,128)(2,1)}, u32[]{:S(2)}, u32[]{:S(2)}) async-start(bf16[8,192,512]{2,1,0:T(8,128)(2,1)} %get-tuple-element.152), calls=%async_computation.1 | async-start | bytes 3145728 | tf_op jit(solution)/shard_map/all_to_all | solution.py:923
  120.2 3.9 collective-permute-start.1
  120.3 3.2 collective-permute-start
  156.9 43.6 %all-to-all-start.2 = ((bf16[8,208,512]{2,1,0:T(8,128)(2,1)}), bf16[8,208,512]{2,1,0:T(8,128)(2,1)S(1)}, u32[]{:S(2)}, u32[]{:S(2)}) async-start(bf16[8,208,512]{2,1,0:T(8,128)(2,1)} %get-tuple-element.156), calls=%async_computation.2 | async-start | bytes 3407872 | tf_op jit(solution)/shard_map/all_to_all | solution.py:923
  179.2 29.8 %copy-start.20 = (bf16[8,64,512]{2,1,0:T(8,128)(2,1)S(1)}, bf16[8,64,512]{2,1,0:T(8,128)(2,1)}, u32[]{:S(2)}) copy-start(bf16[8,64,512]{2,1,0:T(8,128)(2,1)} %get-tuple-element.168.mixed_ref) | copy-start | bytes 1572868
  200.5 40.9 %all-to-all-start.3 = ((bf16[8,192,512]{2,1,0:T(8,128)(2,1)}), bf16[8,192,512]{2,1,0:T(8,128)(2,1)}, u32[]{:S(2)}, u32[]{:S(2)}) async-start(bf16[8,192,512]{2,1,0:T(8,128)(2,1)} %get-tuple-element.160), calls=%async_computation.3 | async-start | bytes 3145728 | tf_op jit(solution)/shard_map/all_to_all | solution.py:923
  204.8 5.3 collective-permute-start.2
  204.9 4.2 collective-permute-start.4
  241.4 30.0 %all-to-all-start.4 = ((bf16[8,128,512]{2,1,0:T(8,128)(2,1)}), bf16[8,128,512]{2,1,0:T(8,128)(2,1)S(1)}, u32[]{:S(2)}, u32[]{:S(2)}) async-start(bf16[8,128,512]{2,1,0:T(8,128)(2,1)} %pad_maximum_fusion.2), calls=%async_computation.4 | async-start | bytes 2097152 | tf_op jit(solution)/shard_map/all_to_all | solution.py:923
  245.6 22.6 %collective-permute-start.3 = (bf16[8,64,512]{2,1,0:T(8,128)(2,1)}, bf16[8,64,512]{2,1,0:T(8,128)(2,1)S(1)}, u32[]{:S(2)}, u32[]{:S(2)}) collective-permute-start(bf16[8,64,512]{2,1,0:T(8,128)(2,1)} %get-tuple-element.167.mixed_ref), channel_id=1, source_target_pairs={{0,8},{1,9},{2,10},{3,11},{4,12},{5,13},{6,14},{7,15},{8,0},{9,1},... | collective-permute-start | bytes 1572872 | tf_op jit(solution)/shard_map/ppermute | solution.py:932
  272.4 48.4 %all-to-all-start.5 = ((bf16[8,128,512]{2,1,0:T(8,128)(2,1)}), bf16[8,128,512]{2,1,0:T(8,128)(2,1)S(1)}, u32[]{:S(2)}, u32[]{:S(2)}) async-start(bf16[8,128,512]{2,1,0:T(8,128)(2,1)} %pad_maximum_fusion.1), calls=%async_computation.5 | async-start | bytes 2097152 | tf_op jit(solution)/shard_map/all_to_all | solution.py:923
  320.9 50.9 %all-to-all-start.6 = ((bf16[8,128,512]{2,1,0:T(8,128)(2,1)}), bf16[8,128,512]{2,1,0:T(8,128)(2,1)}, u32[]{:S(2)}, u32[]{:S(2)}) async-start(bf16[8,128,512]{2,1,0:T(8,128)(2,1)} %bitcast.28), calls=%async_computation.6 | async-start | bytes 2097152 | tf_op jit(solution)/shard_map/all_to_all | solution.py:923
  388.1 30.1 %all-to-all-start.7 = ((bf16[8,128,512]{2,1,0:T(8,128)(2,1)}), bf16[8,128,512]{2,1,0:T(8,128)(2,1)S(1)}, u32[]{:S(2)}, u32[]{:S(2)}) async-start(bf16[8,128,512]{2,1,0:T(8,128)(2,1)} %bitcast.29), calls=%async_computation.7 | async-start | bytes 2097152 | tf_op jit(solution)/shard_map/all_to_all | solution.py:923
  408.0 26.3 %collective-permute-start.6 = (bf16[512,4096]{1,0:T(8,128)(2,1)}, bf16[512,4096]{1,0:T(8,128)(2,1)}, u32[]{:S(2)}, u32[]{:S(2)}) collective-permute-start(bf16[512,4096]{1,0:T(8,128)(2,1)} %get-tuple-element.205), channel_id=1, source_target_pairs={{0,8},{1,9},{2,10},{3,11},{4,12},{5,13},{6,14},{7,15},{8,0},{9,1},... | collective-permute-start | bytes 12582920 | tf_op jit(solution)/shard_map/ppermute | solution.py:932
  408.0 26.3 %collective-permute-start.5 = (bf16[2048,1024]{1,0:T(8,128)(2,1)}, bf16[2048,1024]{1,0:T(8,128)(2,1)}, u32[]{:S(2)}, u32[]{:S(2)}) collective-permute-start(bf16[2048,1024]{1,0:T(8,128)(2,1)} %get-tuple-element.204), channel_id=1, source_target_pairs={{0,8},{1,9},{2,10},{3,11},{4,12},{5,13},{6,14},{7,15},{8,0},{9,1},... | collective-permute-start | bytes 12582920 | tf_op jit(solution)/shard_map/ppermute | solution.py:932
  432.0 22.9 %collective-permute-start.8 = (bf16[512,4096]{1,0:T(8,128)(2,1)}, bf16[512,4096]{1,0:T(8,128)(2,1)}, u32[]{:S(2)}, u32[]{:S(2)}) collective-permute-start(bf16[512,4096]{1,0:T(8,128)(2,1)} %get-tuple-element.216), channel_id=1, source_target_pairs={{0,8},{1,9},{2,10},{3,11},{4,12},{5,13},{6,14},{7,15},{8,0},{9,1},... | collective-permute-start | bytes 12582920 | tf_op jit(solution)/shard_map/ppermute | solution.py:932
  433.8 6.7 collective-permute-start.7
  440.5 52.3 %collective-permute-start.10 = (bf16[8,64,512]{2,1,0:T(8,128)(2,1)S(1)}, bf16[8,64,512]{2,1,0:T(8,128)(2,1)}, u32[]{:S(2)}, u32[]{:S(2)}) collective-permute-start(bf16[8,64,512]{2,1,0:T(8,128)(2,1)S(1)} %slice.277), channel_id=1, source_target_pairs={{0,8},{1,9},{2,10},{3,11},{4,12},{5,13},{6,14},{7,15},{8,0},{9,1},... | collective-permute-start | bytes 1572872 | tf_op jit(solution)/shard_map/ppermute | solution.py:932
  440.6 11.1 %collective-permute-start.9 = (bf16[512,1024]{1,0:T(8,128)(2,1)}, bf16[512,1024]{1,0:T(8,128)(2,1)S(1)}, u32[]{:S(2)}, u32[]{:S(2)}) collective-permute-start(bf16[512,1024]{1,0:T(8,128)(2,1)} %get-tuple-element.218), channel_id=1, source_target_pairs={{0,8},{1,9},{2,10},{3,11},{4,12},{5,13},{6,14},{7,15},{8,0},{9,1},... | collective-permute-start | bytes 3145736 | tf_op jit(solution)/shard_map/ppermute | solution.py:932
  446.7 69.2 %collective-permute-start.12 = (bf16[256,4096]{1,0:T(8,128)(2,1)}, bf16[256,4096]{1,0:T(8,128)(2,1)}, u32[]{:S(2)}, u32[]{:S(2)}) collective-permute-start(bf16[256,4096]{1,0:T(8,128)(2,1)} %get-tuple-element.291), channel_id=1, source_target_pairs={{0,16},{1,17},{2,18},{3,19},{4,20},{5,21},{6,22},{7,23},{8,24},{9,... | collective-permute-start | bytes 6291464 | tf_op jit(solution)/shard_map/ppermute | solution.py:932
  451.6 59.7 %collective-permute-start.11 = (bf16[1024,1024]{1,0:T(8,128)(2,1)}, bf16[1024,1024]{1,0:T(8,128)(2,1)}, u32[]{:S(2)}, u32[]{:S(2)}) collective-permute-start(bf16[1024,1024]{1,0:T(8,128)(2,1)} %get-tuple-element.293), channel_id=1, source_target_pairs={{0,2},{1,3},{2,0},{3,1},{4,6},{5,7},{6,4},{7,5},{8,10},{9,11},{10,... | collective-permute-start | bytes 6291464 | tf_op jit(solution)/shard_map/ppermute | solution.py:932
  452.9 57.5 %collective-permute-start.14 = (bf16[256,1024]{1,0:T(8,128)(2,1)}, bf16[256,1024]{1,0:T(8,128)(2,1)S(1)}, u32[]{:S(2)}, u32[]{:S(2)}) collective-permute-start(bf16[256,1024]{1,0:T(8,128)(2,1)} %get-tuple-element.307), channel_id=1, source_target_pairs={{0,2},{1,3},{2,0},{3,1},{4,6},{5,7},{6,4},{7,5},{8,10},{9,11},{10,... | collective-permute-start | bytes 1572872 | tf_op jit(solution)/shard_map/ppermute | solution.py:932
  459.1 60.5 %collective-permute-start.13 = (bf16[256,4096]{1,0:T(8,128)(2,1)}, bf16[256,4096]{1,0:T(8,128)(2,1)}, u32[]{:S(2)}, u32[]{:S(2)}) collective-permute-start(bf16[256,4096]{1,0:T(8,128)(2,1)} %get-tuple-element.289), channel_id=1, source_target_pairs={{0,1},{1,0},{2,3},{3,2},{4,5},{5,4},{6,7},{7,6},{8,9},{9,8},{10,11... | collective-permute-start | bytes 6291464 | tf_op jit(solution)/shard_map/ppermute | solution.py:932
  523.1 40.4 %all-to-all-start.8 = ((bf16[8,192,512]{2,1,0:T(8,128)(2,1)}), bf16[8,192,512]{2,1,0:T(8,128)(2,1)S(1)}, u32[]{:S(2)}, u32[]{:S(2)}) async-start(bf16[8,192,512]{2,1,0:T(8,128)(2,1)} %get-tuple-element.229), calls=%async_computation.8 | async-start | bytes 3145728 | tf_op jit(solution)/shard_map/all_to_all | solution.py:923
  526.6 43.1 %collective-permute-start.16 = (bf16[512,1024]{1,0:T(8,128)(2,1)}, bf16[512,1024]{1,0:T(8,128)(2,1)}, u32[]{:S(2)}, u32[]{:S(2)}) collective-permute-start(bf16[512,1024]{1,0:T(8,128)(2,1)} %get-tuple-element.299), channel_id=1, source_target_pairs={{0,1},{1,0},{2,3},{3,2},{4,5},{5,4},{6,7},{7,6},{8,9},{9,8},{10,11... | collective-permute-start | bytes 3145736 | tf_op jit(solution)/shard_map/ppermute | solution.py:932
  528.6 48.5 %collective-permute-start.18 = (bf16[128,4096]{1,0:T(8,128)(2,1)}, bf16[128,4096]{1,0:T(8,128)(2,1)}, u32[]{:S(2)}, u32[]{:S(2)}) collective-permute-start(bf16[128,4096]{1,0:T(8,128)(2,1)} %get-tuple-element.295), channel_id=1, source_target_pairs={{0,16},{1,17},{2,18},{3,19},{4,20},{5,21},{6,22},{7,23},{8,24},{9,... | collective-permute-start | bytes 3145736 | tf_op jit(solution)/shard_map/ppermute | solution.py:932
  530.0 45.3 %collective-permute-start.19 = (bf16[128,1024]{1,0:T(8,128)(2,1)}, bf16[128,1024]{1,0:T(8,128)(2,1)}, u32[]{:S(2)}, u32[]{:S(2)}) collective-permute-start(bf16[128,1024]{1,0:T(8,128)(2,1)} %get-tuple-element.315), channel_id=1, source_target_pairs={{0,1},{1,0},{2,3},{3,2},{4,5},{5,4},{6,7},{7,6},{8,9},{9,8},{10,11... | collective-permute-start | bytes 786440 | tf_op jit(solution)/shard_map/ppermute | solution.py:932
  530.2 65.6 %collective-permute-start.17 = (bf16[128,4096]{1,0:T(8,128)(2,1)}, bf16[128,4096]{1,0:T(8,128)(2,1)}, u32[]{:S(2)}, u32[]{:S(2)}) collective-permute-start(bf16[128,4096]{1,0:T(8,128)(2,1)} %get-tuple-element.297), channel_id=1, source_target_pairs={{0,1},{1,0},{2,3},{3,2},{4,5},{5,4},{6,7},{7,6},{8,9},{9,8},{10,11... | collective-permute-start | bytes 3145736 | tf_op jit(solution)/shard_map/ppermute | solution.py:932
  550.1 27.0 %copy-start.12 = (bf16[128,4096]{1,0:T(8,128)(2,1)S(1)}, bf16[128,4096]{1,0:T(8,128)(2,1)}, u32[]{:S(2)}) copy-start(bf16[128,4096]{1,0:T(8,128)(2,1)} %get-tuple-element.233) | copy-start | bytes 3145732
  550.1 48.1 %collective-permute-start.15 = (bf16[8,192,512]{2,1,0:T(8,128)(2,1)}, bf16[8,192,512]{2,1,0:T(8,128)(2,1)}, u32[]{:S(2)}, u32[]{:S(2)}) collective-permute-start(bf16[8,192,512]{2,1,0:T(8,128)(2,1)} %get-tuple-element.227), channel_id=1, source_target_pairs={{0,8},{1,9},{2,10},{3,11},{4,12},{5,13},{6,14},{7,15},{8,0},{9,1},... | collective-permute-start | bytes 4718600 | tf_op jit(solution)/shard_map/ppermute | solution.py:932
  572.6 23.2 %copy-start.11 = (bf16[128,4096]{1,0:T(8,128)(2,1)S(1)}, bf16[128,4096]{1,0:T(8,128)(2,1)}, u32[]{:S(2)}) copy-start(bf16[128,4096]{1,0:T(8,128)(2,1)} %get-tuple-element.232) | copy-start | bytes 3145732
  598.2 51.3 %all-to-all-start.9 = ((bf16[8,192,512]{2,1,0:T(8,128)(2,1)}), bf16[8,192,512]{2,1,0:T(8,128)(2,1)S(1)}, u32[]{:S(2)}, u32[]{:S(2)}) async-start(bf16[8,192,512]{2,1,0:T(8,128)(2,1)} %collective-permute-done.15), calls=%async_computation.9 | async-start | bytes 3145728 | tf_op jit(solution)/shard_map/all_to_all | solution.py:923
  602.8 46.8 %collective-permute-start.22 = (bf16[64,4096]{1,0:T(8,128)(2,1)}, bf16[64,4096]{1,0:T(8,128)(2,1)}, u32[]{:S(2)}, u32[]{:S(2)}) collective-permute-start(bf16[64,4096]{1,0:T(8,128)(2,1)} %get-tuple-element.301), channel_id=1, source_target_pairs={{0,2},{1,3},{2,0},{3,1},{4,6},{5,7},{6,4},{7,5},{8,10},{9,11},{10,... | collective-permute-start | bytes 1572872 | tf_op jit(solution)/shard_map/ppermute | solution.py:932
  604.8 50.2 %collective-permute-start.23 = (bf16[64,1024]{1,0:T(8,128)(2,1)}, bf16[64,1024]{1,0:T(8,128)(2,1)}, u32[]{:S(2)}, u32[]{:S(2)}) collective-permute-start(bf16[64,1024]{1,0:T(8,128)(2,1)} %get-tuple-element.317), channel_id=1, source_target_pairs={{0,16},{1,17},{2,18},{3,19},{4,20},{5,21},{6,22},{7,23},{8,24},{9,... | collective-permute-start | bytes 393224 | tf_op jit(solution)/shard_map/ppermute | solution.py:932
  608.2 44.8 %collective-permute-start.21 = (bf16[64,4096]{1,0:T(8,128)(2,1)}, bf16[64,4096]{1,0:T(8,128)(2,1)}, u32[]{:S(2)}, u32[]{:S(2)}) collective-permute-start(bf16[64,4096]{1,0:T(8,128)(2,1)} %get-tuple-element.303), channel_id=1, source_target_pairs={{0,2},{1,3},{2,0},{3,1},{4,6},{5,7},{6,4},{7,5},{8,10},{9,11},{10,... | collective-permute-start | bytes 1572872 | tf_op jit(solution)/shard_map/ppermute | solution.py:932
  608.2 48.3 %collective-permute-start.20 = (bf16[256,1024]{1,0:T(8,128)(2,1)}, bf16[256,1024]{1,0:T(8,128)(2,1)}, u32[]{:S(2)}, u32[]{:S(2)}) collective-permute-start(bf16[256,1024]{1,0:T(8,128)(2,1)} %get-tuple-element.305), channel_id=1, source_target_pairs={{0,16},{1,17},{2,18},{3,19},{4,20},{5,21},{6,22},{7,23},{8,24},{9,... | collective-permute-start | bytes 1572872 | tf_op jit(solution)/shard_map/ppermute | solution.py:932
  658.6 47.9 %all-to-all-start.10 = ((bf16[8,192,512]{2,1,0:T(8,128)(2,1)}), bf16[8,192,512]{2,1,0:T(8,128)(2,1)S(1)}, u32[]{:S(2)}, u32[]{:S(2)}) async-start(bf16[8,192,512]{2,1,0:T(8,128)(2,1)} %get-tuple-element.245), calls=%async_computation.10 | async-start | bytes 3145728 | tf_op jit(solution)/shard_map/all_to_all | solution.py:923
  681.8 30.5 %copy-start.27 = (s32[32]{0:T(128)S(1)}, s32[32]{0:T(128)}, u32[]{:S(2)}) copy-start(s32[32]{0:T(128)} %broadcast_xor_fusion.2.table_ref) | copy-start | bytes 388
  681.8 30.5 %copy-start.28 = (s32[32]{0:T(128)S(1)}, s32[32]{0:T(128)}, u32[]{:S(2)}) copy-start(s32[32]{0:T(128)} %get-tuple-element.194.table_ref) | copy-start | bytes 388
  681.8 30.5 %copy-start.29 = (s32[32]{0:T(128)S(1)}, s32[32]{0:T(128)}, u32[]{:S(2)}) copy-start(s32[32]{0:T(128)} %get-tuple-element.200.table_ref) | copy-start | bytes 388
  681.8 31.1 %copy-start.30 = (f32[1,1024]{1,0:T(1,128)S(1)}, f32[1,1024]{1,0:T(1,128)}, u32[]{:S(2)}) copy-start(f32[1,1024]{1,0:T(1,128)} %get-tuple-element.175) | copy-start | bytes 12292
  681.8 31.1 %copy-start.31 = (f32[1,1024]{1,0:T(1,128)S(1)}, f32[1,1024]{1,0:T(1,128)}, u32[]{:S(2)}) copy-start(f32[1,1024]{1,0:T(1,128)} %get-tuple-element.184) | copy-start | bytes 12292
  681.8 31.1 %copy-start.32 = (f32[8,128]{1,0:T(8,128)S(1)}, f32[8,128]{1,0:T(8,128)}, u32[]{:S(2)}) copy-start(f32[8,128]{1,0:T(8,128)} %get-tuple-element.220) | copy-start | bytes 12292
  681.8 31.1 %copy-start.34 = (f32[8,128]{1,0:T(8,128)S(1)}, f32[8,128]{1,0:T(8,128)}, u32[]{:S(2)}) copy-start(f32[8,128]{1,0:T(8,128)} %get-tuple-element.237) | copy-start | bytes 12292
  681.8 37.0 %copy-start.33 = (f32[8,128]{1,0:T(8,128)S(1)}, f32[8,128]{1,0:T(8,128)}, u32[]{:S(2)}) copy-start(f32[8,128]{1,0:T(8,128)} %get-tuple-element.230) | copy-start | bytes 12292
  681.8 37.0 %copy-start.35 = (f32[8,128]{1,0:T(8,128)S(1)}, f32[8,128]{1,0:T(8,128)}, u32[]{:S(2)}) copy-start(f32[8,128]{1,0:T(8,128)} %get-tuple-element.246) | copy-start | bytes 12292
  681.9 37.0 %copy-start.25 = (bf16[32,1024]{1,0:T(8,128)(2,1)S(1)}, bf16[32,1024]{1,0:T(8,128)(2,1)}, u32[]{:S(2)}) copy-start(bf16[32,1024]{1,0:T(8,128)(2,1)} %get-tuple-element.319) | copy-start | bytes 196612
  681.9 24.7 %collective-permute-start.24 = (bf16[8,192,512]{2,1,0:T(8,128)(2,1)}, bf16[8,192,512]{2,1,0:T(8,128)(2,1)}, u32[]{:S(2)}, u32[]{:S(2)}) collective-permute-start(bf16[8,192,512]{2,1,0:T(8,128)(2,1)} %get-tuple-element.243), channel_id=1, source_target_pairs={{0,8},{1,9},{2,10},{3,11},{4,12},{5,13},{6,14},{7,15},{8,0},{9,1},... | collective-permute-start | bytes 4718600 | tf_op jit(solution)/shard_map/ppermute | solution.py:932
  706.5 24.2 %copy-start.6 = (bf16[8,192,512]{2,1,0:T(8,128)(2,1)}, bf16[8,192,512]{2,1,0:T(8,128)(2,1)S(1)}, u32[]{:S(2)}) copy-start(bf16[8,192,512]{2,1,0:T(8,128)(2,1)S(1)} %all-to-all-done.10.rest_0_) | copy-start | bytes 4718596
  706.5 62.5 %all-to-all-start.11 = ((bf16[8,192,512]{2,1,0:T(8,128)(2,1)}), bf16[8,192,512]{2,1,0:T(8,128)(2,1)}, u32[]{:S(2)}, u32[]{:S(2)}) async-start(bf16[8,192,512]{2,1,0:T(8,128)(2,1)} %collective-permute-done.24), calls=%async_computation.11 | async-start | bytes 3145728 | tf_op jit(solution)/shard_map/all_to_all | solution.py:923
  712.9 130.3 %collective-permute-start.28 = (bf16[128,1024]{1,0:T(8,128)(2,1)}, bf16[128,1024]{1,0:T(8,128)(2,1)}, u32[]{:S(2)}, u32[]{:S(2)}) collective-permute-start(bf16[128,1024]{1,0:T(8,128)(2,1)} %get-tuple-element.313), channel_id=1, source_target_pairs={{0,4},{1,5},{2,6},{3,7},{4,0},{5,1},{6,2},{7,3},{8,12},{9,13},{10,... | collective-permute-start | bytes 786440 | tf_op jit(solution)/shard_map/ppermute | solution.py:932
  715.9 64.6 %collective-permute-start.27 = (bf16[32,4096]{1,0:T(8,128)(2,1)}, bf16[32,4096]{1,0:T(8,128)(2,1)}, u32[]{:S(2)}, u32[]{:S(2)}) collective-permute-start(bf16[32,4096]{1,0:T(8,128)(2,1)} %get-tuple-element.309), channel_id=1, source_target_pairs={{0,4},{1,5},{2,6},{3,7},{4,0},{5,1},{6,2},{7,3},{8,12},{9,13},{10,... | collective-permute-start | bytes 786440 | tf_op jit(solution)/shard_map/ppermute | solution.py:932
  716.0 129.2 %collective-permute-start.26 = (bf16[32,4096]{1,0:T(8,128)(2,1)}, bf16[32,4096]{1,0:T(8,128)(2,1)}, u32[]{:S(2)}, u32[]{:S(2)}) collective-permute-start(bf16[32,4096]{1,0:T(8,128)(2,1)} %get-tuple-element.311), channel_id=1, source_target_pairs={{0,4},{1,5},{2,6},{3,7},{4,0},{5,1},{6,2},{7,3},{8,12},{9,13},{10,... | collective-permute-start | bytes 786440 | tf_op jit(solution)/shard_map/ppermute | solution.py:932
  718.9 130.2 %collective-permute-start.25 = (bf16[32,1024]{1,0:T(8,128)(2,1)S(1)}, bf16[32,1024]{1,0:T(8,128)(2,1)S(1)}, u32[]{:S(2)}, u32[]{:S(2)}) collective-permute-start(bf16[32,1024]{1,0:T(8,128)(2,1)S(1)} %copy-done.25), channel_id=1, source_target_pairs={{0,4},{1,5},{2,6},{3,7},{4,0},{5,1},{6,2},{7,3},{8,12},{9,13},{10,... | collective-permute-start | bytes 196616 | tf_op jit(solution)/shard_map/ppermute | solution.py:932
  795.6 47.7 %copy-start.18 = (bf16[128,1024]{1,0:T(8,128)(2,1)S(1)}, bf16[128,1024]{1,0:T(8,128)(2,1)}, u32[]{:S(2)}) copy-start(bf16[128,1024]{1,0:T(8,128)(2,1)} %get-tuple-element.275) | copy-start | bytes 786436
  795.6 56.1 %copy-start.1 = (f32[16,2]{0,1:T(2,128)S(1)}, f32[16,2]{0,1:T(2,128)}, u32[]{:S(2)}) copy-start(f32[16,2]{0,1:T(2,128)} %param.31) | copy-start | bytes 388
  (25 other events, 203.0 us)
Sparse Core Ops, SparseCore 0:
  10.2 49.0 all-gather.5
  60.8 22.5 all-gather.7
  85.0 58.2 all-gather.9
  144.8 58.2 all-gather.11
  204.5 58.2 all-gather.13
where the time goes:
time: 862 us; the launch traced here: 858 us
  Pallas kernels  413 us (48%)
  waiting for transfers between devices  240 us (28%)
  starting transfers between devices  117 us (14%)
  other arithmetic  65.2 us (8%)
  between operations  14.6 us (2%)
  local copies, waits for them, and re-layouts  9.15 us (1%)
    all_to_all x12, waiting for transfers between devices, exchange(): lax.all_to_all(values, 'seq', split_axis=0, concat_axis=0, tiled=True)  140 us
    pallas_call x4, Pallas kernels, attend_backward(): pl.pallas_call(functools.partial(backward_kernel, (local, head_dim, block...  110 us
    pallas_call x2, Pallas kernels, middle_part(): pl.pallas_call(functools.partial(middle_kernel, (head_dim, output is not...  84.6 us
    pallas_call x4, Pallas kernels, attend_forward(): pl.pallas_call(functools.partial(forward_kernel, (local, head_dim, block,...  64.1 us
    all_to_all x12, starting transfers between devices, exchange(): lax.all_to_all(values, 'seq', split_axis=0, concat_axis=0, tiled=True)  58.3 us
    ppermute x29, starting transfers between devices, permute(): lax.ppermute(value, ('shard', 'seq'), [(i, i ^ mask) for i in range(devic...  58.2 us
    ppermute x29, waiting for transfers between devices, permute(): lax.ppermute(value, ('shard', 'seq'), [(i, i ^ mask) for i in range(devic...  52.6 us
    pallas_call x1, Pallas kernels, reduce_rows(): pl.pallas_call(functools.partial(reduce_kernel, orders, count), in_specs=...  47.6 us
  transfers between devices with their start and end apart: 46, of which 16 were waited for; matrix products, arithmetic and copies ran while one was open for 7% of the time, Pallas kernels for 46%

commit v1 on v0

--- a/solution.py
+++ b/solution.py
@@ -735,56 +735,51 @@
     )(table, *lefts, *rights)
 
 
-def tall_kernel(units, pieces_here, table_ref, *refs):
-    keep_ref, send_ref = refs[-2:]
-    total = None
-    for u in range(units):
-        left = [refs[u * pieces_here + i][...] for i in range(pieces_here)]
-        made = dot(jnp.concatenate(left, axis=0), refs[units * pieces_here + u][...])
-        total = made if total is None else total + made
-    kept = pl.program_id(0) < pl.num_programs(0) // 2
-
-    @pl.when(kept)
-    def _():
-        keep_ref[...] = total.astype(BF16)
-
-    @pl.when(jnp.logical_not(kept))
-    def _():
-        send_ref[...] = total.astype(BF16)
-
-
-def tall_grads(table, lefts, rights, rows, name):
+def weights_kernel(units, *refs):
+    out_ref = refs[-1]
+    total = dot(refs[0][...], refs[units][...])
+    for u in range(1, units):
+        total += dot(refs[u][...], refs[units + u][...])
+    out_ref[...] = total.astype(BF16).reshape(out_ref.shape)
+
+
+def weight_grad(lefts, rights, by_left, out_struct, out_spec, steps, into, name):
     units = len(lefts)
-    width = lefts[0].shape[1]
-    columns = rights[0].shape[1]
-    places = table.shape[0]
-    each = 4
-    middle = places // each // 2
-    in_specs = []
-    for _ in lefts:
-        for i in range(each):
-            in_specs.append(pl.BlockSpec((rows, width), lambda n, table, i=i: (table[n * each + i], 0)))
-    in_specs += [pl.BlockSpec(a.shape, lambda n, *_: (0, 0)) for a in rights]
+
+    def fixed(a):
+        return pl.BlockSpec(a.shape, lambda n: (0, 0))
+
+    def left_spec(a):
+        return pl.BlockSpec((a.shape[0] // steps, a.shape[1]), lambda n: (n, 0))
+
+    def right_spec(a):
+        return pl.BlockSpec((a.shape[0], a.shape[1] // steps), lambda n: (0, n))
+
+    operands = list(lefts) + list(rights)
+    if by_left:
+        in_specs = [left_spec(a) for a in lefts] + [fixed(a) for a in rights]
+    else:
+        in_specs = [fixed(a) for a in lefts] + [right_spec(a) for a in rights]
+    aliases = {}
+    if into is not None:
+        aliases = {len(operands): 0}
+        operands.append(into)
+        in_specs.append(pl.BlockSpec(memory_space=pl.ANY))
     return pl.pallas_call(
-        functools.partial(tall_kernel, units, each),
-        grid_spec=pltpu.PrefetchScalarGridSpec(
-            num_scalar_prefetch=1,
-            grid=(places // each,),
-            in_specs=in_specs,
-            out_specs=[
-                pl.BlockSpec((each * rows, columns), lambda n, *_: (jnp.minimum(n, middle - 1), 0)),
-                pl.BlockSpec((each * rows, columns), lambda n, *_: (jnp.maximum(n - middle, 0), 0)),
-            ],
-        ),
-        out_shape=[jax.ShapeDtypeStruct((places // 2 * rows, columns), BF16)] * 2,
+        functools.partial(weights_kernel, units),
+        grid=(steps,),
+        in_specs=in_specs,
+        out_specs=out_spec,
+        out_shape=out_struct,
+        input_output_aliases=aliases,
         compiler_params=pltpu.CompilerParams(vmem_limit_bytes=62 << 20),
         cost_estimate=pl.CostEstimate(
-            flops=2 * units * places * rows * width * columns // COVER,
-            bytes_accessed=2 * places * rows * columns,
+            flops=2 * units * lefts[0].shape[0] * lefts[0].shape[1] * rights[0].shape[1] // COVER,
+            bytes_accessed=2 * lefts[0].shape[0] * rights[0].shape[1],
             transcendentals=0,
         ),
         name=name,
-    )(table, *[a for a in lefts for _ in range(each)], *rights)
+    )(*operands)
 
 
 def reduce_kernel(orders, count, *refs):
@@ -1049,45 +1044,24 @@
                     ([mixed_tok[u] for u in range(len(units))], column(6)),
                 )
             ]
-        tables = [after(places_of(order), *token) for order in orders]
-        span = [(0, devices)]
-        down = tall_grads(tables[2], column(1), column(4), tall, "down_grad")
-        came = [permute(down[1], orders[2][0])]
-        table = after(tables[0], down[0])
-        gate = picked_grads(table, span, column(0), column(2), rows, False, 2, 1024, "gate_grad")
-        came.append(permute(gate[1], orders[0][0]))
-        table = after(tables[1], gate[0], *holder["flying"])
-        up = picked_grads(table, span, column(0), column(3), rows, False, 2, 1024, "up_grad")
-        came.append(permute(up[1], orders[1][0]))
-        table = after(tables[2], up[0], *came[:2])
+        part = ffn // fold
+        spare = -(-(3 * part + model // fold) // 384) * 384
+        struct = jax.ShapeDtypeStruct((devices, fold, rows, spare), BF16)
+        down = pl.BlockSpec((512 // tall, fold, rows, model), lambda n: (n, 0, 0, 0))
+        gate = pl.BlockSpec((devices, 1, rows, part), lambda n: (0, n, 0, 1))
+        up = pl.BlockSpec((devices, 1, rows, part), lambda n: (0, n, 0, 2))
+        narrow = model // fold
+        out = pl.BlockSpec((devices, 1, rows, narrow), lambda n: (0, n, 0, 3 * part // narrow))
+        firsts = [after(middle[0][4], *token)] + [item[4] for item in middle[1:]]
+        terms = weight_grad(column(1), firsts, True, struct, down, ffn // 512, None, "down_grad")
+        rights = [after(middle[0][2], *holder["flying"])] + [item[2] for item in middle[1:]]
+        terms = weight_grad(column(0), rights, False, struct, gate, fold, terms, "gate_grad")
+        terms = weight_grad(column(0), column(3), False, struct, up, fold, terms, "up_grad")
         mixed_all = [mixed_tok[u] for u in range(len(units))]
-        out = picked_grads(table, span, mixed_all, column(6), rows, False, 2, 512, "out_grad")
-        came.append(permute(out[1], orders[2][0]))
-        kept = [down[0], gate[0], up[0], out[0]]
-        masks = [orders[2], orders[0], orders[1], orders[2]]
-        streams = [[keep, got, mask[1:]] for keep, got, mask in zip(kept, came, masks)]
-        holder["streams"] = streams
-        return out[0]
-
-    def wide_sum(a, b):
-        return a.astype(F32) + b.astype(F32)
-
-    def advance(token):
-        out = ()
-        if not direct:
-            return out
-        for stream in holder["streams"]:
-            keep, came, masks = stream
-            if not masks:
-                continue
-            keep = after(keep, *token)
-            half = keep.shape[0] // 2
-            send = wide_sum(keep[half:], came[half:]).astype(BF16)
-            stream[0] = wide_sum(keep[:half], came[:half]).astype(BF16)
-            stream[1] = permute(send, masks[0])
-            stream[2] = masks[1:]
-            out = out + (send, stream[0])
-        return out
+        terms = weight_grad(mixed_all, column(6), False, struct, out, fold, terms, "out_grad")
+        terms = terms.reshape(ffn, spare)
+        holder["owned"] = lax.psum_scatter(terms, ("shard", "seq"), scatter_dimension=0, tiled=True)
+        return terms
 
     holder = {}
 
@@ -1169,7 +1143,6 @@
             steps += [(work(run_backward, *at), None), (None, send_back(*at))]
         steps += [(work(run_final, u), None) for u in range(total)]
 
-    late = [task for task, _ in steps[-2:]]
     token = ()
     pending = []
     for task, send in steps:
@@ -1177,9 +1150,6 @@
         moved = None
         waited = tuple(pending)
         pending.clear()
-        if "streams" in holder:
-            leaving = advance(token)
-            token = token if task in late else token + leaving
         if send is not None:
             moved = exchange(after(send[0](), *token))
             done = (moved,)
@@ -1200,11 +1170,15 @@
     gain_attn = sum(item[3][0] for item in finals)
     gain_ffn = sum(item[8][0] for item in middle)
     if direct:
-        while holder["streams"][0][2]:
-            advance(token)
-        down_own, gate_own, up_own, out_own = [
-            wide_sum(after(keep, *token), came) for keep, came, _ in holder["streams"]
-        ]
+        owned, part = holder["owned"], ffn // fold
+
+        def joined(start, size):
+            piece = owned[:, start : start + size].reshape(fold, rows, size)
+            return jnp.swapaxes(piece, 0, 1).reshape(rows, fold * size).astype(F32)
+
+        down_own = owned[:, :part].astype(F32)
+        gate_own, up_own = joined(part, part), joined(2 * part, part)
+        out_own = joined(3 * part, model // fold)
         table = jnp.concatenate([places_of(order) for order in orders])
         attn_terms = picked_grads(
             table, [(i * devices, devices) for i in range(3)], flats,

time: 862 us -> 836 us (0.970)
  other arithmetic: 65.2 us -> 14.1 us
  starting transfers between devices: 117 us -> 66.2 us
  Pallas kernels: 413 us -> 460 us
  waiting for transfers between devices: 240 us -> 270 us
    all_to_all x12, waiting for transfers between devices: 140 us -> 208 us  [exchange(): lax.all_to_all(values, 'seq', split_axis=0, concat_axis=0, tiled=True)]
    ppermute x29 -> x9, starting transfers between devices: 58.2 us -> 4.12 us  [permute(): lax.ppermute(value, ('shard', 'seq'), [(i, i ^ mask) for i in range(devic...]
    convert_element_type x16 -> x1, other arithmetic: 45.9 us -> 1.99 us  [on_device(): down_own = owned[:, :part].astype(F32)]
    ppermute x29 -> x9, waiting for transfers between devices: 52.6 us -> 14.3 us  [permute(): lax.ppermute(value, ('shard', 'seq'), [(i, i ^ mask) for i in range(devic...]
    pallas_call x4 -> x1, Pallas kernels: 45.5 us -> 11.9 us  [picked_grads(): pl.pallas_call(functools.partial(picked_kernel, units, rows, places, flip...]
    pallas_call x1 -> x4, Pallas kernels: 16.3 us -> 46.9 us  [weight_grad(): pl.pallas_call(functools.partial(weights_kernel, units), grid=(steps,), i...]
    pallas_call x4, Pallas kernels: 110 us -> 135 us  [attend_backward(): pl.pallas_call(functools.partial(backward_kernel, (local, head_dim, block...]
    pallas_call x1, Pallas kernels: 47.6 us -> 61.1 us  [reduce_rows(): pl.pallas_call(functools.partial(reduce_kernel, orders, count), in_specs=...]
  transfers between devices with their start and end apart: 46 -> 27, of which waited for: 16 -> 15; matrix products, arithmetic and copies ran while one was open for 7% -> 2% of each run, Pallas kernels for 46% -> 51%
where the time goes in v1:
time: 836 us; the launch traced here: 840 us
  Pallas kernels  460 us (55%)
  waiting for transfers between devices  270 us (32%)
  starting transfers between devices  66.2 us (8%)
  between operations  15 us (2%)
  other arithmetic  14.1 us (2%)
  local copies, waits for them, and re-layouts  13.8 us (2%)
    all_to_all x12, waiting for transfers between devices, exchange(): lax.all_to_all(values, 'seq', split_axis=0, concat_axis=0, tiled=True)  208 us
    pallas_call x4, Pallas kernels, attend_backward(): pl.pallas_call(functools.partial(backward_kernel, (local, head_dim, block...  135 us
    pallas_call x2, Pallas kernels, middle_part(): pl.pallas_call(functools.partial(middle_kernel, (head_dim, output is not...  84.6 us
    pallas_call x4, Pallas kernels, attend_forward(): pl.pallas_call(functools.partial(forward_kernel, (local, head_dim, block,...  76 us
    all_to_all x12, starting transfers between devices, exchange(): lax.all_to_all(values, 'seq', split_axis=0, concat_axis=0, tiled=True)  61.6 us
    pallas_call x1, Pallas kernels, reduce_rows(): pl.pallas_call(functools.partial(reduce_kernel, orders, count), in_specs=...  61.1 us
    pallas_call x4, Pallas kernels, weight_grad(): pl.pallas_call(functools.partial(weights_kernel, units), grid=(steps,), i...  46.9 us
    all_gather x5, waiting for transfers between devices, gather(): return lax.all_gather(weight, 'shard', axis=0, tiled=True)  45.5 us
  transfers between devices with their start and end apart: 27, of which 15 were waited for; matrix products, arithmetic and copies ran while one was open for 2% of the time, Pallas kernels for 51%

profile of v1, /device:TPU:0, one launch (start us, length us, event | category | flops | bytes accessed | tf_op | source)
XLA Modules:
  0.0 839.5 jit_solution(3606310082779094986)
XLA Ops:
  7.2 2.6 pad_maximum_fusion
  12.6 1.2 multiply_sine_fusion
  13.8 45.5 %all-gather.6.cloned.1.call-done.query_ref.key_ref.value_ref = bf16[1024,3072]{1,0:T(8,128)(2,1)} async-done(((bf16[256,3072]{1,0:T(8,128)(2,1)}), bf16[1024,3072]{1,0:T(8,128)(2,1)}) %all-gather.6.cloned.1.call-update) | async-done | bytes 6291472 | tf_op jit(solution)/shard_map/all_gather | solution.py:915
  59.3 10.9 %project.2 = (bf16[1024,512]{1,0:T(8,128)(2,1)}, bf16[8,192,512]{2,1,0:T(8,128)(2,1)}, bf16[8,208,512]{2,1,0:T(8,128)(2,1)}) custom-call(s32[1]{0:T(128)} %bitcast.2.core_ref, bf16[2,1,512,1024]{3,2,1,0:T(8,128)(2,1)} %tokens_ref.11, f32[1,1024]{1,0:T(1,128)} %bitcast.56, bf16[1024,3072]{1,0:T(8,128)(2,1)} %all-gather.6.cloned.1.call-done.query_ref.key_ref.value_ref, ...), custom_call_target="tpu_custom_call" | custom-call | flops 201326592 | bytes 12582912 | tf_op jit(solution)/shard_map/project/pallas_call | solution.py:420
  70.2 5.5 all-to-all-start
  76.3 11.0 %project.3 = (bf16[1024,512]{1,0:T(8,128)(2,1)}, bf16[8,192,512]{2,1,0:T(8,128)(2,1)}, bf16[8,208,512]{2,1,0:T(8,128)(2,1)}) custom-call(s32[1]{0:T(128)} %bitcast.2.core_ref, bf16[2,1,512,1024]{3,2,1,0:T(8,128)(2,1)} %tokens_ref.11, f32[1,1024]{1,0:T(1,128)} %bitcast.57, bf16[1024,3072]{1,0:T(8,128)(2,1)} %all-gather.6.cloned.1.call-done.query_ref.key_ref.value_ref, ...), custom_call_target="tpu_custom_call" | custom-call | flops 201326592 | bytes 12582912 | tf_op jit(solution)/shard_map/project/pallas_call | solution.py:420
  87.3 28.7 %all-to-all-done.ids_ref = bf16[8,208,512]{2,1,0:T(8,128)(2,1)S(1)} async-done(((bf16[8,208,512]{2,1,0:T(8,128)(2,1)}), bf16[8,208,512]{2,1,0:T(8,128)(2,1)S(1)}, u32[]{:S(2)}, u32[]{:S(2)}) %all-to-all-start) | async-done | bytes 1703968 | tf_op jit(solution)/shard_map/all_to_all | solution.py:918
  116.0 4.3 all-to-all-start.1
  121.6 2.0 collective-permute-done
  124.1 7.6 attend_forward.4
  131.8 25.1 %all-to-all-done.1.x_ref = bf16[8,192,512]{2,1,0:T(8,128)(2,1)} async-done(((bf16[8,192,512]{2,1,0:T(8,128)(2,1)}), bf16[8,192,512]{2,1,0:T(8,128)(2,1)}, u32[]{:S(2)}, u32[]{:S(2)}) %all-to-all-start.1) | async-done | bytes 1572896 | tf_op jit(solution)/shard_map/all_to_all | solution.py:918
  156.9 3.6 all-to-all-start.2
  161.1 22.7 %attend_forward.5 = (bf16[8,64,512]{2,1,0:T(8,128)(2,1)}, f32[8,1,512]{2,1,0:T(1,128)}) custom-call(s32[1]{0:T(128)} %bitcast.9.len_ref, f32[1,2]{1,0:T(1,128)} %copy.45.bias_ref, bf16[8,192,512]{2,1,0:T(8,128)(2,1)} %all-to-all-done.1.x_ref, bf16[8,208,512]{2,1,0:T(8,128)(2,1)} %copy-done.7), custom_call_target="tpu_custom_call" | custom-call | flops 2147483648 | bytes 3145728 | tf_op jit(solution)/shard_map/attend_forward/pallas_call | solution.py:171
  183.8 16.7 %all-to-all-done.2.ids_ref = bf16[8,208,512]{2,1,0:T(8,128)(2,1)S(1)} async-done(((bf16[8,208,512]{2,1,0:T(8,128)(2,1)}), bf16[8,208,512]{2,1,0:T(8,128)(2,1)S(1)}, u32[]{:S(2)}, u32[]{:S(2)}) %all-to-all-start.2) | async-done | bytes 1703968 | tf_op jit(solution)/shard_map/all_to_all | solution.py:918
  200.5 4.3 all-to-all-start.3
  205.4 3.7 collective-permute-done.4
  209.1 1.1 pad_maximum_fusion.2
  210.2 27.6 %attend_forward.6 = (bf16[8,64,512]{2,1,0:T(8,128)(2,1)}, f32[8,1,512]{2,1,0:T(1,128)}) custom-call(s32[1]{0:T(128)} %bitcast.10.len_ref, f32[1,2]{1,0:T(1,128)} %copy.45.bias_ref, bf16[8,208,512]{2,1,0:T(8,128)(2,1)} %collective-permute-done.2.x_ref.ids_ref, bf16[8,208,512]{2,1,0:T(8,128)(2,1)} %collective-permute-done.2.x_ref.ids_ref), custom_call_target="tpu_custom_call" | custom-call | flops 2147483648 | bytes 3407872 | tf_op jit(solution)/shard_map/attend_forward/pallas_call | solution.py:171
  237.8 3.7 all-to-all-done.3.x_ref
  241.5 3.9 all-to-all-start.4
  245.4 18.1 %attend_forward.7 = (bf16[8,64,512]{2,1,0:T(8,128)(2,1)}, f32[8,1,512]{2,1,0:T(1,128)}) custom-call(s32[1]{0:T(128)} %bitcast.len_ref, f32[1,2]{1,0:T(1,128)} %copy.45.bias_ref, bf16[8,192,512]{2,1,0:T(8,128)(2,1)} %all-to-all-done.3.x_ref, bf16[8,208,512]{2,1,0:T(8,128)(2,1)} %copy-done.8), custom_call_target="tpu_custom_call" | custom-call | flops 2147483648 | bytes 3145728 | tf_op jit(solution)/shard_map/attend_forward/pallas_call | solution.py:171
  263.5 2.1 pad_maximum_fusion.1
  265.6 5.6 all-to-all-done.4
  271.2 1.0 copy-done.5
  272.2 3.6 all-to-all-start.5
  275.9 1.3 add_add_fusion.1.info_ref
  277.2 42.3 %middle_part.2 = (bf16[2,1,512,1024]{3,2,1,0:T(8,128)(2,1)}, bf16[1024,512]{1,0:T(8,128)(2,1)}, bf16[1024,512]{1,0:T(8,128)(2,1)}, bf16[4096,512]{1,0:T(8,128)(2...) custom-call(s32[3]{0:T(128)} %add_add_fusion.1.info_ref, ...), custom_call_target="tpu_custom_call" | custom-call | flops 1610612736 | bytes 33554432 | tf_op jit(solution)/shard_map/middle_part/pallas_call | solution.py:543
  319.5 6.5 all-to-all-start.6
  326.0 1.2 add_add_fusion.info_ref
  327.2 42.3 %middle_part.3 = (bf16[2,1,512,1024]{3,2,1,0:T(8,128)(2,1)}, bf16[1024,512]{1,0:T(8,128)(2,1)}, bf16[1024,512]{1,0:T(8,128)(2,1)}, bf16[4096,512]{1,0:T(8,128)(2...) custom-call(s32[3]{0:T(128)} %add_add_fusion.info_ref, ...), custom_call_target="tpu_custom_call", output_to_operand_aliasing={{0}: (9, {})} | custom-call | flops 1610612736 | bytes 33554432 | tf_op jit(solution)/shard_map/middle_part/pallas_call | solution.py:543
  369.5 6.0 all-to-all-start.7
  375.7 14.2 %down_grad.1.refs_4_ = bf16[32,4,32,3456]{3,2,1,0:T(8,128)(2,1)} custom-call(bf16[4096,512]{1,0:T(8,128)(2,1)} %get-tuple-element.165.refs_0_, bf16[4096,512]{1,0:T(8,128)(2,1)} %get-tuple-element.166.refs_1_, bf16[512,1024]{1,0:T(8,128)(2,1)} %get-tuple-element.168.refs_2_, bf16[512,1024]{1,0:T(8,128)(2,1)} %get-tuple-element.169.refs_3_), custom_call_target="tpu_custom_call" | custom-call | flops 536870912 | bytes 8388608 | tf_op jit(solution)/shard_map/down_grad/pallas_call | solution.py:768
  390.0 10.8 %all-to-all-done.7.grad_ref = bf16[8,128,512]{2,1,0:T(8,128)(2,1)S(1)} async-done(((bf16[8,128,512]{2,1,0:T(8,128)(2,1)}), bf16[8,128,512]{2,1,0:T(8,128)(2,1)S(1)}, u32[]{:S(2)}, u32[]{:S(2)}) %all-to-all-start.7) | async-done | bytes 1048608 | tf_op jit(solution)/shard_map/all_to_all | solution.py:918
  400.7 13.5 %gate_grad.1.refs_4_ = bf16[32,4,32,3456]{3,2,1,0:T(8,128)(2,1)} custom-call(bf16[1024,512]{1,0:T(8,128)(2,1)} %get-tuple-element.158.refs_0_, bf16[1024,512]{1,0:T(8,128)(2,1)} %get-tuple-element.159.refs_1_, bf16[512,4096]{1,0:T(8,128)(2,1)} %get-tuple-element.163.refs_2_, ...), custom_call_target="tpu_custom_call", output_to_operand_aliasing={{}: (4, {})} | custom-call | flops 536870912 | bytes 8388608 | tf_op jit(solution)/shard_map/gate_grad/pallas_call | solution.py:768
  414.2 13.2 %up_grad.1.refs_4_ = bf16[32,4,32,3456]{3,2,1,0:T(8,128)(2,1)} custom-call(bf16[1024,512]{1,0:T(8,128)(2,1)} %get-tuple-element.158.refs_0_, bf16[1024,512]{1,0:T(8,128)(2,1)} %get-tuple-element.159.refs_1_, bf16[512,4096]{1,0:T(8,128)(2,1)} %get-tuple-element.160.refs_2_, ...), custom_call_target="tpu_custom_call", output_to_operand_aliasing={{}: (4, {})} | custom-call | flops 536870912 | bytes 8388608 | tf_op jit(solution)/shard_map/up_grad/pallas_call | solution.py:768
  427.3 6.0 out_grad.1
  433.4 1.1 slice.80
  434.5 2.3 collective-permute-start.5
  436.9 1.5 collective-permute-done.5.grad_ref
  438.5 41.7 %attend_backward.4 = (bf16[8,192,512]{2,1,0:T(8,128)(2,1)}, f32[8,128]{1,0:T(8,128)}) custom-call(s32[1]{0:T(128)} %bitcast.9.len_ref, f32[1,2]{1,0:T(1,128)} %copy.45.bias_ref, bf16[8,192,512]{2,1,0:T(8,128)(2,1)} %all-to-all-done.1.x_ref, bf16[8,208,512]{2,1,0:T(8,128)(2,1)} %copy-done.7, bf16[8,128,512]{2,1,0:T(8,128)(2,1)} %all-to-all-done.6.grad_ref, ...), custom_call_target="tpu_custom_call" | custom-call | flops 5368709120 | bytes 4718592 | tf_op jit(solution)/shard_map/attend_backward/pallas_call | solution.py:310
  480.2 0.8 copy-done.25
  481.0 3.6 all-to-all-start.8
  484.6 9.7 %attend_backward.5 = (bf16[8,192,512]{2,1,0:T(8,128)(2,1)}, f32[8,128]{1,0:T(8,128)}) custom-call(s32[1]{0:T(128)} %bitcast.8.len_ref, f32[1,2]{1,0:T(1,128)} %copy.45.bias_ref, bf16[8,208,512]{2,1,0:T(8,128)(2,1)} %collective-permute-done.1.x_ref.ids_ref, bf16[8,208,512]{2,1,0:T(8,128)(2,1)} %collective-permute-done.1.x_ref.ids_ref, ...), custom_call_target="tpu_custom_call" | custom-call | flops 5368709120 | bytes 5111808 | tf_op jit(solution)/shard_map/attend_backward/pallas_call | solution.py:310
  494.7 3.4 collective-permute-done.7
  498.0 29.0 %all-to-all-done.8.rest_0_ = bf16[8,192,512]{2,1,0:T(8,128)(2,1)S(1)} async-done(((bf16[8,192,512]{2,1,0:T(8,128)(2,1)}), bf16[8,192,512]{2,1,0:T(8,128)(2,1)S(1)}, u32[]{:S(2)}, u32[]{:S(2)}) %all-to-all-start.8) | async-done | bytes 1572896 | tf_op jit(solution)/shard_map/all_to_all | solution.py:918
  527.1 10.8 %all-to-all-start.9 = ((bf16[8,192,512]{2,1,0:T(8,128)(2,1)}), bf16[8,192,512]{2,1,0:T(8,128)(2,1)}, u32[]{:S(2)}, u32[]{:S(2)}) async-start(bf16[8,192,512]{2,1,0:T(8,128)(2,1)} %collective-permute-done.7), calls=%async_computation.9 | async-start | bytes 3145728 | tf_op jit(solution)/shard_map/all_to_all | solution.py:918
  537.9 32.1 %attend_backward.6 = (bf16[8,192,512]{2,1,0:T(8,128)(2,1)}, f32[8,128]{1,0:T(8,128)}) custom-call(s32[1]{0:T(128)} %bitcast.len_ref, f32[1,2]{1,0:T(1,128)} %copy.45.bias_ref, bf16[8,192,512]{2,1,0:T(8,128)(2,1)} %all-to-all-done.3.x_ref, bf16[8,208,512]{2,1,0:T(8,128)(2,1)} %copy-done.8, bf16[8,128,512]{2,1,0:T(8,128)(2,1)} %copy-done.6, ...), custom_call_target="tpu_custom_call" | custom-call | flops 5368709120 | bytes 4718592 | tf_op jit(solution)/shard_map/attend_backward/pallas_call | solution.py:310
  569.9 42.4 %all-to-all-done.9.rest_1_ = bf16[8,192,512]{2,1,0:T(8,128)(2,1)} async-done(((bf16[8,192,512]{2,1,0:T(8,128)(2,1)}), bf16[8,192,512]{2,1,0:T(8,128)(2,1)}, u32[]{:S(2)}, u32[]{:S(2)}) %all-to-all-start.9) | async-done | bytes 1572896 | tf_op jit(solution)/shard_map/all_to_all | solution.py:918
  612.3 3.6 all-to-all-start.10
  615.9 51.4 %attend_backward.7 = (bf16[8,192,512]{2,1,0:T(8,128)(2,1)}, f32[8,128]{1,0:T(8,128)}) custom-call(s32[1]{0:T(128)} %bitcast.10.len_ref, f32[1,2]{1,0:T(1,128)} %copy.45.bias_ref, bf16[8,208,512]{2,1,0:T(8,128)(2,1)} %collective-permute-done.2.x_ref.ids_ref, bf16[8,208,512]{2,1,0:T(8,128)(2,1)} %collective-permute-done.2.x_ref.ids_ref, ...), custom_call_target="tpu_custom_call" | custom-call | flops 5368709120 | bytes 5111808 | tf_op jit(solution)/shard_map/attend_backward/pallas_call | solution.py:310
  667.5 3.7 collective-permute-done.8
  671.2 5.9 all-to-all-start.11
  678.3 11.5 %final_part.2 = (bf16[2,1,512,1024]{3,2,1,0:T(8,128)(2,1)}, bf16[1024,512]{1,0:T(8,128)(2,1)}, bf16[1024,512]{1,0:T(8,128)(2,1)}, bf16[1024,512]{1,0:T(8,128)(2,1)}, f32[1,1024]{1,0:T(1,128)}) custom-call(s32[1]{0:T(128)} %bitcast.2.core_ref, bf16[2,1,512,1024]{3,2,1,0:T(8,128)(2,1)} %tokens_ref.11, f32[512,1024]{1,0:T(8,128)} %get-tuple-element.188.grad_res_ref, ...), custom_call_target="tpu_custom_call" | custom-call | flops 201326592 | bytes 12582912 | tf_op jit(solution)/shard_map/final_part/pallas_call | solution.py:657
  689.8 46.0 %all-to-all-done.11.rest_1_ = bf16[8,192,512]{2,1,0:T(8,128)(2,1)} async-done(((bf16[8,192,512]{2,1,0:T(8,128)(2,1)}), bf16[8,192,512]{2,1,0:T(8,128)(2,1)}, u32[]{:S(2)}, u32[]{:S(2)}) %all-to-all-start.11) | async-done | bytes 1572896 | tf_op jit(solution)/shard_map/all_to_all | solution.py:918
  735.7 11.6 %final_part.3 = (bf16[2,1,512,1024]{3,2,1,0:T(8,128)(2,1)}, bf16[1024,512]{1,0:T(8,128)(2,1)}, bf16[1024,512]{1,0:T(8,128)(2,1)}, bf16[1024,512]{1,0:T(8,128)(2,1)}, f32[1,1024]{1,0:T(1,128)}) custom-call(s32[1]{0:T(128)} %bitcast.2.core_ref, bf16[2,1,512,1024]{3,2,1,0:T(8,128)(2,1)} %tokens_ref.11, ...), custom_call_target="tpu_custom_call", output_to_operand_aliasing={{0}: (11, {})} | custom-call | flops 201326592 | bytes 12582912 | tf_op jit(solution)/shard_map/final_part/pallas_call | solution.py:657
  747.3 0.7 add.45
  748.0 11.9 %attn_grads.1 = (bf16[1024,1024]{1,0:T(8,128)(2,1)}, bf16[1024,1024]{1,0:T(8,128)(2,1)}, bf16[1024,1024]{1,0:T(8,128)(2,1)}) custom-call(s32[96]{0:T(128)} %pad_add_fusion.table_ref, bf16[1024,512]{1,0:T(8,128)(2,1)} %get-tuple-element.112.refs_0_, bf16[1024,512]{1,0:T(8,128)(2,1)} %get-tuple-element.119.refs_1_, ...), custom_call_target="tpu_custom_call" | custom-call | flops 402653184 | bytes 12582912 | tf_op jit(solution)/shard_map/attn_grads/pallas_call | solution.py:714
  760.5 61.1 %reduce_rows.1 = (f32[32,1024]{1,0:T(8,128)}, f32[32,1024]{1,0:T(8,128)}, f32[32,1024]{1,0:T(8,128)}, f32[24,128]{1,0:T(8,128)}) custom-call(bf16[1024,1024]{1,0:T(8,128)(2,1)} %get-tuple-element.204.refs_0_, bf16[1024,1024]{1,0:T(8,128)(2,1)} %get-tuple-element.205.refs_1_, bf16[1024,1024]{1,0:T(8,128)(2,1)} %get-tuple-element.206.refs_2_, ...), custom_call_target="tpu_custom_call" | custom-call | tf_op jit(solution)/shard_map/reduce_rows/pallas_call | solution.py:871
  821.6 1.4 slice.87
  823.7 1.3 slice_bitcast_fusion
  825.0 0.8 slice.94
  826.5 2.0 slice_convert_fusion
  828.6 0.8 copy.47
  829.4 0.8 copy.48
  (112 shorter events, 12.3 us)
Async XLA Ops:
  7.2 113.7 %copy-start = (f32[16,2]{0,1:T(2,128)S(1)}, f32[16,2]{0,1:T(2,128)}, u32[]{:S(2)}) copy-start(f32[16,2]{0,1:T(2,128)} %param.28) | copy-start | bytes 388
  7.2 52.1 %all-gather.6.cloned.1.call-start = ((), (), s32[]{:S(2)}) async-start(), calls=%async_computation.13 | async-start | bytes 7864320 | tf_op jit(solution)/shard_map/all_gather | solution.py:915
  9.9 267.3 %all-gather.8.cloned.1.call-start = ((), (), s32[]{:S(2)}) async-start(), calls=%async_computation.14 | async-start | bytes 2621440 | tf_op jit(solution)/shard_map/all_gather | solution.py:915
  10.6 1.3 copy-start.20
  10.6 1.9 copy-start.21
  10.7 266.5 %all-gather.10.cloned.1.call-start = ((), (), s32[]{:S(2)}) async-start(), calls=%async_computation.15 | async-start | bytes 10485760 | tf_op jit(solution)/shard_map/all_gather | solution.py:915
  11.4 265.8 %all-gather.12.cloned.1.call-start = ((), (), s32[]{:S(2)}) async-start(), calls=%async_computation.16 | async-start | bytes 10485760 | tf_op jit(solution)/shard_map/all_gather | solution.py:915
  70.2 45.8 %all-to-all-start = ((bf16[8,208,512]{2,1,0:T(8,128)(2,1)}), bf16[8,208,512]{2,1,0:T(8,128)(2,1)S(1)}, u32[]{:S(2)}, u32[]{:S(2)}) async-start(bf16[8,208,512]{2,1,0:T(8,128)(2,1)} %get-tuple-element.118), calls=%async_computation | async-start | bytes 3407872 | tf_op jit(solution)/shard_map/all_to_all | solution.py:918
  75.7 201.4 %all-gather.14.cloned.1.call-start = ((), (), s32[]{:S(2)}) async-start(), calls=%async_computation.17 | async-start | bytes 10485760 | tf_op jit(solution)/shard_map/all_gather | solution.py:915
  87.3 33.0 %copy-start.22 = (s32[2,1]{0,1:T(1,128)S(1)}, s32[2,1]{0,1:T(1,128)}, u32[]{:S(2)}) copy-start(s32[2,1]{0,1:T(1,128)} %param.20) | copy-start | bytes 28
  116.0 15.8 %copy-start.7 = (bf16[8,208,512]{2,1,0:T(8,128)(2,1)}, bf16[8,208,512]{2,1,0:T(8,128)(2,1)S(1)}, u32[]{:S(2)}) copy-start(bf16[8,208,512]{2,1,0:T(8,128)(2,1)S(1)} %all-to-all-done.ids_ref) | copy-start | bytes 5111812
  116.0 40.9 %all-to-all-start.1 = ((bf16[8,192,512]{2,1,0:T(8,128)(2,1)}), bf16[8,192,512]{2,1,0:T(8,128)(2,1)}, u32[]{:S(2)}, u32[]{:S(2)}) async-start(bf16[8,192,512]{2,1,0:T(8,128)(2,1)} %get-tuple-element.120), calls=%async_computation.1 | async-start | bytes 3145728 | tf_op jit(solution)/shard_map/all_to_all | solution.py:918
  120.3 3.9 collective-permute-start.1
  120.3 3.2 collective-permute-start
  156.9 43.6 %all-to-all-start.2 = ((bf16[8,208,512]{2,1,0:T(8,128)(2,1)}), bf16[8,208,512]{2,1,0:T(8,128)(2,1)S(1)}, u32[]{:S(2)}, u32[]{:S(2)}) async-start(bf16[8,208,512]{2,1,0:T(8,128)(2,1)} %get-tuple-element.124), calls=%async_computation.2 | async-start | bytes 3407872 | tf_op jit(solution)/shard_map/all_to_all | solution.py:918
  183.8 25.3 %copy-start.9 = (bf16[8,64,512]{2,1,0:T(8,128)(2,1)S(1)}, bf16[8,64,512]{2,1,0:T(8,128)(2,1)}, u32[]{:S(2)}) copy-start(bf16[8,64,512]{2,1,0:T(8,128)(2,1)} %get-tuple-element.136.mixed_ref) | copy-start | bytes 1572868
  200.5 9.6 %copy-start.8 = (bf16[8,208,512]{2,1,0:T(8,128)(2,1)}, bf16[8,208,512]{2,1,0:T(8,128)(2,1)S(1)}, u32[]{:S(2)}) copy-start(bf16[8,208,512]{2,1,0:T(8,128)(2,1)S(1)} %all-to-all-done.2.ids_ref) | copy-start | bytes 5111812
  200.5 40.9 %all-to-all-start.3 = ((bf16[8,192,512]{2,1,0:T(8,128)(2,1)}), bf16[8,192,512]{2,1,0:T(8,128)(2,1)}, u32[]{:S(2)}, u32[]{:S(2)}) async-start(bf16[8,192,512]{2,1,0:T(8,128)(2,1)} %get-tuple-element.128), calls=%async_computation.3 | async-start | bytes 3145728 | tf_op jit(solution)/shard_map/all_to_all | solution.py:918
  204.8 5.3 collective-permute-start.2
  204.9 4.2 collective-permute-start.4
  241.5 29.8 %all-to-all-start.4 = ((bf16[8,128,512]{2,1,0:T(8,128)(2,1)}), bf16[8,128,512]{2,1,0:T(8,128)(2,1)S(1)}, u32[]{:S(2)}, u32[]{:S(2)}) async-start(bf16[8,128,512]{2,1,0:T(8,128)(2,1)} %pad_maximum_fusion.2), calls=%async_computation.4 | async-start | bytes 2097152 | tf_op jit(solution)/shard_map/all_to_all | solution.py:918
  245.3 18.1 %collective-permute-start.3 = (bf16[8,64,512]{2,1,0:T(8,128)(2,1)}, bf16[8,64,512]{2,1,0:T(8,128)(2,1)S(1)}, u32[]{:S(2)}, u32[]{:S(2)}) collective-permute-start(bf16[8,64,512]{2,1,0:T(8,128)(2,1)} %get-tuple-element.135.mixed_ref), channel_id=1, source_target_pairs={{0,8},{1,9},{2,10},{3,11},{4,12},{5,13},{6,14},{7,15},{8,0},{9,1},... | collective-permute-start | bytes 1572872 | tf_op jit(solution)/shard_map/ppermute | solution.py:927
  271.2 1.0 copy-start.5
  272.2 47.3 %all-to-all-start.5 = ((bf16[8,128,512]{2,1,0:T(8,128)(2,1)}), bf16[8,128,512]{2,1,0:T(8,128)(2,1)S(1)}, u32[]{:S(2)}, u32[]{:S(2)}) async-start(bf16[8,128,512]{2,1,0:T(8,128)(2,1)} %pad_maximum_fusion.1), calls=%async_computation.5 | async-start | bytes 2097152 | tf_op jit(solution)/shard_map/all_to_all | solution.py:918
  319.5 7.7 copy-start.4
  319.5 50.0 %all-to-all-start.6 = ((bf16[8,128,512]{2,1,0:T(8,128)(2,1)}), bf16[8,128,512]{2,1,0:T(8,128)(2,1)}, u32[]{:S(2)}, u32[]{:S(2)}) async-start(bf16[8,128,512]{2,1,0:T(8,128)(2,1)} %bitcast.50), calls=%async_computation.6 | async-start | bytes 2097152 | tf_op jit(solution)/shard_map/all_to_all | solution.py:918
  369.5 31.2 %all-to-all-start.7 = ((bf16[8,128,512]{2,1,0:T(8,128)(2,1)}), bf16[8,128,512]{2,1,0:T(8,128)(2,1)S(1)}, u32[]{:S(2)}, u32[]{:S(2)}) async-start(bf16[8,128,512]{2,1,0:T(8,128)(2,1)} %bitcast.51), calls=%async_computation.7 | async-start | bytes 2097152 | tf_op jit(solution)/shard_map/all_to_all | solution.py:918
  375.5 449.4 %reduce-scatter.2.cloned.1.call-start = ((), (), s32[]{:S(2)}) async-start(), calls=%async_computation.18 | async-start | bytes 29196288 | tf_op jit(solution)/shard_map/reduce_scatter | solution.py:1063
  400.7 36.1 %copy-start.6 = (bf16[8,128,512]{2,1,0:T(8,128)(2,1)}, bf16[8,128,512]{2,1,0:T(8,128)(2,1)S(1)}, u32[]{:S(2)}) copy-start(bf16[8,128,512]{2,1,0:T(8,128)(2,1)S(1)} %all-to-all-done.7.grad_ref) | copy-start | bytes 3145732
  434.5 4.0 collective-permute-start.5
  436.8 43.3 %collective-permute-start.6 = (bf16[8,64,512]{2,1,0:T(8,128)(2,1)S(1)}, bf16[8,64,512]{2,1,0:T(8,128)(2,1)S(1)}, u32[]{:S(2)}, u32[]{:S(2)}) collective-permute-start(bf16[8,64,512]{2,1,0:T(8,128)(2,1)S(1)} %slice.81), channel_id=1, source_target_pairs={{0,8},{1,9},{2,10},{3,11},{4,12},{5,13},{6,14},{7,15},{8,0},{9,1},... | collective-permute-start | bytes 1572872 | tf_op jit(solution)/shard_map/ppermute | solution.py:927
  480.1 0.8 copy-start.25
  481.0 46.1 %all-to-all-start.8 = ((bf16[8,192,512]{2,1,0:T(8,128)(2,1)}), bf16[8,192,512]{2,1,0:T(8,128)(2,1)S(1)}, u32[]{:S(2)}, u32[]{:S(2)}) async-start(bf16[8,192,512]{2,1,0:T(8,128)(2,1)} %get-tuple-element.177), calls=%async_computation.8 | async-start | bytes 3145728 | tf_op jit(solution)/shard_map/all_to_all | solution.py:918
  494.2 3.8 collective-permute-start.7
  527.1 42.9 %copy-start.2 = (bf16[8,192,512]{2,1,0:T(8,128)(2,1)}, bf16[8,192,512]{2,1,0:T(8,128)(2,1)S(1)}, u32[]{:S(2)}) copy-start(bf16[8,192,512]{2,1,0:T(8,128)(2,1)S(1)} %all-to-all-done.8.rest_0_) | copy-start | bytes 4718596
  527.1 85.3 %all-to-all-start.9 = ((bf16[8,192,512]{2,1,0:T(8,128)(2,1)}), bf16[8,192,512]{2,1,0:T(8,128)(2,1)}, u32[]{:S(2)}, u32[]{:S(2)}) async-start(bf16[8,192,512]{2,1,0:T(8,128)(2,1)} %collective-permute-done.7), calls=%async_computation.9 | async-start | bytes 3145728 | tf_op jit(solution)/shard_map/all_to_all | solution.py:918
  612.3 58.9 %all-to-all-start.10 = ((bf16[8,192,512]{2,1,0:T(8,128)(2,1)}), bf16[8,192,512]{2,1,0:T(8,128)(2,1)S(1)}, u32[]{:S(2)}, u32[]{:S(2)}) async-start(bf16[8,192,512]{2,1,0:T(8,128)(2,1)} %get-tuple-element.185), calls=%async_computation.10 | async-start | bytes 3145728 | tf_op jit(solution)/shard_map/all_to_all | solution.py:918
  667.3 9.8 %copy-start.26 = (s32[32]{0:T(128)S(1)}, s32[32]{0:T(128)}, u32[]{:S(2)}) copy-start(s32[32]{0:T(128)} %constant.42.clone) | copy-start | bytes 388
  667.3 9.9 %copy-start.23 = (s32[32]{0:T(128)S(1)}, s32[32]{0:T(128)}, u32[]{:S(2)}) copy-start(s32[32]{0:T(128)} %constant.44.clone) | copy-start | bytes 388
  667.3 9.9 %copy-start.24 = (s32[32]{0:T(128)S(1)}, s32[32]{0:T(128)}, u32[]{:S(2)}) copy-start(s32[32]{0:T(128)} %constant.43.clone) | copy-start | bytes 388
  667.3 10.5 %copy-start.13 = (f32[1,1024]{1,0:T(1,128)S(1)}, f32[1,1024]{1,0:T(1,128)}, u32[]{:S(2)}) copy-start(f32[1,1024]{1,0:T(1,128)} %get-tuple-element.143) | copy-start | bytes 12292
  667.3 10.5 %copy-start.14 = (f32[1,1024]{1,0:T(1,128)S(1)}, f32[1,1024]{1,0:T(1,128)}, u32[]{:S(2)}) copy-start(f32[1,1024]{1,0:T(1,128)} %get-tuple-element.152) | copy-start | bytes 12292
  667.4 10.5 %copy-start.15 = (f32[8,128]{1,0:T(8,128)S(1)}, f32[8,128]{1,0:T(8,128)}, u32[]{:S(2)}) copy-start(f32[8,128]{1,0:T(8,128)} %get-tuple-element.172) | copy-start | bytes 12292
  667.4 10.5 %copy-start.17 = (f32[8,128]{1,0:T(8,128)S(1)}, f32[8,128]{1,0:T(8,128)}, u32[]{:S(2)}) copy-start(f32[8,128]{1,0:T(8,128)} %get-tuple-element.181) | copy-start | bytes 12292
  667.4 10.5 %copy-start.16 = (f32[8,128]{1,0:T(8,128)S(1)}, f32[8,128]{1,0:T(8,128)}, u32[]{:S(2)}) copy-start(f32[8,128]{1,0:T(8,128)} %get-tuple-element.178) | copy-start | bytes 12292
  667.4 10.5 %copy-start.18 = (f32[8,128]{1,0:T(8,128)S(1)}, f32[8,128]{1,0:T(8,128)}, u32[]{:S(2)}) copy-start(f32[8,128]{1,0:T(8,128)} %get-tuple-element.186) | copy-start | bytes 12292
  667.4 3.8 collective-permute-start.8
  671.2 18.5 %copy-start.3 = (bf16[8,192,512]{2,1,0:T(8,128)(2,1)}, bf16[8,192,512]{2,1,0:T(8,128)(2,1)S(1)}, u32[]{:S(2)}) copy-start(bf16[8,192,512]{2,1,0:T(8,128)(2,1)S(1)} %all-to-all-done.10.rest_0_) | copy-start | bytes 4718596
  671.2 64.5 %all-to-all-start.11 = ((bf16[8,192,512]{2,1,0:T(8,128)(2,1)}), bf16[8,192,512]{2,1,0:T(8,128)(2,1)}, u32[]{:S(2)}, u32[]{:S(2)}) async-start(bf16[8,192,512]{2,1,0:T(8,128)(2,1)} %collective-permute-done.8), calls=%async_computation.11 | async-start | bytes 3145728 | tf_op jit(solution)/shard_map/all_to_all | solution.py:918
  735.7 11.6 %copy-start.19 = (f32[1,1024]{1,0:T(1,128)S(1)}, f32[1,1024]{1,0:T(1,128)}, u32[]{:S(2)}) copy-start(f32[1,1024]{1,0:T(1,128)} %get-tuple-element.192) | copy-start | bytes 12292
  828.5 1.8 copy-start.12
  828.5 2.4 copy-start.11
  828.5 3.7 copy-start.1
  828.5 3.1 copy-start.10
Sparse Core Ops, SparseCore 0:
  10.2 49.0 all-gather.5
  60.8 22.5 all-gather.7
  85.0 58.2 all-gather.9
  144.8 58.2 all-gather.11
  204.5 58.2 all-gather.13
  433.5 371.8 reduce-scatter.1

commit v2 on v1

--- a/solution.py
+++ b/solution.py
@@ -518,7 +518,7 @@
     width, model = tokens.shape[2:]
     out_w, gate_w, up_w, down_w = weights
     ffn = gate_w.shape[1]
-    block = 512
+    block = 1024
 
     def fixed(a):
         return pl.BlockSpec(a.shape, lambda f, *_: (0,) * a.ndim)
@@ -989,6 +989,7 @@
 
     def run_backward(u, h, token):
         if swap:
+            token = token + ((heads_cross[1],) if (u, h) == (0, 1) else ())
             grad = grad_heads[u] if h == 0 else heads_cross[u]
             mixed = mixed_part[u, h]
         else:
@@ -1045,24 +1046,46 @@
                 )
             ]
         part = ffn // fold
-        spare = -(-(3 * part + model // fold) // 384) * 384
+        narrow = model // fold
+        spare = -(-(2 * part + narrow) // 384) * 384
         struct = jax.ShapeDtypeStruct((devices, fold, rows, spare), BF16)
         down = pl.BlockSpec((512 // tall, fold, rows, model), lambda n: (n, 0, 0, 0))
         gate = pl.BlockSpec((devices, 1, rows, part), lambda n: (0, n, 0, 1))
-        up = pl.BlockSpec((devices, 1, rows, part), lambda n: (0, n, 0, 2))
-        narrow = model // fold
-        out = pl.BlockSpec((devices, 1, rows, narrow), lambda n: (0, n, 0, 3 * part // narrow))
-        firsts = [after(middle[0][4], *token)] + [item[4] for item in middle[1:]]
+        out = pl.BlockSpec((devices, 1, rows, narrow), lambda n: (0, n, 0, 2 * part // narrow))
+        table = after(places_of(orders[0]), *token)
+        up = picked_grads(table, [(0, devices)], column(0), column(3), rows, False, 2, 1024, "up_grad")
+        holder["streams"] = [[up[0], permute(up[1], orders[0][0]), orders[0][1:]]]
+        firsts = [after(middle[0][4], up[0])] + [item[4] for item in middle[1:]]
         terms = weight_grad(column(1), firsts, True, struct, down, ffn // 512, None, "down_grad")
-        rights = [after(middle[0][2], *holder["flying"])] + [item[2] for item in middle[1:]]
+        landed = (holder["streams"][0][1],) + ((heads_cross[0],) if swap else ())
+        rights = [after(middle[0][2], *holder["flying"], *landed)] + [item[2] for item in middle[1:]]
         terms = weight_grad(column(0), rights, False, struct, gate, fold, terms, "gate_grad")
-        terms = weight_grad(column(0), column(3), False, struct, up, fold, terms, "up_grad")
         mixed_all = [mixed_tok[u] for u in range(len(units))]
         terms = weight_grad(mixed_all, column(6), False, struct, out, fold, terms, "out_grad")
         terms = terms.reshape(ffn, spare)
         holder["owned"] = lax.psum_scatter(terms, ("shard", "seq"), scatter_dimension=0, tiled=True)
         return terms
 
+    def wide_sum(a, b):
+        return a.astype(F32) + b.astype(F32)
+
+    def advance(token):
+        out = ()
+        if not direct:
+            return out
+        for stream in holder["streams"]:
+            keep, came, masks = stream
+            if not masks:
+                continue
+            keep = after(keep, *token)
+            half = keep.shape[0] // 2
+            send = wide_sum(keep[half:], came[half:]).astype(BF16)
+            stream[0] = wide_sum(keep[:half], came[:half]).astype(BF16)
+            stream[1] = permute(send, masks[0])
+            stream[2] = masks[1:]
+            out = out + (send, stream[0])
+        return out
+
     holder = {}
 
     def weights_work(token):
@@ -1090,7 +1113,6 @@
             grad_heads[u] = moved
             if swap:
                 heads_cross[u] = cross(moved[:, head_dim:])
-                pending.append(heads_cross[u])
 
         return lambda: middle[u][7].reshape(count, here * head_dim, width), keep
 
@@ -1143,13 +1165,14 @@
             steps += [(work(run_backward, *at), None), (None, send_back(*at))]
         steps += [(work(run_final, u), None) for u in range(total)]
 
+    late = [task for task, _ in steps[-2:]]
     token = ()
-    pending = []
     for task, send in steps:
         done = ()
         moved = None
-        waited = tuple(pending)
-        pending.clear()
+        if "streams" in holder:
+            leaving = advance(token)
+            token = token if task in late else token + leaving
         if send is not None:
             moved = exchange(after(send[0](), *token))
             done = (moved,)
@@ -1158,7 +1181,7 @@
             done = done + (task(token),)
         if send is not None:
             send[1](after(moved, *done[1:]))
-        token = done + waited
+        token = done
     acc_bias = jnp.concatenate(
         [sum(bias_terms[u, h] for u in range(total))[0:1, 0:2] for h in range(here)], axis=0
     )
@@ -1170,6 +1193,10 @@
     gain_attn = sum(item[3][0] for item in finals)
     gain_ffn = sum(item[8][0] for item in middle)
     if direct:
+        while holder["streams"][0][2]:
+            advance(token)
+        keep, came, _ = holder["streams"][0]
+        up_own = wide_sum(after(keep, *token), came)
         owned, part = holder["owned"], ffn // fold
 
         def joined(start, size):
@@ -1177,8 +1204,7 @@
             return jnp.swapaxes(piece, 0, 1).reshape(rows, fold * size).astype(F32)
 
         down_own = owned[:, :part].astype(F32)
-        gate_own, up_own = joined(part, part), joined(2 * part, part)
-        out_own = joined(3 * part, model // fold)
+        gate_own, out_own = joined(part, part), joined(2 * part, model // fold)
         table = jnp.concatenate([places_of(order) for order in orders])
         attn_terms = picked_grads(
             table, [(i * devices, devices) for i in range(3)], flats,

time: 836 us -> 849 us (1.016); the launches traced: 840 us -> 841 us
  Pallas kernels: 460 us -> 402 us
  waiting for transfers between devices: 270 us -> 304 us
  other arithmetic: 14.1 us -> 30.3 us
  starting transfers between devices: 66.2 us -> 79.5 us
    pallas_call x4, Pallas kernels: 135 us -> 104 us  [attend_backward(): pl.pallas_call(functools.partial(backward_kernel, (local, head_dim, block...]
    ppermute x9 -> x14, waiting for transfers between devices: 14.3 us -> 45.3 us  [permute(): lax.ppermute(value, ('shard', 'seq'), [(i, i ^ mask) for i in range(devic...]
    ppermute x9 -> x14, starting transfers between devices: 4.12 us -> 19.9 us  [permute(): lax.ppermute(value, ('shard', 'seq'), [(i, i ^ mask) for i in range(devic...]
    pallas_call x1, Pallas kernels: 61.1 us -> 45.5 us  [reduce_rows(): pl.pallas_call(functools.partial(reduce_kernel, orders, count), in_specs=...]
    pallas_call x4, Pallas kernels: 76 us -> 61.5 us  [attend_forward(): pl.pallas_call(functools.partial(forward_kernel, (local, head_dim, block,...]
    convert_element_type x0 -> x4, other arithmetic: none -> 14 us  [advance(): stream[0] = wide_sum(keep[:half], came[:half]).astype(BF16)]
    pallas_call x1 -> x2, Pallas kernels: 11.9 us -> 25.7 us  [picked_grads(): pl.pallas_call(functools.partial(picked_kernel, units, rows, places, flip...]
    pallas_call x4 -> x3, Pallas kernels: 46.9 us -> 33.5 us  [weight_grad(): pl.pallas_call(functools.partial(weights_kernel, units), grid=(steps,), i...]
  transfers between devices with their start and end apart: 27 -> 32, of which waited for: 15 -> 15; matrix products, arithmetic and copies ran while one was open for 2% -> 4% of each run, Pallas kernels for 51% -> 44%
where the time goes in v2:
time: 849 us; the launch traced here: 841 us
  Pallas kernels  402 us (47%)
  waiting for transfers between devices  304 us (36%)
  starting transfers between devices  79.5 us (9%)
  other arithmetic  30.3 us (4%)
  between operations  15 us (2%)
  local copies, waits for them, and re-layouts  11.1 us (1%)
    all_to_all x12, waiting for transfers between devices, exchange(): lax.all_to_all(values, 'seq', split_axis=0, concat_axis=0, tiled=True)  210 us
    pallas_call x4, Pallas kernels, attend_backward(): pl.pallas_call(functools.partial(backward_kernel, (local, head_dim, block...  104 us
    pallas_call x2, Pallas kernels, middle_part(): pl.pallas_call(functools.partial(middle_kernel, (head_dim, output is not...  86.3 us
    pallas_call x4, Pallas kernels, attend_forward(): pl.pallas_call(functools.partial(forward_kernel, (local, head_dim, block,...  61.5 us
    all_to_all x12, starting transfers between devices, exchange(): lax.all_to_all(values, 'seq', split_axis=0, concat_axis=0, tiled=True)  59.3 us
    pallas_call x1, Pallas kernels, reduce_rows(): pl.pallas_call(functools.partial(reduce_kernel, orders, count), in_specs=...  45.5 us
    all_gather x5, waiting for transfers between devices, gather(): return lax.all_gather(weight, 'shard', axis=0, tiled=True)  45.5 us
    ppermute x14, waiting for transfers between devices, permute(): lax.ppermute(value, ('shard', 'seq'), [(i, i ^ mask) for i in range(devic...  45.3 us
  transfers between devices with their start and end apart: 32, of which 15 were waited for; matrix products, arithmetic and copies ran while one was open for 4% of the time, Pallas kernels for 44%

profile of v2, /device:TPU:0, one launch (start us, length us, event | category | flops | bytes accessed | tf_op | source)
XLA Modules:
  0.0 841.0 jit_solution(4778756097173012760)
XLA Ops:
  7.2 2.6 pad_maximum_fusion
  12.6 1.2 multiply_sine_fusion
  13.8 45.5 %all-gather.6.cloned.1.call-done.query_ref.key_ref.value_ref = bf16[1024,3072]{1,0:T(8,128)(2,1)} async-done(((bf16[256,3072]{1,0:T(8,128)(2,1)}), bf16[1024,3072]{1,0:T(8,128)(2,1)}) %all-gather.6.cloned.1.call-update) | async-done | bytes 6291472 | tf_op jit(solution)/shard_map/all_gather | solution.py:915
  59.3 10.9 %project.2 = (bf16[1024,512]{1,0:T(8,128)(2,1)}, bf16[8,192,512]{2,1,0:T(8,128)(2,1)}, bf16[8,208,512]{2,1,0:T(8,128)(2,1)}) custom-call(s32[1]{0:T(128)} %bitcast.2.core_ref, bf16[2,1,512,1024]{3,2,1,0:T(8,128)(2,1)} %tokens_ref.11, f32[1,1024]{1,0:T(1,128)} %bitcast.48, bf16[1024,3072]{1,0:T(8,128)(2,1)} %all-gather.6.cloned.1.call-done.query_ref.key_ref.value_ref, ...), custom_call_target="tpu_custom_call" | custom-call | flops 201326592 | bytes 12582912 | tf_op jit(solution)/shard_map/project/pallas_call | solution.py:420
  70.2 5.5 all-to-all-start
  76.3 11.0 %project.3 = (bf16[1024,512]{1,0:T(8,128)(2,1)}, bf16[8,192,512]{2,1,0:T(8,128)(2,1)}, bf16[8,208,512]{2,1,0:T(8,128)(2,1)}) custom-call(s32[1]{0:T(128)} %bitcast.2.core_ref, bf16[2,1,512,1024]{3,2,1,0:T(8,128)(2,1)} %tokens_ref.11, f32[1,1024]{1,0:T(1,128)} %bitcast.49, bf16[1024,3072]{1,0:T(8,128)(2,1)} %all-gather.6.cloned.1.call-done.query_ref.key_ref.value_ref, ...), custom_call_target="tpu_custom_call" | custom-call | flops 201326592 | bytes 12582912 | tf_op jit(solution)/shard_map/project/pallas_call | solution.py:420
  87.3 28.7 %all-to-all-done.ids_ref = bf16[8,208,512]{2,1,0:T(8,128)(2,1)S(1)} async-done(((bf16[8,208,512]{2,1,0:T(8,128)(2,1)}), bf16[8,208,512]{2,1,0:T(8,128)(2,1)S(1)}, u32[]{:S(2)}, u32[]{:S(2)}) %all-to-all-start) | async-done | bytes 1703968 | tf_op jit(solution)/shard_map/all_to_all | solution.py:918
  116.0 4.3 all-to-all-start.1
  121.5 2.0 collective-permute-done
  124.2 27.5 %attend_forward.4 = (bf16[8,64,512]{2,1,0:T(8,128)(2,1)}, f32[8,1,512]{2,1,0:T(1,128)}) custom-call(s32[1]{0:T(128)} %bitcast.8.len_ref, f32[1,2]{1,0:T(1,128)} %copy.43.bias_ref, bf16[8,208,512]{2,1,0:T(8,128)(2,1)} %collective-permute-done.1.x_ref.ids_ref, bf16[8,208,512]{2,1,0:T(8,128)(2,1)} %collective-permute-done.1.x_ref.ids_ref), custom_call_target="tpu_custom_call" | custom-call | flops 2147483648 | bytes 3407872 | tf_op jit(solution)/shard_map/attend_forward/pallas_call | solution.py:171
  151.7 5.1 all-to-all-done.1.x_ref
  156.9 3.6 all-to-all-start.2
  161.1 7.6 attend_forward.5
  168.7 31.8 %all-to-all-done.2.ids_ref = bf16[8,208,512]{2,1,0:T(8,128)(2,1)S(1)} async-done(((bf16[8,208,512]{2,1,0:T(8,128)(2,1)}), bf16[8,208,512]{2,1,0:T(8,128)(2,1)S(1)}, u32[]{:S(2)}, u32[]{:S(2)}) %all-to-all-start.2) | async-done | bytes 1703968 | tf_op jit(solution)/shard_map/all_to_all | solution.py:918
  200.5 4.3 all-to-all-start.3
  205.4 3.7 collective-permute-done.4
  210.2 14.9 %attend_forward.6 = (bf16[8,64,512]{2,1,0:T(8,128)(2,1)}, f32[8,1,512]{2,1,0:T(1,128)}) custom-call(s32[1]{0:T(128)} %bitcast.10.len_ref, f32[1,2]{1,0:T(1,128)} %copy.43.bias_ref, bf16[8,208,512]{2,1,0:T(8,128)(2,1)} %collective-permute-done.2.x_ref.ids_ref, bf16[8,208,512]{2,1,0:T(8,128)(2,1)} %collective-permute-done.2.x_ref.ids_ref), custom_call_target="tpu_custom_call" | custom-call | flops 2147483648 | bytes 3407872 | tf_op jit(solution)/shard_map/attend_forward/pallas_call | solution.py:171
  225.1 16.4 %all-to-all-done.3.x_ref = bf16[8,192,512]{2,1,0:T(8,128)(2,1)} async-done(((bf16[8,192,512]{2,1,0:T(8,128)(2,1)}), bf16[8,192,512]{2,1,0:T(8,128)(2,1)}, u32[]{:S(2)}, u32[]{:S(2)}) %all-to-all-start.3) | async-done | bytes 1572896 | tf_op jit(solution)/shard_map/all_to_all | solution.py:918
  241.5 3.9 all-to-all-start.4
  245.4 11.5 %attend_forward.7 = (bf16[8,64,512]{2,1,0:T(8,128)(2,1)}, f32[8,1,512]{2,1,0:T(1,128)}) custom-call(s32[1]{0:T(128)} %bitcast.len_ref, f32[1,2]{1,0:T(1,128)} %copy.43.bias_ref, bf16[8,192,512]{2,1,0:T(8,128)(2,1)} %all-to-all-done.3.x_ref, bf16[8,208,512]{2,1,0:T(8,128)(2,1)} %copy-done.9), custom_call_target="tpu_custom_call" | custom-call | flops 2147483648 | bytes 3145728 | tf_op jit(solution)/shard_map/attend_forward/pallas_call | solution.py:171
  256.9 2.1 pad_maximum_fusion.1
  259.0 12.3 %all-to-all-done.4 = bf16[8,128,512]{2,1,0:T(8,128)(2,1)S(1)} async-done(((bf16[8,128,512]{2,1,0:T(8,128)(2,1)}), bf16[8,128,512]{2,1,0:T(8,128)(2,1)S(1)}, u32[]{:S(2)}, u32[]{:S(2)}) %all-to-all-start.4) | async-done | bytes 1048608 | tf_op jit(solution)/shard_map/all_to_all | solution.py:918
  272.2 3.6 all-to-all-start.5
  275.9 1.2 add_add_fusion.1.info_ref
  277.1 43.2 %middle_part.2 = (bf16[2,1,512,1024]{3,2,1,0:T(8,128)(2,1)}, bf16[1024,512]{1,0:T(8,128)(2,1)}, bf16[1024,512]{1,0:T(8,128)(2,1)}, bf16[4096,512]{1,0:T(8,128)(2...) custom-call(s32[3]{0:T(128)} %add_add_fusion.1.info_ref, ...), custom_call_target="tpu_custom_call" | custom-call | flops 1610612736 | bytes 33554432 | tf_op jit(solution)/shard_map/middle_part/pallas_call | solution.py:543
  320.3 6.5 all-to-all-start.6
  326.8 1.2 add_add_fusion.info_ref
  328.5 43.2 %middle_part.3 = (bf16[2,1,512,1024]{3,2,1,0:T(8,128)(2,1)}, bf16[1024,512]{1,0:T(8,128)(2,1)}, bf16[1024,512]{1,0:T(8,128)(2,1)}, bf16[4096,512]{1,0:T(8,128)(2...) custom-call(s32[3]{0:T(128)} %add_add_fusion.info_ref, ...), custom_call_target="tpu_custom_call", output_to_operand_aliasing={{0}: (9, {})} | custom-call | flops 1610612736 | bytes 33554432 | tf_op jit(solution)/shard_map/middle_part/pallas_call | solution.py:543
  371.7 13.8 %up_grad.1 = (bf16[512,4096]{1,0:T(8,128)(2,1)}, bf16[512,4096]{1,0:T(8,128)(2,1)}) custom-call(s32[32]{0:T(128)} %broadcast_xor_fusion.2.table_ref, bf16[1024,512]{1,0:T(8,128)(2,1)} %get-tuple-element.166.refs_0_, bf16[1024,512]{1,0:T(8,128)(2,1)} %get-tuple-element.167.refs_1_, bf16[512,4096]{1,0:T(8,128)(2,1)} %get-tuple-element.170.refs_2_, ...), custom_call_target="tpu_custom_call" | custom-call | flops 536870912 | bytes 16777216 | tf_op jit(solution)/shard_map/up_grad/pallas_call | solution.py:714
  385.5 6.0 all-to-all-start.7
  393.1 14.1 %down_grad.1.refs_4_ = bf16[32,4,32,2304]{3,2,1,0:T(8,128)(2,1)} custom-call(bf16[4096,512]{1,0:T(8,128)(2,1)} %get-tuple-element.176.refs_0_, bf16[4096,512]{1,0:T(8,128)(2,1)} %get-tuple-element.177.refs_1_, bf16[512,1024]{1,0:T(8,128)(2,1)} %get-tuple-element.180.refs_2_, bf16[512,1024]{1,0:T(8,128)(2,1)} %get-tuple-element.181.refs_3_), custom_call_target="tpu_custom_call" | custom-call | flops 536870912 | bytes 8388608 | tf_op jit(solution)/shard_map/down_grad/pallas_call | solution.py:768
  407.2 10.7 %all-to-all-done.7.grad_ref = bf16[8,128,512]{2,1,0:T(8,128)(2,1)S(1)} async-done(((bf16[8,128,512]{2,1,0:T(8,128)(2,1)}), bf16[8,128,512]{2,1,0:T(8,128)(2,1)S(1)}, u32[]{:S(2)}, u32[]{:S(2)}) %all-to-all-start.7) | async-done | bytes 1048608 | tf_op jit(solution)/shard_map/all_to_all | solution.py:918
  418.0 13.4 %gate_grad.1.refs_4_ = bf16[32,4,32,2304]{3,2,1,0:T(8,128)(2,1)} custom-call(bf16[1024,512]{1,0:T(8,128)(2,1)} %get-tuple-element.166.refs_0_, bf16[1024,512]{1,0:T(8,128)(2,1)} %get-tuple-element.167.refs_1_, bf16[512,4096]{1,0:T(8,128)(2,1)} %get-tuple-element.174.refs_2_, ...), custom_call_target="tpu_custom_call", output_to_operand_aliasing={{}: (4, {})} | custom-call | flops 536870912 | bytes 8388608 | tf_op jit(solution)/shard_map/gate_grad/pallas_call | solution.py:768
  431.4 6.0 out_grad.1
  437.4 5.5 add_convert_fusion
  442.9 6.5 collective-permute-start.7
  449.4 9.7 %attend_backward.4 = (bf16[8,192,512]{2,1,0:T(8,128)(2,1)}, f32[8,128]{1,0:T(8,128)}) custom-call(s32[1]{0:T(128)} %bitcast.9.len_ref, f32[1,2]{1,0:T(1,128)} %copy.43.bias_ref, bf16[8,192,512]{2,1,0:T(8,128)(2,1)} %all-to-all-done.1.x_ref, bf16[8,208,512]{2,1,0:T(8,128)(2,1)} %copy-done.10, bf16[8,128,512]{2,1,0:T(8,128)(2,1)} %all-to-all-done.6.grad_ref, ...), custom_call_target="tpu_custom_call" | custom-call | flops 5368709120 | bytes 4718592 | tf_op jit(solution)/shard_map/attend_backward/pallas_call | solution.py:310
  459.1 35.8 %collective-permute-done.7 = bf16[256,4096]{1,0:T(8,128)(2,1)} collective-permute-done((bf16[256,4096]{1,0:T(8,128)(2,1)}, bf16[256,4096]{1,0:T(8,128)(2,1)}, u32[]{:S(2)}, u32[]{:S(2)}) %collective-permute-start.7) | collective-permute-done | bytes 2097184 | tf_op jit(solution)/shard_map/ppermute | solution.py:927
  494.9 4.3 add_convert_fusion.2
  499.3 4.7 all-to-all-start.8
  504.0 5.2 collective-permute-start.8
  509.2 1.7 collective-permute-start.10
  510.9 51.5 %attend_backward.5 = (bf16[8,192,512]{2,1,0:T(8,128)(2,1)}, f32[8,128]{1,0:T(8,128)}) custom-call(s32[1]{0:T(128)} %bitcast.8.len_ref, f32[1,2]{1,0:T(1,128)} %copy.43.bias_ref, bf16[8,208,512]{2,1,0:T(8,128)(2,1)} %collective-permute-done.1.x_ref.ids_ref, bf16[8,208,512]{2,1,0:T(8,128)(2,1)} %collective-permute-done.1.x_ref.ids_ref, ...), custom_call_target="tpu_custom_call" | custom-call | flops 5368709120 | bytes 5111808 | tf_op jit(solution)/shard_map/attend_backward/pallas_call | solution.py:310
  562.5 15.0 %all-to-all-done.8.rest_0_ = bf16[8,192,512]{2,1,0:T(8,128)(2,1)S(1)} async-done(((bf16[8,192,512]{2,1,0:T(8,128)(2,1)}), bf16[8,192,512]{2,1,0:T(8,128)(2,1)S(1)}, u32[]{:S(2)}, u32[]{:S(2)}) %all-to-all-start.8) | async-done | bytes 1572896 | tf_op jit(solution)/shard_map/all_to_all | solution.py:918
  577.5 3.3 add_convert_fusion.4
  580.8 4.3 all-to-all-start.9
  585.1 1.9 collective-permute-start.11
  587.0 18.0 %attend_backward.6 = (bf16[8,192,512]{2,1,0:T(8,128)(2,1)}, f32[8,128]{1,0:T(8,128)}) custom-call(s32[1]{0:T(128)} %bitcast.len_ref, f32[1,2]{1,0:T(1,128)} %copy.43.bias_ref, bf16[8,192,512]{2,1,0:T(8,128)(2,1)} %all-to-all-done.3.x_ref, bf16[8,208,512]{2,1,0:T(8,128)(2,1)} %copy-done.9, bf16[8,128,512]{2,1,0:T(8,128)(2,1)} %copy-done.6, ...), custom_call_target="tpu_custom_call" | custom-call | flops 5368709120 | bytes 4718592 | tf_op jit(solution)/shard_map/attend_backward/pallas_call | solution.py:310
  605.0 16.4 %all-to-all-done.9.rest_1_ = bf16[8,192,512]{2,1,0:T(8,128)(2,1)} async-done(((bf16[8,192,512]{2,1,0:T(8,128)(2,1)}), bf16[8,192,512]{2,1,0:T(8,128)(2,1)}, u32[]{:S(2)}, u32[]{:S(2)}) %all-to-all-start.9) | async-done | bytes 1572896 | tf_op jit(solution)/shard_map/all_to_all | solution.py:918
  622.2 6.1 all-to-all-start.10
  628.4 24.6 %attend_backward.7 = (bf16[8,192,512]{2,1,0:T(8,128)(2,1)}, f32[8,128]{1,0:T(8,128)}) custom-call(s32[1]{0:T(128)} %bitcast.10.len_ref, f32[1,2]{1,0:T(1,128)} %copy.43.bias_ref, bf16[8,208,512]{2,1,0:T(8,128)(2,1)} %collective-permute-done.2.x_ref.ids_ref, bf16[8,208,512]{2,1,0:T(8,128)(2,1)} %collective-permute-done.2.x_ref.ids_ref, ...), custom_call_target="tpu_custom_call" | custom-call | flops 5368709120 | bytes 5111808 | tf_op jit(solution)/shard_map/attend_backward/pallas_call | solution.py:310
  653.1 3.7 collective-permute-done.12
  656.9 32.6 %all-to-all-done.10.rest_0_ = bf16[8,192,512]{2,1,0:T(8,128)(2,1)S(1)} async-done(((bf16[8,192,512]{2,1,0:T(8,128)(2,1)}), bf16[8,192,512]{2,1,0:T(8,128)(2,1)S(1)}, u32[]{:S(2)}, u32[]{:S(2)}) %all-to-all-start.10) | async-done | bytes 1572896 | tf_op jit(solution)/shard_map/all_to_all | solution.py:918
  689.5 6.4 all-to-all-start.11
  696.6 3.0 collective-permute-start.13
  699.8 11.8 %final_part.2 = (bf16[2,1,512,1024]{3,2,1,0:T(8,128)(2,1)}, bf16[1024,512]{1,0:T(8,128)(2,1)}, bf16[1024,512]{1,0:T(8,128)(2,1)}, bf16[1024,512]{1,0:T(8,128)(2,1)}, f32[1,1024]{1,0:T(1,128)}) custom-call(s32[1]{0:T(128)} %bitcast.2.core_ref, bf16[2,1,512,1024]{3,2,1,0:T(8,128)(2,1)} %tokens_ref.11, f32[512,1024]{1,0:T(8,128)} %get-tuple-element.203.grad_res_ref, ...), custom_call_target="tpu_custom_call" | custom-call | flops 201326592 | bytes 12582912 | tf_op jit(solution)/shard_map/final_part/pallas_call | solution.py:657
  711.6 41.3 %all-to-all-done.11.rest_1_ = bf16[8,192,512]{2,1,0:T(8,128)(2,1)} async-done(((bf16[8,192,512]{2,1,0:T(8,128)(2,1)}), bf16[8,192,512]{2,1,0:T(8,128)(2,1)}, u32[]{:S(2)}, u32[]{:S(2)}) %all-to-all-start.11) | async-done | bytes 1572896 | tf_op jit(solution)/shard_map/all_to_all | solution.py:918
  752.9 11.4 %final_part.3 = (bf16[2,1,512,1024]{3,2,1,0:T(8,128)(2,1)}, bf16[1024,512]{1,0:T(8,128)(2,1)}, bf16[1024,512]{1,0:T(8,128)(2,1)}, bf16[1024,512]{1,0:T(8,128)(2,1)}, f32[1,1024]{1,0:T(1,128)}) custom-call(s32[1]{0:T(128)} %bitcast.2.core_ref, bf16[2,1,512,1024]{3,2,1,0:T(8,128)(2,1)} %tokens_ref.11, ...), custom_call_target="tpu_custom_call", output_to_operand_aliasing={{0}: (11, {})} | custom-call | flops 201326592 | bytes 12582912 | tf_op jit(solution)/shard_map/final_part/pallas_call | solution.py:657
  765.6 11.9 %attn_grads.1 = (bf16[1024,1024]{1,0:T(8,128)(2,1)}, bf16[1024,1024]{1,0:T(8,128)(2,1)}, bf16[1024,1024]{1,0:T(8,128)(2,1)}) custom-call(s32[96]{0:T(128)} %pad_add_fusion.table_ref, bf16[1024,512]{1,0:T(8,128)(2,1)} %get-tuple-element.120.refs_0_, bf16[1024,512]{1,0:T(8,128)(2,1)} %get-tuple-element.127.refs_1_, ...), custom_call_target="tpu_custom_call" | custom-call | flops 402653184 | bytes 12582912 | tf_op jit(solution)/shard_map/attn_grads/pallas_call | solution.py:714
  777.5 45.5 %reduce_rows.1 = (f32[32,1024]{1,0:T(8,128)}, f32[32,1024]{1,0:T(8,128)}, f32[32,1024]{1,0:T(8,128)}, f32[24,128]{1,0:T(8,128)}) custom-call(bf16[1024,1024]{1,0:T(8,128)(2,1)} %get-tuple-element.219.refs_0_, bf16[1024,1024]{1,0:T(8,128)(2,1)} %get-tuple-element.220.refs_1_, bf16[1024,1024]{1,0:T(8,128)(2,1)} %get-tuple-element.221.refs_2_, ...), custom_call_target="tpu_custom_call" | custom-call | tf_op jit(solution)/shard_map/reduce_rows/pallas_call | solution.py:871
  823.0 1.4 slice.148
  825.1 1.3 slice_bitcast_fusion
  826.4 1.8 convert_add_fusion
  828.2 1.9 slice_convert_fusion
  (130 shorter events, 17.8 us)
Async XLA Ops:
  7.2 113.7 %copy-start = (f32[16,2]{0,1:T(2,128)S(1)}, f32[16,2]{0,1:T(2,128)}, u32[]{:S(2)}) copy-start(f32[16,2]{0,1:T(2,128)} %param.29) | copy-start | bytes 388
  7.2 52.1 %all-gather.6.cloned.1.call-start = ((), (), s32[]{:S(2)}) async-start(), calls=%async_computation.13 | async-start | bytes 7864320 | tf_op jit(solution)/shard_map/all_gather | solution.py:915
  9.9 267.2 %all-gather.8.cloned.1.call-start = ((), (), s32[]{:S(2)}) async-start(), calls=%async_computation.14 | async-start | bytes 2621440 | tf_op jit(solution)/shard_map/all_gather | solution.py:915
  10.6 1.3 copy-start.22
  10.6 1.9 copy-start.23
  10.7 266.4 %all-gather.10.cloned.1.call-start = ((), (), s32[]{:S(2)}) async-start(), calls=%async_computation.15 | async-start | bytes 10485760 | tf_op jit(solution)/shard_map/all_gather | solution.py:915
  11.4 265.7 %all-gather.12.cloned.1.call-start = ((), (), s32[]{:S(2)}) async-start(), calls=%async_computation.16 | async-start | bytes 10485760 | tf_op jit(solution)/shard_map/all_gather | solution.py:915
  70.2 45.8 %all-to-all-start = ((bf16[8,208,512]{2,1,0:T(8,128)(2,1)}), bf16[8,208,512]{2,1,0:T(8,128)(2,1)S(1)}, u32[]{:S(2)}, u32[]{:S(2)}) async-start(bf16[8,208,512]{2,1,0:T(8,128)(2,1)} %get-tuple-element.126), calls=%async_computation | async-start | bytes 3407872 | tf_op jit(solution)/shard_map/all_to_all | solution.py:918
  75.7 201.4 %all-gather.14.cloned.1.call-start = ((), (), s32[]{:S(2)}) async-start(), calls=%async_computation.17 | async-start | bytes 10485760 | tf_op jit(solution)/shard_map/all_gather | solution.py:915
  87.3 33.1 %copy-start.24 = (s32[2,1]{0,1:T(1,128)S(1)}, s32[2,1]{0,1:T(1,128)}, u32[]{:S(2)}) copy-start(s32[2,1]{0,1:T(1,128)} %param.21) | copy-start | bytes 28
  116.0 35.8 %copy-start.10 = (bf16[8,208,512]{2,1,0:T(8,128)(2,1)}, bf16[8,208,512]{2,1,0:T(8,128)(2,1)S(1)}, u32[]{:S(2)}) copy-start(bf16[8,208,512]{2,1,0:T(8,128)(2,1)S(1)} %all-to-all-done.ids_ref) | copy-start | bytes 5111812
  116.0 40.9 %all-to-all-start.1 = ((bf16[8,192,512]{2,1,0:T(8,128)(2,1)}), bf16[8,192,512]{2,1,0:T(8,128)(2,1)}, u32[]{:S(2)}, u32[]{:S(2)}) async-start(bf16[8,192,512]{2,1,0:T(8,128)(2,1)} %get-tuple-element.128), calls=%async_computation.1 | async-start | bytes 3145728 | tf_op jit(solution)/shard_map/all_to_all | solution.py:918
  120.3 3.9 collective-permute-start.1
  120.4 3.2 collective-permute-start
  156.9 43.6 %all-to-all-start.2 = ((bf16[8,208,512]{2,1,0:T(8,128)(2,1)}), bf16[8,208,512]{2,1,0:T(8,128)(2,1)S(1)}, u32[]{:S(2)}, u32[]{:S(2)}) async-start(bf16[8,208,512]{2,1,0:T(8,128)(2,1)} %get-tuple-element.132), calls=%async_computation.2 | async-start | bytes 3407872 | tf_op jit(solution)/shard_map/all_to_all | solution.py:918
  168.7 40.3 %copy-start.11 = (bf16[8,64,512]{2,1,0:T(8,128)(2,1)S(1)}, bf16[8,64,512]{2,1,0:T(8,128)(2,1)}, u32[]{:S(2)}) copy-start(bf16[8,64,512]{2,1,0:T(8,128)(2,1)} %get-tuple-element.144.mixed_ref) | copy-start | bytes 1572868
  200.5 9.6 %copy-start.9 = (bf16[8,208,512]{2,1,0:T(8,128)(2,1)}, bf16[8,208,512]{2,1,0:T(8,128)(2,1)S(1)}, u32[]{:S(2)}) copy-start(bf16[8,208,512]{2,1,0:T(8,128)(2,1)S(1)} %all-to-all-done.2.ids_ref) | copy-start | bytes 5111812
  200.5 40.9 %all-to-all-start.3 = ((bf16[8,192,512]{2,1,0:T(8,128)(2,1)}), bf16[8,192,512]{2,1,0:T(8,128)(2,1)}, u32[]{:S(2)}, u32[]{:S(2)}) async-start(bf16[8,192,512]{2,1,0:T(8,128)(2,1)} %get-tuple-element.136), calls=%async_computation.3 | async-start | bytes 3145728 | tf_op jit(solution)/shard_map/all_to_all | solution.py:918
  204.8 5.3 collective-permute-start.2
  204.9 4.2 collective-permute-start.4
  241.5 29.8 %all-to-all-start.4 = ((bf16[8,128,512]{2,1,0:T(8,128)(2,1)}), bf16[8,128,512]{2,1,0:T(8,128)(2,1)S(1)}, u32[]{:S(2)}, u32[]{:S(2)}) async-start(bf16[8,128,512]{2,1,0:T(8,128)(2,1)} %pad_maximum_fusion.2), calls=%async_computation.4 | async-start | bytes 2097152 | tf_op jit(solution)/shard_map/all_to_all | solution.py:918
  245.3 11.5 %collective-permute-start.3 = (bf16[8,64,512]{2,1,0:T(8,128)(2,1)}, bf16[8,64,512]{2,1,0:T(8,128)(2,1)S(1)}, u32[]{:S(2)}, u32[]{:S(2)}) collective-permute-start(bf16[8,64,512]{2,1,0:T(8,128)(2,1)} %get-tuple-element.143.mixed_ref), channel_id=1, source_target_pairs={{0,8},{1,9},{2,10},{3,11},{4,12},{5,13},{6,14},{7,15},{8,0},{9,1},... | collective-permute-start | bytes 1572872 | tf_op jit(solution)/shard_map/ppermute | solution.py:927
  271.2 1.0 copy-start.5
  272.2 48.1 %all-to-all-start.5 = ((bf16[8,128,512]{2,1,0:T(8,128)(2,1)}), bf16[8,128,512]{2,1,0:T(8,128)(2,1)S(1)}, u32[]{:S(2)}, u32[]{:S(2)}) async-start(bf16[8,128,512]{2,1,0:T(8,128)(2,1)} %pad_maximum_fusion.1), calls=%async_computation.5 | async-start | bytes 2097152 | tf_op jit(solution)/shard_map/all_to_all | solution.py:918
  320.3 7.7 copy-start.28
  320.3 8.2 copy-start.4
  320.3 51.4 %all-to-all-start.6 = ((bf16[8,128,512]{2,1,0:T(8,128)(2,1)}), bf16[8,128,512]{2,1,0:T(8,128)(2,1)}, u32[]{:S(2)}, u32[]{:S(2)}) async-start(bf16[8,128,512]{2,1,0:T(8,128)(2,1)} %bitcast.43), calls=%async_computation.6 | async-start | bytes 2097152 | tf_op jit(solution)/shard_map/all_to_all | solution.py:918
  385.5 32.4 %collective-permute-start.5 = (bf16[512,4096]{1,0:T(8,128)(2,1)}, bf16[512,4096]{1,0:T(8,128)(2,1)}, u32[]{:S(2)}, u32[]{:S(2)}) collective-permute-start(bf16[512,4096]{1,0:T(8,128)(2,1)} %get-tuple-element.172), channel_id=1, source_target_pairs={{0,8},{1,9},{2,10},{3,11},{4,12},{5,13},{6,14},{7,15},{8,0},{9,1},... | collective-permute-start | bytes 12582920 | tf_op jit(solution)/shard_map/ppermute | solution.py:927
  385.5 32.4 %all-to-all-start.7 = ((bf16[8,128,512]{2,1,0:T(8,128)(2,1)}), bf16[8,128,512]{2,1,0:T(8,128)(2,1)S(1)}, u32[]{:S(2)}, u32[]{:S(2)}) async-start(bf16[8,128,512]{2,1,0:T(8,128)(2,1)} %bitcast.44), calls=%async_computation.7 | async-start | bytes 2097152 | tf_op jit(solution)/shard_map/all_to_all | solution.py:918
  391.5 436.7 %reduce-scatter.2.cloned.1.call-start = ((), (), s32[]{:S(2)}) async-start(), calls=%async_computation.18 | async-start | bytes 19464192 | tf_op jit(solution)/shard_map/reduce_scatter | solution.py:1066
  392.8 14.4 %collective-permute-start.6 = (bf16[8,64,512]{2,1,0:T(8,128)(2,1)S(1)}, bf16[8,64,512]{2,1,0:T(8,128)(2,1)}, u32[]{:S(2)}, u32[]{:S(2)}) collective-permute-start(bf16[8,64,512]{2,1,0:T(8,128)(2,1)S(1)} %slice.125), channel_id=1, source_target_pairs={{0,8},{1,9},{2,10},{3,11},{4,12},{5,13},{6,14},{7,15},{8,0},{9,1},... | collective-permute-start | bytes 1572872 | tf_op jit(solution)/shard_map/ppermute | solution.py:927
  418.0 13.4 %copy-start.6 = (bf16[8,128,512]{2,1,0:T(8,128)(2,1)}, bf16[8,128,512]{2,1,0:T(8,128)(2,1)S(1)}, u32[]{:S(2)}) copy-start(bf16[8,128,512]{2,1,0:T(8,128)(2,1)S(1)} %all-to-all-done.7.grad_ref) | copy-start | bytes 3145732
  442.9 52.0 %collective-permute-start.7 = (bf16[256,4096]{1,0:T(8,128)(2,1)}, bf16[256,4096]{1,0:T(8,128)(2,1)}, u32[]{:S(2)}, u32[]{:S(2)}) collective-permute-start(bf16[256,4096]{1,0:T(8,128)(2,1)} %get-tuple-element.241), channel_id=1, source_target_pairs={{0,16},{1,17},{2,18},{3,19},{4,20},{5,21},{6,22},{7,23},{8,24},{9,... | collective-permute-start | bytes 6291464 | tf_op jit(solution)/shard_map/ppermute | solution.py:927
  499.3 4.7 copy-start.7
  499.3 78.2 %all-to-all-start.8 = ((bf16[8,192,512]{2,1,0:T(8,128)(2,1)}), bf16[8,192,512]{2,1,0:T(8,128)(2,1)S(1)}, u32[]{:S(2)}, u32[]{:S(2)}) async-start(bf16[8,192,512]{2,1,0:T(8,128)(2,1)} %get-tuple-element.190), calls=%async_computation.8 | async-start | bytes 3145728 | tf_op jit(solution)/shard_map/all_to_all | solution.py:918
  504.0 7.0 collective-permute-start.8
  509.2 68.3 %collective-permute-start.10 = (bf16[128,4096]{1,0:T(8,128)(2,1)}, bf16[128,4096]{1,0:T(8,128)(2,1)}, u32[]{:S(2)}, u32[]{:S(2)}) collective-permute-start(bf16[128,4096]{1,0:T(8,128)(2,1)} %get-tuple-element.243), channel_id=1, source_target_pairs={{0,1},{1,0},{2,3},{3,2},{4,5},{5,4},{6,7},{7,6},{8,9},{9,8},{10,11... | collective-permute-start | bytes 3145736 | tf_op jit(solution)/shard_map/ppermute | solution.py:927
  562.5 18.3 %collective-permute-start.9 = (bf16[8,192,512]{2,1,0:T(8,128)(2,1)}, bf16[8,192,512]{2,1,0:T(8,128)(2,1)}, u32[]{:S(2)}, u32[]{:S(2)}) collective-permute-start(bf16[8,192,512]{2,1,0:T(8,128)(2,1)} %get-tuple-element.188), channel_id=1, source_target_pairs={{0,8},{1,9},{2,10},{3,11},{4,12},{5,13},{6,14},{7,15},{8,0},{9,1},... | collective-permute-start | bytes 4718600 | tf_op jit(solution)/shard_map/ppermute | solution.py:927
  577.5 3.3 copy-start.2
  580.8 40.6 %all-to-all-start.9 = ((bf16[8,192,512]{2,1,0:T(8,128)(2,1)}), bf16[8,192,512]{2,1,0:T(8,128)(2,1)}, u32[]{:S(2)}, u32[]{:S(2)}) async-start(bf16[8,192,512]{2,1,0:T(8,128)(2,1)} %collective-permute-done.9), calls=%async_computation.9 | async-start | bytes 3145728 | tf_op jit(solution)/shard_map/all_to_all | solution.py:918
  585.1 36.3 %copy-start.8 = (bf16[64,4096]{1,0:T(8,128)(2,1)S(1)}, bf16[64,4096]{1,0:T(8,128)(2,1)}, u32[]{:S(2)}) copy-start(bf16[64,4096]{1,0:T(8,128)(2,1)} %get-tuple-element.196) | copy-start | bytes 1572868
  585.1 36.3 %collective-permute-start.11 = (bf16[64,4096]{1,0:T(8,128)(2,1)}, bf16[64,4096]{1,0:T(8,128)(2,1)S(1)}, u32[]{:S(2)}, u32[]{:S(2)}) collective-permute-start(bf16[64,4096]{1,0:T(8,128)(2,1)} %get-tuple-element.245), channel_id=1, source_target_pairs={{0,2},{1,3},{2,0},{3,1},{4,6},{5,7},{6,4},{7,5},{8,10},{9,11},{10,... | collective-permute-start | bytes 1572872 | tf_op jit(solution)/shard_map/ppermute | solution.py:927
  622.2 67.3 %all-to-all-start.10 = ((bf16[8,192,512]{2,1,0:T(8,128)(2,1)}), bf16[8,192,512]{2,1,0:T(8,128)(2,1)S(1)}, u32[]{:S(2)}, u32[]{:S(2)}) async-start(bf16[8,192,512]{2,1,0:T(8,128)(2,1)} %get-tuple-element.200), calls=%async_computation.10 | async-start | bytes 3145728 | tf_op jit(solution)/shard_map/all_to_all | solution.py:918
  653.0 43.0 %copy-start.26 = (s32[32]{0:T(128)S(1)}, s32[32]{0:T(128)}, u32[]{:S(2)}) copy-start(s32[32]{0:T(128)} %constant.43.clone) | copy-start | bytes 388
  653.0 43.0 %copy-start.27 = (s32[32]{0:T(128)S(1)}, s32[32]{0:T(128)}, u32[]{:S(2)}) copy-start(s32[32]{0:T(128)} %constant.44.clone) | copy-start | bytes 388
  653.0 43.0 %copy-start.25 = (s32[32]{0:T(128)S(1)}, s32[32]{0:T(128)}, u32[]{:S(2)}) copy-start(s32[32]{0:T(128)} %broadcast_xor_fusion.2.table_ref) | copy-start | bytes 388
  653.0 43.6 %copy-start.15 = (f32[1,1024]{1,0:T(1,128)S(1)}, f32[1,1024]{1,0:T(1,128)}, u32[]{:S(2)}) copy-start(f32[1,1024]{1,0:T(1,128)} %get-tuple-element.151) | copy-start | bytes 12292
  653.0 43.6 %copy-start.16 = (f32[1,1024]{1,0:T(1,128)S(1)}, f32[1,1024]{1,0:T(1,128)}, u32[]{:S(2)}) copy-start(f32[1,1024]{1,0:T(1,128)} %get-tuple-element.160) | copy-start | bytes 12292
  653.0 43.6 %copy-start.17 = (f32[8,128]{1,0:T(8,128)S(1)}, f32[8,128]{1,0:T(8,128)}, u32[]{:S(2)}) copy-start(f32[8,128]{1,0:T(8,128)} %get-tuple-element.184) | copy-start | bytes 12292
  653.0 43.6 %copy-start.19 = (f32[8,128]{1,0:T(8,128)S(1)}, f32[8,128]{1,0:T(8,128)}, u32[]{:S(2)}) copy-start(f32[8,128]{1,0:T(8,128)} %get-tuple-element.195) | copy-start | bytes 12292
  653.0 46.6 %copy-start.18 = (f32[8,128]{1,0:T(8,128)S(1)}, f32[8,128]{1,0:T(8,128)}, u32[]{:S(2)}) copy-start(f32[8,128]{1,0:T(8,128)} %get-tuple-element.191) | copy-start | bytes 12292
  653.0 46.6 %copy-start.20 = (f32[8,128]{1,0:T(8,128)S(1)}, f32[8,128]{1,0:T(8,128)}, u32[]{:S(2)}) copy-start(f32[8,128]{1,0:T(8,128)} %get-tuple-element.201) | copy-start | bytes 12292
  653.0 3.8 collective-permute-start.12
  689.5 22.1 %copy-start.3 = (bf16[8,192,512]{2,1,0:T(8,128)(2,1)}, bf16[8,192,512]{2,1,0:T(8,128)(2,1)S(1)}, u32[]{:S(2)}) copy-start(bf16[8,192,512]{2,1,0:T(8,128)(2,1)S(1)} %all-to-all-done.10.rest_0_) | copy-start | bytes 4718596
  689.5 63.4 %all-to-all-start.11 = ((bf16[8,192,512]{2,1,0:T(8,128)(2,1)}), bf16[8,192,512]{2,1,0:T(8,128)(2,1)}, u32[]{:S(2)}, u32[]{:S(2)}) async-start(bf16[8,192,512]{2,1,0:T(8,128)(2,1)} %collective-permute-done.12), calls=%async_computation.11 | async-start | bytes 3145728 | tf_op jit(solution)/shard_map/all_to_all | solution.py:918
  696.6 129.7 %collective-permute-start.13 = (bf16[32,4096]{1,0:T(8,128)(2,1)}, bf16[32,4096]{1,0:T(8,128)(2,1)}, u32[]{:S(2)}, u32[]{:S(2)}) collective-permute-start(bf16[32,4096]{1,0:T(8,128)(2,1)} %get-tuple-element.247), channel_id=1, source_target_pairs={{0,4},{1,5},{2,6},{3,7},{4,0},{5,1},{6,2},{7,3},{8,12},{9,13},{10,... | collective-permute-start | bytes 786440 | tf_op jit(solution)/shard_map/ppermute | solution.py:927
  752.9 11.4 %copy-start.21 = (f32[1,1024]{1,0:T(1,128)S(1)}, f32[1,1024]{1,0:T(1,128)}, u32[]{:S(2)}) copy-start(f32[1,1024]{1,0:T(1,128)} %get-tuple-element.207) | copy-start | bytes 12292
  826.4 7.4 copy-start.1
  828.2 3.5 copy-start.14
  828.2 4.2 copy-start.13
  828.2 4.9 copy-start.12
  828.2 2.8 slice-start
Sparse Core Ops, SparseCore 0:
  10.2 49.0 all-gather.5
  60.8 22.5 all-gather.7
  85.0 58.2 all-gather.9
  144.8 58.2 all-gather.11
  204.5 58.2 all-gather.13
  437.5 311.4 reduce-scatter.1

commit v3 on v2

--- a/solution.py
+++ b/solution.py
@@ -13,7 +13,6 @@
 LOG2E = 1.4426950408889634
 LN2 = 0.6931471805599453
 CLASSES = 8
-AUX = 16
 COVER = 16
 EXTRA = 32
 MASKED = -1.5e9
@@ -162,7 +161,7 @@
     depth = head_dim + EXTRA
     whole = pl.BlockSpec((count, rows, width), lambda i, *_: (0, 0, 0))
     operands = [length, bias, x, ids]
-    in_specs = [whole, pl.BlockSpec((count, AUX, width), lambda i, *_: (0, 3 * head_dim // AUX, 0))]
+    in_specs = [whole, pl.BlockSpec((count, 1, width), lambda i, *_: (0, 0, 0))]
     aliases = {}
     if mixed is not None:
         operands.append(mixed)
@@ -314,7 +313,7 @@
             grid=(blocks,),
             in_specs=[
                 whole(x),
-                pl.BlockSpec((count, AUX, width), lambda i, *_: (0, 3 * head_dim // AUX, 0)),
+                pl.BlockSpec((count, 1, width), lambda i, *_: (0, 0, 0)),
                 head_spec, head_spec, whole(lse),
             ],
             out_specs=[
@@ -358,10 +357,30 @@
     return 1.0 / (1.0 + jnp.exp2(x * -LOG2E))
 
 
+def turn_kernel(*refs):
+    out_ref = refs[-1]
+    size = refs[0].shape[1]
+    for i, ref in enumerate(refs[:-1]):
+        out_ref[i * size : (i + 1) * size, :] = ref[...].T
+
+
+def turn_weights(*weights):
+    depth, size = weights[0].shape
+    vmem = pl.BlockSpec(memory_space=pltpu.VMEM)
+    return pl.pallas_call(
+        turn_kernel,
+        in_specs=[vmem] * len(weights),
+        out_specs=vmem,
+        out_shape=jax.ShapeDtypeStruct((len(weights) * size, depth), BF16),
+        compiler_params=pltpu.CompilerParams(vmem_limit_bytes=62 << 20),
+        name="turn_weights",
+    )(*weights)
+
+
 def project_kernel(
-    shape, core_ref, tokens_ref, gain_ref, query_ref, key_ref, value_ref, cos_ref, sin_ref, ids_ref, flat_ref, *rest
+    shape, core_ref, tokens_ref, gain_ref, query_ref, key_ref, value_ref, cos_ref, sin_ref, flat_ref, *rest
 ):
-    here, head_dim, extras, swap = shape
+    here, head_dim, swap = shape
     outs, flat_weights = rest[:-1], rest[-1]
     pair = pl.program_id(0)
 
@@ -371,10 +390,13 @@
         inverse = lax.rsqrt(jnp.mean(inputs * inputs, axis=-1, keepdims=True) + EPSILON)
         flat_ref[...] = (inputs * inverse * gain_ref[...]).astype(BF16).T
 
-    flat_weights[0:128, :] = query_ref[...].T
-    flat_weights[128:256, :] = key_ref[...].T
-    flat_weights[256:384, :] = value_ref[...].T
-    made = dot(flat_weights[...], flat_ref[...])
+    made = None
+    depth = query_ref.shape[2]
+    for shard in range(query_ref.shape[0]):
+        for at, ref in enumerate((query_ref, key_ref, value_ref)):
+            flat_weights[shard, at * 128 : (at + 1) * 128, :] = ref[shard]
+        term = dot(flat_weights[shard], flat_ref[shard * depth : (shard + 1) * depth, :])
+        made = term if made is None else made + term
     cosine, sine = cos_ref[...], sin_ref[...]
     half = head_dim // 2
 
@@ -390,8 +412,6 @@
         target[place, 0:head_dim, :] = turned(spot, LOG2E / math.sqrt(head_dim))
         target[place, head_dim : 2 * head_dim, :] = turned(128 + spot, 1.0)
         target[place, 2 * head_dim : 3 * head_dim, :] = made[256 + spot : 256 + spot + head_dim].astype(BF16)
-        if extras[slot]:
-            target[place, 3 * head_dim :, :] = jnp.broadcast_to(ids_ref[...], (AUX, ids_ref.shape[1])).astype(BF16)
 
     if swap:
         for core in range(2):
@@ -406,36 +426,38 @@
             put(at, at % here, 0 if here > 1 else at)
 
 
-def project(core, tokens, unit, gain, weights, cosine, sine, ids, count, here, head_dim, swap):
+def project(core, tokens, unit, gain, weights, cosine, sine, count, here, head_dim, swap):
     width, model = tokens.shape[2:]
     heads = count * here
     pairs = heads * head_dim // 128
     per = 128 // head_dim // here
-    extras = [h == (1 if swap else 0) for h in range(here)]
 
     def fixed(a):
         return pl.BlockSpec(a.shape, lambda p: (0,) * a.ndim)
 
-    weight_specs = [pl.BlockSpec((model, 128), lambda p, i=i: (0, i * pairs + p)) for i in range(3)]
+    shards, _, depth = weights.shape
+    weight_specs = [
+        pl.BlockSpec((shards, 128, depth), lambda p, i=i: (0, i * pairs + p, 0)) for i in range(3)
+    ]
     return pl.pallas_call(
-        functools.partial(project_kernel, (here, head_dim, extras, swap)),
+        functools.partial(project_kernel, (here, head_dim, swap)),
         grid=(pairs,),
         in_specs=[
             pl.BlockSpec(memory_space=pltpu.SMEM),
             pl.BlockSpec((1, 1, width, model), lambda p: unit + (0, 0)),
-            fixed(gain), *weight_specs, fixed(cosine), fixed(sine), fixed(ids),
+            fixed(gain), *weight_specs, fixed(cosine), fixed(sine),
         ],
         out_specs=[pl.BlockSpec((model, width), lambda p: (0, 0))]
-        + [pl.BlockSpec((per, 3 * head_dim + AUX * e, width), lambda p: (p, 0, 0)) for e in extras],
+        + [pl.BlockSpec((per, 3 * head_dim, width), lambda p: (p, 0, 0))] * here,
         out_shape=[jax.ShapeDtypeStruct((model, width), BF16)]
-        + [jax.ShapeDtypeStruct((count, 3 * head_dim + AUX * e, width), BF16) for e in extras],
-        scratch_shapes=[pltpu.VMEM((384, model), BF16)],
+        + [jax.ShapeDtypeStruct((count, 3 * head_dim, width), BF16)] * here,
+        scratch_shapes=[pltpu.VMEM((shards, 384, depth), BF16)],
         compiler_params=pltpu.CompilerParams(vmem_limit_bytes=62 << 20),
         cost_estimate=pl.CostEstimate(
             flops=6 * width * model * model // COVER, bytes_accessed=12 * model * model, transcendentals=0
         ),
         name="project",
-    )(core, tokens, gain, weights, weights, weights, cosine, sine, ids)
+    )(core, tokens, gain, weights, weights, weights, cosine, sine)
 
 
 def middle_kernel(
@@ -518,7 +540,7 @@
     width, model = tokens.shape[2:]
     out_w, gate_w, up_w, down_w = weights
     ffn = gate_w.shape[1]
-    block = 1024
+    block = 512
 
     def fixed(a):
         return pl.BlockSpec(a.shape, lambda f, *_: (0,) * a.ndim)
@@ -605,19 +627,16 @@
         grad_q_ref[place, :] = turned(part[at // here, 0:head_dim, :])
         grad_k_ref[place, :] = turned(part[at // here, head_dim : 2 * head_dim, :])
         grad_v_ref[place, :] = part[at // here, 2 * head_dim : 3 * head_dim, :]
-    made = (
-        contract(grad_q_ref[...].T, query_ref[...], 1, 1)
-        + contract(grad_k_ref[...].T, key_ref[...], 1, 1)
-        + contract(grad_v_ref[...].T, value_ref[...], 1, 1)
-    )
+    rows = [ref[...].T for ref in (grad_q_ref, grad_k_ref, grad_v_ref)]
 
     @pl.when(step == 0)
     def _():
-        total[...] = made
-
-    @pl.when(step > 0)
-    def _():
-        total[...] += made
+        total[...] = jnp.zeros_like(total)
+
+    depth = query_ref.shape[2]
+    for shard in range(query_ref.shape[0]):
+        made = dot(rows[0], query_ref[shard]) + dot(rows[1], key_ref[shard]) + dot(rows[2], value_ref[shard])
+        total[:, shard * depth : (shard + 1) * depth] += made
 
     @pl.when(step == pl.num_programs(0) - 1)
     def _():
@@ -639,7 +658,10 @@
         return pl.BlockSpec(a.shape, lambda c: (0,) * a.ndim)
 
     token_spec = pl.BlockSpec((1, 1, width, model), lambda c: unit + (0, 0))
-    weight_specs = [pl.BlockSpec((model, 256), lambda c, i=i: (0, i * steps + c)) for i in range(3)]
+    shards, _, depth = weights.shape
+    weight_specs = [
+        pl.BlockSpec((shards, 256, depth), lambda c, i=i: (0, i * steps + c, 0)) for i in range(3)
+    ]
     row_spec = pl.BlockSpec((256, width), lambda c: (c, 0))
     operands = [core, tokens, grad_res, gain, weights, weights, weights, cosine, sine, *back]
     in_specs = [
@@ -920,7 +942,8 @@
     def after(value, *before):
         return lax.optimization_barrier((value,) + before)[0]
 
-    attn_joined = gather(jnp.concatenate([w_query, w_key, w_value], axis=1))
+    attn_rows = turn_weights(w_query, w_key, w_value)
+    attn_joined = lax.all_gather(attn_rows, "shard", axis=0, tiled=False)
     ffn_weights = [gather(w_out), gather(w_gate), gather(w_up), gather(w_down)]
 
     def permute(value, mask):
@@ -930,14 +953,22 @@
         return permute(value, count)
 
     lengths_of = [lengths, cross(lengths)] if swap else [lengths] * here
+    ids_own = lax.all_gather(variates, "seq", axis=0, tiled=False)
+    ids_of = [ids_own, cross(ids_own)] if swap else [ids_own] * here
+    attn_joined = after(attn_joined, *ids_of)
+
+    def ids_rows(u, h):
+        m, s = units[u]
+        return ids_of[h][:, m, s].astype(F32)[:, None, :]
+
     packed_list, flats, tables = [], [], []
 
     def run_project(u, token):
         m, s = units[u]
         cosine, sine = rotary_tables(positions[m, s], head_dim // 2)
-        ids = after(variates[m, s].astype(F32)[None, :], *token)
         flat, *packed = project(
-            core, tokens, (m, s), attn_row, attn_joined, cosine, sine, ids, count, here, head_dim, swap
+            core, tokens, (m, s), after(attn_row, *token), attn_joined, cosine, sine, count, here, head_dim,
+            swap,
         )
         flats.append(flat)
         tables.append((cosine, sine))
@@ -961,9 +992,7 @@
         return after(lengths_of[h][m, s].reshape(1), *token)
 
     def inputs_of(u, h):
-        if not swap:
-            return sent[u, h], sent[u, 0]
-        return (sent[u, 0], sent[u, 1]) if h == 0 else (crossed[u], crossed[u])
+        return (crossed[u] if swap and h == 1 else sent[u, h]), ids_rows(u, h)
 
     def run_forward(u, h, token):
         made, sums[u, h] = attend_forward(
@@ -1197,6 +1226,7 @@
             advance(token)
         keep, came, _ = holder["streams"][0]
         up_own = wide_sum(after(keep, *token), came)
+        flats[0] = after(flats[0], up_own)
         owned, part = holder["owned"], ffn // fold
 
         def joined(start, size):

time: 849 us -> 843 us (level)
  waiting for transfers between devices: 304 us -> 229 us
  blocking collectives: 0 us -> 32.2 us
  Pallas kernels: 402 us -> 433 us
    all_gather x5 -> x4, waiting for transfers between devices: 45.5 us -> 0.01 us  [gather(): return lax.all_gather(weight, 'shard', axis=0, tiled=True)]
    all_to_all x12, waiting for transfers between devices: 210 us -> 167 us  [exchange(): lax.all_to_all(values, 'seq', split_axis=0, concat_axis=0, tiled=True)]
    all_gather x0 -> x1, blocking collectives: none -> 32.2 us  [on_device(): ids_own = lax.all_gather(variates, 'seq', axis=0, tiled=False)]
    pallas_call x4, Pallas kernels: 104 us -> 127 us  [attend_backward(): pl.pallas_call(functools.partial(backward_kernel, (local, head_dim, block...]
    all_gather x0 -> x1, waiting for transfers between devices: none -> 13.5 us  [on_device(): attn_joined = lax.all_gather(attn_rows, 'shard', axis=0, tiled=False)]
    pallas_call x4, Pallas kernels: 61.5 us -> 72 us  [attend_forward(): pl.pallas_call(functools.partial(forward_kernel, (local, head_dim, block,...]
    ppermute x14 -> x15, starting transfers between devices: 19.9 us -> 25.1 us  [permute(): lax.ppermute(value, ('shard', 'seq'), [(i, i ^ mask) for i in range(devic...]
    pallas_call x2 -> x3, Pallas kernels: 21.9 us -> 24.2 us  [the longest x2 21.2 us: project(): pl.pallas_call(functools.partial(project_kernel, (here, head_dim, swap)),...]
  transfers between devices with their start and end apart: 32 -> 33, of which waited for: 15 -> 14; matrix products, arithmetic and copies ran while one was open for 4% -> 4% of each run, Pallas kernels for 44% -> 48%
where the time goes in v3:
time: 843 us; the launch traced here: 833 us
  Pallas kernels  433 us (51%)
  waiting for transfers between devices  229 us (27%)
  starting transfers between devices  81.7 us (10%)
  blocking collectives  32.2 us (4%)
  other arithmetic  28.5 us (3%)
  between operations  15.1 us (2%)
  local copies, waits for them, and re-layouts  13.5 us (2%)
    all_to_all x12, waiting for transfers between devices, exchange(): lax.all_to_all(values, 'seq', split_axis=0, concat_axis=0, tiled=True)  167 us
    pallas_call x4, Pallas kernels, attend_backward(): pl.pallas_call(functools.partial(backward_kernel, (local, head_dim, block...  127 us
    pallas_call x2, Pallas kernels, middle_part(): pl.pallas_call(functools.partial(middle_kernel, (head_dim, output is not...  84.6 us
    pallas_call x4, Pallas kernels, attend_forward(): pl.pallas_call(functools.partial(forward_kernel, (local, head_dim, block,...  72 us
    all_to_all x12, starting transfers between devices, exchange(): lax.all_to_all(values, 'seq', split_axis=0, concat_axis=0, tiled=True)  56.2 us
    ppermute x15, waiting for transfers between devices, permute(): lax.ppermute(value, ('shard', 'seq'), [(i, i ^ mask) for i in range(devic...  46.3 us
    pallas_call x1, Pallas kernels, reduce_rows(): pl.pallas_call(functools.partial(reduce_kernel, orders, count), in_specs=...  43.4 us
    pallas_call x3, Pallas kernels, weight_grad(): pl.pallas_call(functools.partial(weights_kernel, units), grid=(steps,), i...  33.5 us
  transfers between devices with their start and end apart: 33, of which 14 were waited for; matrix products, arithmetic and copies ran while one was open for 4% of the time, Pallas kernels for 48%

profile of v3, /device:TPU:0, one launch (start us, length us, event | category | flops | bytes accessed | tf_op | source)
XLA Modules:
  0.0 833.1 jit_solution(7780062984291748984)
XLA Ops:
  7.2 3.0 turn_weights.1
  12.3 32.2 %all-gather.1 = s32[16,1,512]{2,1,0:T(1,128)S(1)} all-gather(s32[2,1,512]{2,1,0:T(1,128)S(1)} %copy-done.16), channel_id=3, replica_groups=mesh['shard'=4,'seq'=8] {'seq'}, dimensions={0}, use_global_device_ids=true | all-gather | bytes 36864 | tf_op jit(solution)/shard_map/all_gather | solution.py:956
  44.7 1.2 multiply_sine_fusion
  45.9 13.5 %all-gather.16.cloned.1.call-done = bf16[12288,256]{1,0:T(8,128)(2,1)} async-done(((bf16[3072,256]{1,0:T(8,128)(2,1)}), bf16[12288,256]{1,0:T(8,128)(2,1)}) %all-gather.16.cloned.1.call-update) | async-done | bytes 6291472 | tf_op jit(solution)/shard_map/all_gather | solution.py:946
  59.5 10.6 %project.2 = (bf16[1024,512]{1,0:T(8,128)(2,1)}, bf16[8,192,512]{2,1,0:T(8,128)(2,1)}, bf16[8,192,512]{2,1,0:T(8,128)(2,1)}) custom-call(s32[1]{0:T(128)} %bitcast.2.core_ref, bf16[2,1,512,1024]{3,2,1,0:T(8,128)(2,1)} %tokens_ref.11, f32[1,1024]{1,0:T(1,128)} %bitcast.65, bf16[4,3072,256]{2,1,0:T(8,128)(2,1)} %bitcast.44, bf16[4,3072,256]{2,1,0:T(8,128)(2,1)} %bitcast.45, ...), custom_call_target="tpu_custom_call" | custom-call | flops 201326592 | bytes 12582912 | tf_op jit(solution)/shard_map/project/pallas_call | solution.py:442
  70.1 5.5 all-to-all-start
  76.2 10.6 %project.3 = (bf16[1024,512]{1,0:T(8,128)(2,1)}, bf16[8,192,512]{2,1,0:T(8,128)(2,1)}, bf16[8,192,512]{2,1,0:T(8,128)(2,1)}) custom-call(s32[1]{0:T(128)} %bitcast.2.core_ref, bf16[2,1,512,1024]{3,2,1,0:T(8,128)(2,1)} %tokens_ref.11, f32[1,1024]{1,0:T(1,128)} %bitcast.66, bf16[4,3072,256]{2,1,0:T(8,128)(2,1)} %bitcast.47, bf16[4,3072,256]{2,1,0:T(8,128)(2,1)} %bitcast.48, ...), custom_call_target="tpu_custom_call" | custom-call | flops 201326592 | bytes 12582912 | tf_op jit(solution)/shard_map/project/pallas_call | solution.py:442
  86.7 26.2 %all-to-all-done = bf16[8,192,512]{2,1,0:T(8,128)(2,1)S(1)} async-done(((bf16[8,192,512]{2,1,0:T(8,128)(2,1)}), bf16[8,192,512]{2,1,0:T(8,128)(2,1)S(1)}, u32[]{:S(2)}, u32[]{:S(2)}) %all-to-all-start) | async-done | bytes 1572896 | tf_op jit(solution)/shard_map/all_to_all | solution.py:940
  114.1 3.6 all-to-all-start.1
  119.0 1.8 collective-permute-done.1
  122.1 27.4 %attend_forward.4 = (bf16[8,64,512]{2,1,0:T(8,128)(2,1)}, f32[8,1,512]{2,1,0:T(1,128)}) custom-call(s32[1]{0:T(128)} %bitcast.7.len_ref, f32[1,2]{1,0:T(1,128)} %copy.48.bias_ref, bf16[8,192,512]{2,1,0:T(8,128)(2,1)} %collective-permute-done.2.x_ref, f32[8,1,512]{2,1,0:T(1,128)} %get-tuple-element.269.ids_ref), custom_call_target="tpu_custom_call" | custom-call | flops 2147483648 | bytes 3145728 | tf_op jit(solution)/shard_map/attend_forward/pallas_call | solution.py:170
  149.5 5.5 all-to-all-done.1.x_ref
  155.0 4.3 all-to-all-start.2
  160.5 7.6 attend_forward.5
  168.1 27.8 %all-to-all-done.2 = bf16[8,192,512]{2,1,0:T(8,128)(2,1)} async-done(((bf16[8,192,512]{2,1,0:T(8,128)(2,1)}), bf16[8,192,512]{2,1,0:T(8,128)(2,1)}, u32[]{:S(2)}, u32[]{:S(2)}) %all-to-all-start.2) | async-done | bytes 1572896 | tf_op jit(solution)/shard_map/all_to_all | solution.py:940
  195.9 3.6 all-to-all-start.3
  200.1 3.5 collective-permute-done.5
  204.7 14.5 %attend_forward.6 = (bf16[8,64,512]{2,1,0:T(8,128)(2,1)}, f32[8,1,512]{2,1,0:T(1,128)}) custom-call(s32[1]{0:T(128)} %bitcast.11.len_ref, f32[1,2]{1,0:T(1,128)} %copy.48.bias_ref, bf16[8,192,512]{2,1,0:T(8,128)(2,1)} %collective-permute-done.3.x_ref, f32[8,1,512]{2,1,0:T(1,128)} %get-tuple-element.268.ids_ref), custom_call_target="tpu_custom_call" | custom-call | flops 2147483648 | bytes 3145728 | tf_op jit(solution)/shard_map/attend_forward/pallas_call | solution.py:170
  219.2 17.5 %all-to-all-done.3.x_ref = bf16[8,192,512]{2,1,0:T(8,128)(2,1)S(1)} async-done(((bf16[8,192,512]{2,1,0:T(8,128)(2,1)}), bf16[8,192,512]{2,1,0:T(8,128)(2,1)S(1)}, u32[]{:S(2)}, u32[]{:S(2)}) %all-to-all-start.3) | async-done | bytes 1572896 | tf_op jit(solution)/shard_map/all_to_all | solution.py:940
  237.9 3.9 all-to-all-start.4
  241.9 22.5 %attend_forward.7 = (bf16[8,64,512]{2,1,0:T(8,128)(2,1)}, f32[8,1,512]{2,1,0:T(1,128)}) custom-call(s32[1]{0:T(128)} %bitcast.len_ref, f32[1,2]{1,0:T(1,128)} %copy.48.bias_ref, bf16[8,192,512]{2,1,0:T(8,128)(2,1)} %copy-done.9, f32[8,1,512]{2,1,0:T(1,128)} %get-tuple-element.266.ids_ref), custom_call_target="tpu_custom_call" | custom-call | flops 2147483648 | bytes 3145728 | tf_op jit(solution)/shard_map/attend_forward/pallas_call | solution.py:170
  264.4 2.1 pad_maximum_fusion
  266.5 1.2 all-to-all-done.4
  268.7 4.8 all-to-all-start.5
  273.4 1.3 add_add_fusion.1.info_ref
  274.7 42.3 %middle_part.2 = (bf16[2,1,512,1024]{3,2,1,0:T(8,128)(2,1)}, bf16[1024,512]{1,0:T(8,128)(2,1)}, bf16[1024,512]{1,0:T(8,128)(2,1)}, bf16[4096,512]{1,0:T(8,128)(2...) custom-call(s32[3]{0:T(128)} %add_add_fusion.1.info_ref, ...), custom_call_target="tpu_custom_call" | custom-call | flops 1610612736 | bytes 33554432 | tf_op jit(solution)/shard_map/middle_part/pallas_call | solution.py:565
  317.1 6.5 all-to-all-start.6
  323.5 1.3 add_add_fusion.info_ref
  325.4 42.3 %middle_part.3 = (bf16[2,1,512,1024]{3,2,1,0:T(8,128)(2,1)}, bf16[1024,512]{1,0:T(8,128)(2,1)}, bf16[1024,512]{1,0:T(8,128)(2,1)}, bf16[4096,512]{1,0:T(8,128)(2...) custom-call(s32[3]{0:T(128)} %add_add_fusion.info_ref, ...), custom_call_target="tpu_custom_call", output_to_operand_aliasing={{0}: (9, {})} | custom-call | flops 1610612736 | bytes 33554432 | tf_op jit(solution)/shard_map/middle_part/pallas_call | solution.py:565
  367.7 13.8 %up_grad.1 = (bf16[512,4096]{1,0:T(8,128)(2,1)}, bf16[512,4096]{1,0:T(8,128)(2,1)}) custom-call(s32[32]{0:T(128)} %broadcast_xor_fusion.2.table_ref, bf16[1024,512]{1,0:T(8,128)(2,1)} %get-tuple-element.169.refs_0_, bf16[1024,512]{1,0:T(8,128)(2,1)} %get-tuple-element.170.refs_1_, bf16[512,4096]{1,0:T(8,128)(2,1)} %get-tuple-element.173.refs_2_, ...), custom_call_target="tpu_custom_call" | custom-call | flops 536870912 | bytes 16777216 | tf_op jit(solution)/shard_map/up_grad/pallas_call | solution.py:736
  381.5 6.0 all-to-all-start.7
  389.1 14.1 %down_grad.1.refs_4_ = bf16[32,4,32,2304]{3,2,1,0:T(8,128)(2,1)} custom-call(bf16[4096,512]{1,0:T(8,128)(2,1)} %get-tuple-element.179.refs_0_, bf16[4096,512]{1,0:T(8,128)(2,1)} %get-tuple-element.180.refs_1_, bf16[512,1024]{1,0:T(8,128)(2,1)} %get-tuple-element.183.refs_2_, bf16[512,1024]{1,0:T(8,128)(2,1)} %get-tuple-element.184.refs_3_), custom_call_target="tpu_custom_call" | custom-call | flops 536870912 | bytes 8388608 | tf_op jit(solution)/shard_map/down_grad/pallas_call | solution.py:790
  403.3 10.7 %all-to-all-done.7.grad_ref = bf16[8,128,512]{2,1,0:T(8,128)(2,1)S(1)} async-done(((bf16[8,128,512]{2,1,0:T(8,128)(2,1)}), bf16[8,128,512]{2,1,0:T(8,128)(2,1)S(1)}, u32[]{:S(2)}, u32[]{:S(2)}) %all-to-all-start.7) | async-done | bytes 1048608 | tf_op jit(solution)/shard_map/all_to_all | solution.py:940
  414.0 13.4 %gate_grad.1.refs_4_ = bf16[32,4,32,2304]{3,2,1,0:T(8,128)(2,1)} custom-call(bf16[1024,512]{1,0:T(8,128)(2,1)} %get-tuple-element.169.refs_0_, bf16[1024,512]{1,0:T(8,128)(2,1)} %get-tuple-element.170.refs_1_, bf16[512,4096]{1,0:T(8,128)(2,1)} %get-tuple-element.177.refs_2_, ...), custom_call_target="tpu_custom_call", output_to_operand_aliasing={{}: (4, {})} | custom-call | flops 536870912 | bytes 8388608 | tf_op jit(solution)/shard_map/gate_grad/pallas_call | solution.py:790
  427.4 6.0 out_grad.1
  433.4 5.5 add_convert_fusion
  439.0 9.6 %attend_backward.4 = (bf16[8,192,512]{2,1,0:T(8,128)(2,1)}, f32[8,128]{1,0:T(8,128)}) custom-call(s32[1]{0:T(128)} %bitcast.9.len_ref, f32[1,2]{1,0:T(1,128)} %copy.48.bias_ref, bf16[8,192,512]{2,1,0:T(8,128)(2,1)} %copy-done.10, f32[8,1,512]{2,1,0:T(1,128)} %get-tuple-element.267.ids_ref, bf16[8,128,512]{2,1,0:T(8,128)(2,1)} %all-to-all-done.6.grad_ref, ...), custom_call_target="tpu_custom_call" | custom-call | flops 5368709120 | bytes 4718592 | tf_op jit(solution)/shard_map/attend_backward/pallas_call | solution.py:309
  448.6 37.6 %collective-permute-done.8 = bf16[256,4096]{1,0:T(8,128)(2,1)} collective-permute-done((bf16[256,4096]{1,0:T(8,128)(2,1)}, bf16[256,4096]{1,0:T(8,128)(2,1)}, u32[]{:S(2)}, u32[]{:S(2)}) %collective-permute-start.8) | collective-permute-done | bytes 2097184 | tf_op jit(solution)/shard_map/ppermute | solution.py:950
  486.2 4.3 add_convert_fusion.2
  490.5 4.7 all-to-all-start.8
  495.2 3.6 collective-permute-start.9
  498.8 1.7 collective-permute-start.11
  500.5 51.4 %attend_backward.5 = (bf16[8,192,512]{2,1,0:T(8,128)(2,1)}, f32[8,128]{1,0:T(8,128)}) custom-call(s32[1]{0:T(128)} %bitcast.7.len_ref, f32[1,2]{1,0:T(1,128)} %copy.48.bias_ref, bf16[8,192,512]{2,1,0:T(8,128)(2,1)} %collective-permute-done.2.x_ref, f32[8,1,512]{2,1,0:T(1,128)} %get-tuple-element.269.ids_ref, ...), custom_call_target="tpu_custom_call" | custom-call | flops 5368709120 | bytes 4718592 | tf_op jit(solution)/shard_map/attend_backward/pallas_call | solution.py:309
  552.0 18.0 %all-to-all-done.8.rest_0_ = bf16[8,192,512]{2,1,0:T(8,128)(2,1)S(1)} async-done(((bf16[8,192,512]{2,1,0:T(8,128)(2,1)}), bf16[8,192,512]{2,1,0:T(8,128)(2,1)S(1)}, u32[]{:S(2)}, u32[]{:S(2)}) %all-to-all-start.8) | async-done | bytes 1572896 | tf_op jit(solution)/shard_map/all_to_all | solution.py:940
  569.9 3.3 add_convert_fusion.4
  573.2 4.3 all-to-all-start.9
  577.5 1.9 collective-permute-start.12
  579.4 41.4 %attend_backward.6 = (bf16[8,192,512]{2,1,0:T(8,128)(2,1)}, f32[8,128]{1,0:T(8,128)}) custom-call(s32[1]{0:T(128)} %bitcast.len_ref, f32[1,2]{1,0:T(1,128)} %copy.48.bias_ref, bf16[8,192,512]{2,1,0:T(8,128)(2,1)} %copy-done.9, f32[8,1,512]{2,1,0:T(1,128)} %get-tuple-element.266.ids_ref, bf16[8,128,512]{2,1,0:T(8,128)(2,1)} %copy-done.6, ...), custom_call_target="tpu_custom_call" | custom-call | flops 5368709120 | bytes 4718592 | tf_op jit(solution)/shard_map/attend_backward/pallas_call | solution.py:309
  621.7 4.5 all-to-all-start.10
  626.2 24.5 %attend_backward.7 = (bf16[8,192,512]{2,1,0:T(8,128)(2,1)}, f32[8,128]{1,0:T(8,128)}) custom-call(s32[1]{0:T(128)} %bitcast.11.len_ref, f32[1,2]{1,0:T(1,128)} %copy.48.bias_ref, bf16[8,192,512]{2,1,0:T(8,128)(2,1)} %collective-permute-done.3.x_ref, f32[8,1,512]{2,1,0:T(1,128)} %get-tuple-element.268.ids_ref, ...), custom_call_target="tpu_custom_call" | custom-call | flops 5368709120 | bytes 4718592 | tf_op jit(solution)/shard_map/attend_backward/pallas_call | solution.py:309
  650.7 13.4 %collective-permute-start.13 = (bf16[8,192,512]{2,1,0:T(8,128)(2,1)}, bf16[8,192,512]{2,1,0:T(8,128)(2,1)}, u32[]{:S(2)}, u32[]{:S(2)}) collective-permute-start(bf16[8,192,512]{2,1,0:T(8,128)(2,1)} %get-tuple-element.201), channel_id=1, source_target_pairs={{0,8},{1,9},{2,10},{3,11},{4,12},{5,13},{6,14},{7,15},{8,0},{9,1},... | collective-permute-start | bytes 4718600 | tf_op jit(solution)/shard_map/ppermute | solution.py:950
  664.2 3.4 collective-permute-done.13
  667.6 18.2 %all-to-all-done.10.rest_0_ = bf16[8,192,512]{2,1,0:T(8,128)(2,1)S(1)} async-done(((bf16[8,192,512]{2,1,0:T(8,128)(2,1)}), bf16[8,192,512]{2,1,0:T(8,128)(2,1)S(1)}, u32[]{:S(2)}, u32[]{:S(2)}) %all-to-all-start.10) | async-done | bytes 1572896 | tf_op jit(solution)/shard_map/all_to_all | solution.py:940
  685.7 4.6 all-to-all-start.11
  691.0 2.9 collective-permute-start.14
  694.1 11.4 %final_part.2 = (bf16[2,1,512,1024]{3,2,1,0:T(8,128)(2,1)}, bf16[1024,512]{1,0:T(8,128)(2,1)}, bf16[1024,512]{1,0:T(8,128)(2,1)}, bf16[1024,512]{1,0:T(8,128)(2,1)}, f32[1,1024]{1,0:T(1,128)}) custom-call(s32[1]{0:T(128)} %bitcast.2.core_ref, bf16[2,1,512,1024]{3,2,1,0:T(8,128)(2,1)} %tokens_ref.11, f32[512,1024]{1,0:T(8,128)} %get-tuple-element.206.grad_res_ref, ...), custom_call_target="tpu_custom_call" | custom-call | flops 201326592 | bytes 12582912 | tf_op jit(solution)/shard_map/final_part/pallas_call | solution.py:679
  705.5 41.5 %all-to-all-done.11.rest_1_ = bf16[8,192,512]{2,1,0:T(8,128)(2,1)} async-done(((bf16[8,192,512]{2,1,0:T(8,128)(2,1)}), bf16[8,192,512]{2,1,0:T(8,128)(2,1)}, u32[]{:S(2)}, u32[]{:S(2)}) %all-to-all-start.11) | async-done | bytes 1572896 | tf_op jit(solution)/shard_map/all_to_all | solution.py:940
  747.0 11.5 %final_part.3 = (bf16[2,1,512,1024]{3,2,1,0:T(8,128)(2,1)}, bf16[1024,512]{1,0:T(8,128)(2,1)}, bf16[1024,512]{1,0:T(8,128)(2,1)}, bf16[1024,512]{1,0:T(8,128)(2,1)}, f32[1,1024]{1,0:T(1,128)}) custom-call(s32[1]{0:T(128)} %bitcast.2.core_ref, bf16[2,1,512,1024]{3,2,1,0:T(8,128)(2,1)} %tokens_ref.11, ...), custom_call_target="tpu_custom_call", output_to_operand_aliasing={{0}: (11, {})} | custom-call | flops 201326592 | bytes 12582912 | tf_op jit(solution)/shard_map/final_part/pallas_call | solution.py:679
  759.2 1.8 convert_add_fusion
  761.0 11.9 %attn_grads.1 = (bf16[1024,1024]{1,0:T(8,128)(2,1)}, bf16[1024,1024]{1,0:T(8,128)(2,1)}, bf16[1024,1024]{1,0:T(8,128)(2,1)}) custom-call(s32[96]{0:T(128)} %pad_add_fusion.table_ref, bf16[1024,512]{1,0:T(8,128)(2,1)} %get-tuple-element.218.refs_0_, bf16[1024,512]{1,0:T(8,128)(2,1)} %get-tuple-element.130.refs_1_, ...), custom_call_target="tpu_custom_call" | custom-call | flops 402653184 | bytes 12582912 | tf_op jit(solution)/shard_map/attn_grads/pallas_call | solution.py:736
  773.5 43.4 %reduce_rows.1 = (f32[32,1024]{1,0:T(8,128)}, f32[32,1024]{1,0:T(8,128)}, f32[32,1024]{1,0:T(8,128)}, f32[24,128]{1,0:T(8,128)}) custom-call(bf16[1024,1024]{1,0:T(8,128)(2,1)} %get-tuple-element.225.refs_0_, bf16[1024,1024]{1,0:T(8,128)(2,1)} %get-tuple-element.226.refs_1_, bf16[1024,1024]{1,0:T(8,128)(2,1)} %get-tuple-element.227.refs_2_, ...), custom_call_target="tpu_custom_call" | custom-call | tf_op jit(solution)/shard_map/reduce_rows/pallas_call | solution.py:893
  816.9 1.4 slice.160
  819.0 1.3 slice_bitcast_fusion
  820.3 1.9 slice_convert_fusion
  (138 shorter events, 21.0 us)
Async XLA Ops:
  7.2 111.1 %copy-start = (f32[16,2]{0,1:T(2,128)S(1)}, f32[16,2]{0,1:T(2,128)}, u32[]{:S(2)}) copy-start(f32[16,2]{0,1:T(2,128)} %param.29) | copy-start | bytes 388
  7.2 52.3 %all-gather.16.cloned.1.call-start = ((), (), s32[]{:S(2)}) async-start(), calls=%async_computation.18 | async-start | bytes 7864320 | tf_op jit(solution)/shard_map/all_gather | solution.py:946
  10.2 264.5 %all-gather.8.cloned.1.call-start = ((), (), s32[]{:S(2)}) async-start(), calls=%async_computation.13 | async-start | bytes 2621440 | tf_op jit(solution)/shard_map/all_gather | solution.py:937
  11.0 1.3 copy-start.16
  11.0 33.7 %copy-start.24 = (s32[2,1,512]{2,1,0:T(1,128)S(1)}, s32[2,1,512]{2,1,0:T(1,128)}, u32[]{:S(2)}) copy-start(s32[2,1,512]{2,1,0:T(1,128)} %param.23) | copy-start | bytes 12292
  11.0 263.7 %all-gather.10.cloned.1.call-start = ((), (), s32[]{:S(2)}) async-start(), calls=%async_computation.14 | async-start | bytes 10485760 | tf_op jit(solution)/shard_map/all_gather | solution.py:937
  11.7 263.0 %all-gather.12.cloned.1.call-start = ((), (), s32[]{:S(2)}) async-start(), calls=%async_computation.15 | async-start | bytes 10485760 | tf_op jit(solution)/shard_map/all_gather | solution.py:937
  44.6 1.3 collective-permute-start
  70.1 42.9 %all-to-all-start = ((bf16[8,192,512]{2,1,0:T(8,128)(2,1)}), bf16[8,192,512]{2,1,0:T(8,128)(2,1)S(1)}, u32[]{:S(2)}, u32[]{:S(2)}) async-start(bf16[8,192,512]{2,1,0:T(8,128)(2,1)} %get-tuple-element.129), calls=%async_computation | async-start | bytes 3145728 | tf_op jit(solution)/shard_map/all_to_all | solution.py:940
  75.6 199.1 %all-gather.14.cloned.1.call-start = ((), (), s32[]{:S(2)}) async-start(), calls=%async_computation.16 | async-start | bytes 10485760 | tf_op jit(solution)/shard_map/all_gather | solution.py:937
  86.7 31.1 %copy-start.25 = (s32[2,1]{0,1:T(1,128)S(1)}, s32[2,1]{0,1:T(1,128)}, u32[]{:S(2)}) copy-start(s32[2,1]{0,1:T(1,128)} %param.21) | copy-start | bytes 28
  113.0 1.1 copy-start.11
  114.1 40.8 %all-to-all-start.1 = ((bf16[8,192,512]{2,1,0:T(8,128)(2,1)}), bf16[8,192,512]{2,1,0:T(8,128)(2,1)S(1)}, u32[]{:S(2)}, u32[]{:S(2)}) async-start(bf16[8,192,512]{2,1,0:T(8,128)(2,1)} %get-tuple-element.131), calls=%async_computation.1 | async-start | bytes 3145728 | tf_op jit(solution)/shard_map/all_to_all | solution.py:940
  117.8 4.4 collective-permute-start.2
  117.8 3.0 collective-permute-start.1
  155.0 5.6 copy-start.10
  155.0 40.9 %all-to-all-start.2 = ((bf16[8,192,512]{2,1,0:T(8,128)(2,1)}), bf16[8,192,512]{2,1,0:T(8,128)(2,1)}, u32[]{:S(2)}, u32[]{:S(2)}) async-start(bf16[8,192,512]{2,1,0:T(8,128)(2,1)} %get-tuple-element.135), calls=%async_computation.2 | async-start | bytes 3145728 | tf_op jit(solution)/shard_map/all_to_all | solution.py:940
  168.1 35.4 %copy-start.12 = (bf16[8,64,512]{2,1,0:T(8,128)(2,1)S(1)}, bf16[8,64,512]{2,1,0:T(8,128)(2,1)}, u32[]{:S(2)}) copy-start(bf16[8,64,512]{2,1,0:T(8,128)(2,1)} %get-tuple-element.147.mixed_ref) | copy-start | bytes 1572868
  195.9 40.8 %all-to-all-start.3 = ((bf16[8,192,512]{2,1,0:T(8,128)(2,1)}), bf16[8,192,512]{2,1,0:T(8,128)(2,1)S(1)}, u32[]{:S(2)}, u32[]{:S(2)}) async-start(bf16[8,192,512]{2,1,0:T(8,128)(2,1)} %get-tuple-element.139), calls=%async_computation.3 | async-start | bytes 3145728 | tf_op jit(solution)/shard_map/all_to_all | solution.py:940
  199.5 5.1 collective-permute-start.3
  199.6 4.0 collective-permute-start.5
  236.7 1.2 copy-start.9
  237.9 29.8 %all-to-all-start.4 = ((bf16[8,128,512]{2,1,0:T(8,128)(2,1)}), bf16[8,128,512]{2,1,0:T(8,128)(2,1)S(1)}, u32[]{:S(2)}, u32[]{:S(2)}) async-start(bf16[8,128,512]{2,1,0:T(8,128)(2,1)} %pad_maximum_fusion.1), calls=%async_computation.4 | async-start | bytes 2097152 | tf_op jit(solution)/shard_map/all_to_all | solution.py:940
  241.8 22.6 %collective-permute-start.4 = (bf16[8,64,512]{2,1,0:T(8,128)(2,1)}, bf16[8,64,512]{2,1,0:T(8,128)(2,1)S(1)}, u32[]{:S(2)}, u32[]{:S(2)}) collective-permute-start(bf16[8,64,512]{2,1,0:T(8,128)(2,1)} %get-tuple-element.146.mixed_ref), channel_id=1, source_target_pairs={{0,8},{1,9},{2,10},{3,11},{4,12},{5,13},{6,14},{7,15},{8,0},{9,1},... | collective-permute-start | bytes 1572872 | tf_op jit(solution)/shard_map/ppermute | solution.py:950
  267.7 1.0 copy-start.5
  268.7 48.4 %all-to-all-start.5 = ((bf16[8,128,512]{2,1,0:T(8,128)(2,1)}), bf16[8,128,512]{2,1,0:T(8,128)(2,1)S(1)}, u32[]{:S(2)}, u32[]{:S(2)}) async-start(bf16[8,128,512]{2,1,0:T(8,128)(2,1)} %pad_maximum_fusion), calls=%async_computation.5 | async-start | bytes 2097152 | tf_op jit(solution)/shard_map/all_to_all | solution.py:940
  317.0 7.8 copy-start.29
  317.0 8.4 %copy-start.4 = (bf16[8,128,512]{2,1,0:T(8,128)(2,1)}, bf16[8,128,512]{2,1,0:T(8,128)(2,1)S(1)}, u32[]{:S(2)}) copy-start(bf16[8,128,512]{2,1,0:T(8,128)(2,1)S(1)} %all-to-all-done.5) | copy-start | bytes 3145732
  317.1 50.7 %all-to-all-start.6 = ((bf16[8,128,512]{2,1,0:T(8,128)(2,1)}), bf16[8,128,512]{2,1,0:T(8,128)(2,1)}, u32[]{:S(2)}, u32[]{:S(2)}) async-start(bf16[8,128,512]{2,1,0:T(8,128)(2,1)} %bitcast.60), calls=%async_computation.6 | async-start | bytes 2097152 | tf_op jit(solution)/shard_map/all_to_all | solution.py:940
  381.5 32.4 %collective-permute-start.6 = (bf16[512,4096]{1,0:T(8,128)(2,1)}, bf16[512,4096]{1,0:T(8,128)(2,1)}, u32[]{:S(2)}, u32[]{:S(2)}) collective-permute-start(bf16[512,4096]{1,0:T(8,128)(2,1)} %get-tuple-element.175), channel_id=1, source_target_pairs={{0,8},{1,9},{2,10},{3,11},{4,12},{5,13},{6,14},{7,15},{8,0},{9,1},... | collective-permute-start | bytes 12582920 | tf_op jit(solution)/shard_map/ppermute | solution.py:950
  381.5 32.4 %all-to-all-start.7 = ((bf16[8,128,512]{2,1,0:T(8,128)(2,1)}), bf16[8,128,512]{2,1,0:T(8,128)(2,1)S(1)}, u32[]{:S(2)}, u32[]{:S(2)}) async-start(bf16[8,128,512]{2,1,0:T(8,128)(2,1)} %bitcast.61), calls=%async_computation.7 | async-start | bytes 2097152 | tf_op jit(solution)/shard_map/all_to_all | solution.py:940
  387.6 432.7 %reduce-scatter.2.cloned.1.call-start = ((), (), s32[]{:S(2)}) async-start(), calls=%async_computation.17 | async-start | bytes 19464192 | tf_op jit(solution)/shard_map/reduce_scatter | solution.py:1095
  388.9 14.4 %collective-permute-start.7 = (bf16[8,64,512]{2,1,0:T(8,128)(2,1)S(1)}, bf16[8,64,512]{2,1,0:T(8,128)(2,1)}, u32[]{:S(2)}, u32[]{:S(2)}) collective-permute-start(bf16[8,64,512]{2,1,0:T(8,128)(2,1)S(1)} %slice.137), channel_id=1, source_target_pairs={{0,8},{1,9},{2,10},{3,11},{4,12},{5,13},{6,14},{7,15},{8,0},{9,1},... | collective-permute-start | bytes 1572872 | tf_op jit(solution)/shard_map/ppermute | solution.py:950
  414.0 13.4 %copy-start.6 = (bf16[8,128,512]{2,1,0:T(8,128)(2,1)}, bf16[8,128,512]{2,1,0:T(8,128)(2,1)S(1)}, u32[]{:S(2)}) copy-start(bf16[8,128,512]{2,1,0:T(8,128)(2,1)S(1)} %all-to-all-done.7.grad_ref) | copy-start | bytes 3145732
  439.0 47.3 %collective-permute-start.8 = (bf16[256,4096]{1,0:T(8,128)(2,1)}, bf16[256,4096]{1,0:T(8,128)(2,1)}, u32[]{:S(2)}, u32[]{:S(2)}) collective-permute-start(bf16[256,4096]{1,0:T(8,128)(2,1)} %get-tuple-element.257), channel_id=1, source_target_pairs={{0,16},{1,17},{2,18},{3,19},{4,20},{5,21},{6,22},{7,23},{8,24},{9,... | collective-permute-start | bytes 6291464 | tf_op jit(solution)/shard_map/ppermute | solution.py:950
  490.5 4.7 copy-start.7
  490.5 79.4 %all-to-all-start.8 = ((bf16[8,192,512]{2,1,0:T(8,128)(2,1)}), bf16[8,192,512]{2,1,0:T(8,128)(2,1)S(1)}, u32[]{:S(2)}, u32[]{:S(2)}) async-start(bf16[8,192,512]{2,1,0:T(8,128)(2,1)} %get-tuple-element.193), calls=%async_computation.8 | async-start | bytes 3145728 | tf_op jit(solution)/shard_map/all_to_all | solution.py:940
  495.2 5.3 collective-permute-start.9
  498.8 71.1 %collective-permute-start.11 = (bf16[128,4096]{1,0:T(8,128)(2,1)}, bf16[128,4096]{1,0:T(8,128)(2,1)}, u32[]{:S(2)}, u32[]{:S(2)}) collective-permute-start(bf16[128,4096]{1,0:T(8,128)(2,1)} %get-tuple-element.259), channel_id=1, source_target_pairs={{0,1},{1,0},{2,3},{3,2},{4,5},{5,4},{6,7},{7,6},{8,9},{9,8},{10,11... | collective-permute-start | bytes 3145736 | tf_op jit(solution)/shard_map/ppermute | solution.py:950
  552.0 21.3 %collective-permute-start.10 = (bf16[8,192,512]{2,1,0:T(8,128)(2,1)}, bf16[8,192,512]{2,1,0:T(8,128)(2,1)}, u32[]{:S(2)}, u32[]{:S(2)}) collective-permute-start(bf16[8,192,512]{2,1,0:T(8,128)(2,1)} %get-tuple-element.191), channel_id=1, source_target_pairs={{0,8},{1,9},{2,10},{3,11},{4,12},{5,13},{6,14},{7,15},{8,0},{9,1},... | collective-permute-start | bytes 4718600 | tf_op jit(solution)/shard_map/ppermute | solution.py:950
  569.9 3.3 copy-start.2
  573.2 47.6 %all-to-all-start.9 = ((bf16[8,192,512]{2,1,0:T(8,128)(2,1)}), bf16[8,192,512]{2,1,0:T(8,128)(2,1)}, u32[]{:S(2)}, u32[]{:S(2)}) async-start(bf16[8,192,512]{2,1,0:T(8,128)(2,1)} %collective-permute-done.10), calls=%async_computation.9 | async-start | bytes 3145728 | tf_op jit(solution)/shard_map/all_to_all | solution.py:940
  577.5 43.3 %copy-start.8 = (bf16[64,4096]{1,0:T(8,128)(2,1)S(1)}, bf16[64,4096]{1,0:T(8,128)(2,1)}, u32[]{:S(2)}) copy-start(bf16[64,4096]{1,0:T(8,128)(2,1)} %get-tuple-element.199) | copy-start | bytes 1572868
  577.5 43.3 %collective-permute-start.12 = (bf16[64,4096]{1,0:T(8,128)(2,1)}, bf16[64,4096]{1,0:T(8,128)(2,1)S(1)}, u32[]{:S(2)}, u32[]{:S(2)}) collective-permute-start(bf16[64,4096]{1,0:T(8,128)(2,1)} %get-tuple-element.261), channel_id=1, source_target_pairs={{0,2},{1,3},{2,0},{3,1},{4,6},{5,7},{6,4},{7,5},{8,10},{9,11},{10,... | collective-permute-start | bytes 1572872 | tf_op jit(solution)/shard_map/ppermute | solution.py:950
  621.7 64.0 %all-to-all-start.10 = ((bf16[8,192,512]{2,1,0:T(8,128)(2,1)}), bf16[8,192,512]{2,1,0:T(8,128)(2,1)S(1)}, u32[]{:S(2)}, u32[]{:S(2)}) async-start(bf16[8,192,512]{2,1,0:T(8,128)(2,1)} %get-tuple-element.203), calls=%async_computation.10 | async-start | bytes 3145728 | tf_op jit(solution)/shard_map/all_to_all | solution.py:940
  650.7 39.6 %copy-start.27 = (s32[32]{0:T(128)S(1)}, s32[32]{0:T(128)}, u32[]{:S(2)}) copy-start(s32[32]{0:T(128)} %constant.43.clone) | copy-start | bytes 388
  650.7 39.6 %copy-start.28 = (s32[32]{0:T(128)S(1)}, s32[32]{0:T(128)}, u32[]{:S(2)}) copy-start(s32[32]{0:T(128)} %constant.44.clone) | copy-start | bytes 388
  650.7 39.7 %copy-start.26 = (s32[32]{0:T(128)S(1)}, s32[32]{0:T(128)}, u32[]{:S(2)}) copy-start(s32[32]{0:T(128)} %broadcast_xor_fusion.2.table_ref) | copy-start | bytes 388
  650.7 40.2 %copy-start.17 = (f32[1,1024]{1,0:T(1,128)S(1)}, f32[1,1024]{1,0:T(1,128)}, u32[]{:S(2)}) copy-start(f32[1,1024]{1,0:T(1,128)} %get-tuple-element.154) | copy-start | bytes 12292
  650.7 40.2 %copy-start.18 = (f32[1,1024]{1,0:T(1,128)S(1)}, f32[1,1024]{1,0:T(1,128)}, u32[]{:S(2)}) copy-start(f32[1,1024]{1,0:T(1,128)} %get-tuple-element.163) | copy-start | bytes 12292
  650.7 40.2 %copy-start.19 = (f32[8,128]{1,0:T(8,128)S(1)}, f32[8,128]{1,0:T(8,128)}, u32[]{:S(2)}) copy-start(f32[8,128]{1,0:T(8,128)} %get-tuple-element.187) | copy-start | bytes 12292
  650.7 40.2 %copy-start.21 = (f32[8,128]{1,0:T(8,128)S(1)}, f32[8,128]{1,0:T(8,128)}, u32[]{:S(2)}) copy-start(f32[8,128]{1,0:T(8,128)} %get-tuple-element.198) | copy-start | bytes 12292
  650.7 40.3 %copy-start.20 = (f32[8,128]{1,0:T(8,128)S(1)}, f32[8,128]{1,0:T(8,128)}, u32[]{:S(2)}) copy-start(f32[8,128]{1,0:T(8,128)} %get-tuple-element.194) | copy-start | bytes 12292
  650.7 40.3 %copy-start.22 = (f32[8,128]{1,0:T(8,128)S(1)}, f32[8,128]{1,0:T(8,128)}, u32[]{:S(2)}) copy-start(f32[8,128]{1,0:T(8,128)} %get-tuple-element.204) | copy-start | bytes 12292
  650.7 16.8 %collective-permute-start.13 = (bf16[8,192,512]{2,1,0:T(8,128)(2,1)}, bf16[8,192,512]{2,1,0:T(8,128)(2,1)}, u32[]{:S(2)}, u32[]{:S(2)}) collective-permute-start(bf16[8,192,512]{2,1,0:T(8,128)(2,1)} %get-tuple-element.201), channel_id=1, source_target_pairs={{0,8},{1,9},{2,10},{3,11},{4,12},{5,13},{6,14},{7,15},{8,0},{9,1},... | collective-permute-start | bytes 4718600 | tf_op jit(solution)/shard_map/ppermute | solution.py:950
  685.7 19.8 %copy-start.3 = (bf16[8,192,512]{2,1,0:T(8,128)(2,1)}, bf16[8,192,512]{2,1,0:T(8,128)(2,1)S(1)}, u32[]{:S(2)}) copy-start(bf16[8,192,512]{2,1,0:T(8,128)(2,1)S(1)} %all-to-all-done.10.rest_0_) | copy-start | bytes 4718596
  685.7 61.3 %all-to-all-start.11 = ((bf16[8,192,512]{2,1,0:T(8,128)(2,1)}), bf16[8,192,512]{2,1,0:T(8,128)(2,1)}, u32[]{:S(2)}, u32[]{:S(2)}) async-start(bf16[8,192,512]{2,1,0:T(8,128)(2,1)} %collective-permute-done.13), calls=%async_computation.11 | async-start | bytes 3145728 | tf_op jit(solution)/shard_map/all_to_all | solution.py:940
  691.0 68.1 %collective-permute-start.14 = (bf16[32,4096]{1,0:T(8,128)(2,1)}, bf16[32,4096]{1,0:T(8,128)(2,1)}, u32[]{:S(2)}, u32[]{:S(2)}) collective-permute-start(bf16[32,4096]{1,0:T(8,128)(2,1)} %get-tuple-element.263), channel_id=1, source_target_pairs={{0,4},{1,5},{2,6},{3,7},{4,0},{5,1},{6,2},{7,3},{8,12},{9,13},{10,... | collective-permute-start | bytes 786440 | tf_op jit(solution)/shard_map/ppermute | solution.py:950
  747.0 11.5 %copy-start.23 = (f32[1,1024]{1,0:T(1,128)S(1)}, f32[1,1024]{1,0:T(1,128)}, u32[]{:S(2)}) copy-start(f32[1,1024]{1,0:T(1,128)} %get-tuple-element.210) | copy-start | bytes 12292
  818.3 5.5 copy-start.15
  818.3 6.1 copy-start.14
  819.0 6.8 copy-start.1
  820.3 4.8 copy-start.13
  820.3 2.8 slice-start
Sparse Core Ops, SparseCore 0:
  10.3 49.0 all-gather.15
  61.0 22.5 all-gather.7
  85.2 58.2 all-gather.9
  145.0 58.9 all-gather.11
  205.4 58.3 all-gather.13
  433.6 307.8 reduce-scatter.1

commit v4 on v3

--- a/solution.py
+++ b/solution.py
@@ -1196,18 +1196,22 @@
 
     late = [task for task, _ in steps[-2:]]
     token = ()
-    for task, send in steps:
+    for index, (task, send) in enumerate(steps):
         done = ()
         moved = None
+        ahead = ()
         if "streams" in holder:
-            leaving = advance(token)
-            token = token if task in late else token + leaving
+            leaving = advance(token[-1:])
+            if index == len(steps) - 5:
+                ahead = leaving
+            elif task not in late:
+                token = token + leaving
         if send is not None:
             moved = exchange(after(send[0](), *token))
             done = (moved,)
         holder["flying"] = done
         if task is not None:
-            done = done + (task(token),)
+            done = done + (task(token + ahead),)
         if send is not None:
             send[1](after(moved, *done[1:]))
         token = done

time: 843 us -> 822 us (0.975)
  Pallas kernels: 433 us -> 393 us
  waiting for transfers between devices: 229 us -> 251 us
    pallas_call x4, Pallas kernels: 127 us -> 97.6 us  [attend_backward(): pl.pallas_call(functools.partial(backward_kernel, (local, head_dim, block...]
    ppermute x15, waiting for transfers between devices: 46.3 us -> 74.1 us  [permute(): lax.ppermute(value, ('shard', 'seq'), [(i, i ^ mask) for i in range(devic...]
    pallas_call x4, Pallas kernels: 72 us -> 57.8 us  [attend_forward(): pl.pallas_call(functools.partial(forward_kernel, (local, head_dim, block,...]
    ppermute x15, starting transfers between devices: 25.1 us -> 16.5 us  [permute(): lax.ppermute(value, ('shard', 'seq'), [(i, i ^ mask) for i in range(devic...]
  transfers between devices with their start and end apart: 33 -> 33, of which waited for: 14 -> 15; matrix products, arithmetic and copies ran while one was open for 4% -> 4% of each run, Pallas kernels for 48% -> 44%
where the time goes in v4:
time: 822 us; the launch traced here: 809 us
  Pallas kernels  393 us (48%)
  waiting for transfers between devices  251 us (31%)
  starting transfers between devices  73.5 us (9%)
  blocking collectives  32.2 us (4%)
  other arithmetic  28 us (3%)
  local copies, waits for them, and re-layouts  16.9 us (2%)
  between operations  15 us (2%)
    all_to_all x12, waiting for transfers between devices, exchange(): lax.all_to_all(values, 'seq', split_axis=0, concat_axis=0, tiled=True)  161 us
    pallas_call x4, Pallas kernels, attend_backward(): pl.pallas_call(functools.partial(backward_kernel, (local, head_dim, block...  97.6 us
    pallas_call x2, Pallas kernels, middle_part(): pl.pallas_call(functools.partial(middle_kernel, (head_dim, output is not...  84.6 us
    ppermute x15, waiting for transfers between devices, permute(): lax.ppermute(value, ('shard', 'seq'), [(i, i ^ mask) for i in range(devic...  74.1 us
    pallas_call x4, Pallas kernels, attend_forward(): pl.pallas_call(functools.partial(forward_kernel, (local, head_dim, block,...  57.8 us
    all_to_all x12, starting transfers between devices, exchange(): lax.all_to_all(values, 'seq', split_axis=0, concat_axis=0, tiled=True)  56.6 us
    pallas_call x1, Pallas kernels, reduce_rows(): pl.pallas_call(functools.partial(reduce_kernel, orders, count), in_specs=...  46 us
    pallas_call x3, Pallas kernels, weight_grad(): pl.pallas_call(functools.partial(weights_kernel, units), grid=(steps,), i...  33.7 us
  transfers between devices with their start and end apart: 33, of which 15 were waited for; matrix products, arithmetic and copies ran while one was open for 4% of the time, Pallas kernels for 44%

profile of v4, /device:TPU:0, one launch (start us, length us, event | category | flops | bytes accessed | tf_op | source)
XLA Modules:
  0.0 809.4 jit_solution(1132292325216334987)
XLA Ops:
  7.2 3.0 turn_weights.1
  12.3 32.2 %all-gather.1 = s32[16,1,512]{2,1,0:T(1,128)S(1)} all-gather(s32[2,1,512]{2,1,0:T(1,128)S(1)} %copy-done.17), channel_id=3, replica_groups=mesh['shard'=4,'seq'=8] {'seq'}, dimensions={0}, use_global_device_ids=true | all-gather | bytes 36864 | tf_op jit(solution)/shard_map/all_gather | solution.py:956
  45.9 13.5 %all-gather.16.cloned.1.call-done = bf16[12288,256]{1,0:T(8,128)(2,1)} async-done(((bf16[3072,256]{1,0:T(8,128)(2,1)}), bf16[12288,256]{1,0:T(8,128)(2,1)}) %all-gather.16.cloned.1.call-update) | async-done | bytes 6291472 | tf_op jit(solution)/shard_map/all_gather | solution.py:946
  59.5 10.6 %project.2 = (bf16[1024,512]{1,0:T(8,128)(2,1)}, bf16[8,192,512]{2,1,0:T(8,128)(2,1)}, bf16[8,192,512]{2,1,0:T(8,128)(2,1)}) custom-call(s32[1]{0:T(128)} %bitcast.2.core_ref, bf16[2,1,512,1024]{3,2,1,0:T(8,128)(2,1)} %tokens_ref.11, f32[1,1024]{1,0:T(1,128)} %bitcast.65, bf16[4,3072,256]{2,1,0:T(8,128)(2,1)} %bitcast.44, bf16[4,3072,256]{2,1,0:T(8,128)(2,1)} %bitcast.45, ...), custom_call_target="tpu_custom_call" | custom-call | flops 201326592 | bytes 12582912 | tf_op jit(solution)/shard_map/project/pallas_call | solution.py:442
  70.1 5.5 all-to-all-start
  76.2 10.6 %project.3 = (bf16[1024,512]{1,0:T(8,128)(2,1)}, bf16[8,192,512]{2,1,0:T(8,128)(2,1)}, bf16[8,192,512]{2,1,0:T(8,128)(2,1)}) custom-call(s32[1]{0:T(128)} %bitcast.2.core_ref, bf16[2,1,512,1024]{3,2,1,0:T(8,128)(2,1)} %tokens_ref.11, f32[1,1024]{1,0:T(1,128)} %bitcast.66, bf16[4,3072,256]{2,1,0:T(8,128)(2,1)} %bitcast.47, bf16[4,3072,256]{2,1,0:T(8,128)(2,1)} %bitcast.48, ...), custom_call_target="tpu_custom_call" | custom-call | flops 201326592 | bytes 12582912 | tf_op jit(solution)/shard_map/project/pallas_call | solution.py:442
  86.8 26.2 %all-to-all-done = bf16[8,192,512]{2,1,0:T(8,128)(2,1)S(1)} async-done(((bf16[8,192,512]{2,1,0:T(8,128)(2,1)}), bf16[8,192,512]{2,1,0:T(8,128)(2,1)S(1)}, u32[]{:S(2)}, u32[]{:S(2)}) %all-to-all-start) | async-done | bytes 1572896 | tf_op jit(solution)/shard_map/all_to_all | solution.py:940
  114.2 3.6 all-to-all-start.1
  119.1 1.8 collective-permute-done.1
  122.1 9.1 %attend_forward.4 = (bf16[8,64,512]{2,1,0:T(8,128)(2,1)}, f32[8,1,512]{2,1,0:T(1,128)}) custom-call(s32[1]{0:T(128)} %bitcast.7.len_ref, f32[1,2]{1,0:T(1,128)} %copy.48.bias_ref, bf16[8,192,512]{2,1,0:T(8,128)(2,1)} %collective-permute-done.2.x_ref, f32[8,1,512]{2,1,0:T(1,128)} %get-tuple-element.268.ids_ref), custom_call_target="tpu_custom_call" | custom-call | flops 2147483648 | bytes 3145728 | tf_op jit(solution)/shard_map/attend_forward/pallas_call | solution.py:170
  131.2 23.8 %all-to-all-done.1.x_ref = bf16[8,192,512]{2,1,0:T(8,128)(2,1)S(1)} async-done(((bf16[8,192,512]{2,1,0:T(8,128)(2,1)}), bf16[8,192,512]{2,1,0:T(8,128)(2,1)S(1)}, u32[]{:S(2)}, u32[]{:S(2)}) %all-to-all-start.1) | async-done | bytes 1572896 | tf_op jit(solution)/shard_map/all_to_all | solution.py:940
  155.0 4.3 all-to-all-start.2
  160.6 11.5 %attend_forward.5 = (bf16[8,64,512]{2,1,0:T(8,128)(2,1)}, f32[8,1,512]{2,1,0:T(1,128)}) custom-call(s32[1]{0:T(128)} %bitcast.9.len_ref, f32[1,2]{1,0:T(1,128)} %copy.48.bias_ref, bf16[8,192,512]{2,1,0:T(8,128)(2,1)} %copy-done.9, f32[8,1,512]{2,1,0:T(1,128)} %get-tuple-element.266.ids_ref), custom_call_target="tpu_custom_call" | custom-call | flops 2147483648 | bytes 3145728 | tf_op jit(solution)/shard_map/attend_forward/pallas_call | solution.py:170
  172.2 23.8 %all-to-all-done.2 = bf16[8,192,512]{2,1,0:T(8,128)(2,1)} async-done(((bf16[8,192,512]{2,1,0:T(8,128)(2,1)}), bf16[8,192,512]{2,1,0:T(8,128)(2,1)}, u32[]{:S(2)}, u32[]{:S(2)}) %all-to-all-start.2) | async-done | bytes 1572896 | tf_op jit(solution)/shard_map/all_to_all | solution.py:940
  195.9 3.6 all-to-all-start.3
  200.1 3.5 collective-permute-done.5
  204.7 22.5 %attend_forward.6 = (bf16[8,64,512]{2,1,0:T(8,128)(2,1)}, f32[8,1,512]{2,1,0:T(1,128)}) custom-call(s32[1]{0:T(128)} %bitcast.11.len_ref, f32[1,2]{1,0:T(1,128)} %copy.48.bias_ref, bf16[8,192,512]{2,1,0:T(8,128)(2,1)} %collective-permute-done.3.x_ref, f32[8,1,512]{2,1,0:T(1,128)} %get-tuple-element.267.ids_ref), custom_call_target="tpu_custom_call" | custom-call | flops 2147483648 | bytes 3145728 | tf_op jit(solution)/shard_map/attend_forward/pallas_call | solution.py:170
  227.2 9.5 %all-to-all-done.3.x_ref = bf16[8,192,512]{2,1,0:T(8,128)(2,1)S(1)} async-done(((bf16[8,192,512]{2,1,0:T(8,128)(2,1)}), bf16[8,192,512]{2,1,0:T(8,128)(2,1)S(1)}, u32[]{:S(2)}, u32[]{:S(2)}) %all-to-all-start.3) | async-done | bytes 1572896 | tf_op jit(solution)/shard_map/all_to_all | solution.py:940
  237.9 3.9 all-to-all-start.4
  241.9 14.6 %attend_forward.7 = (bf16[8,64,512]{2,1,0:T(8,128)(2,1)}, f32[8,1,512]{2,1,0:T(1,128)}) custom-call(s32[1]{0:T(128)} %bitcast.len_ref, f32[1,2]{1,0:T(1,128)} %copy.48.bias_ref, bf16[8,192,512]{2,1,0:T(8,128)(2,1)} %copy-done.8, f32[8,1,512]{2,1,0:T(1,128)} %get-tuple-element.265.ids_ref), custom_call_target="tpu_custom_call" | custom-call | flops 2147483648 | bytes 3145728 | tf_op jit(solution)/shard_map/attend_forward/pallas_call | solution.py:170
  256.5 2.1 pad_maximum_fusion
  258.6 9.1 %all-to-all-done.4 = bf16[8,128,512]{2,1,0:T(8,128)(2,1)S(1)} async-done(((bf16[8,128,512]{2,1,0:T(8,128)(2,1)}), bf16[8,128,512]{2,1,0:T(8,128)(2,1)S(1)}, u32[]{:S(2)}, u32[]{:S(2)}) %all-to-all-start.4) | async-done | bytes 1048608 | tf_op jit(solution)/shard_map/all_to_all | solution.py:940
  268.7 3.6 all-to-all-start.5
  273.6 42.3 %middle_part.2 = (bf16[2,1,512,1024]{3,2,1,0:T(8,128)(2,1)}, bf16[1024,512]{1,0:T(8,128)(2,1)}, bf16[1024,512]{1,0:T(8,128)(2,1)}, bf16[4096,512]{1,0:T(8,128)(2...) custom-call(s32[3]{0:T(128)} %add_add_fusion.1.info_ref, ...), custom_call_target="tpu_custom_call" | custom-call | flops 1610612736 | bytes 33554432 | tf_op jit(solution)/shard_map/middle_part/pallas_call | solution.py:565
  315.9 6.5 all-to-all-start.6
  322.4 1.3 add_add_fusion.info_ref
  324.3 42.3 %middle_part.3 = (bf16[2,1,512,1024]{3,2,1,0:T(8,128)(2,1)}, bf16[1024,512]{1,0:T(8,128)(2,1)}, bf16[1024,512]{1,0:T(8,128)(2,1)}, bf16[4096,512]{1,0:T(8,128)(2...) custom-call(s32[3]{0:T(128)} %add_add_fusion.info_ref, ...), custom_call_target="tpu_custom_call", output_to_operand_aliasing={{0}: (9, {})} | custom-call | flops 1610612736 | bytes 33554432 | tf_op jit(solution)/shard_map/middle_part/pallas_call | solution.py:565
  366.6 13.7 %up_grad.1 = (bf16[512,4096]{1,0:T(8,128)(2,1)}, bf16[512,4096]{1,0:T(8,128)(2,1)}) custom-call(s32[32]{0:T(128)} %broadcast_xor_fusion.2.table_ref, bf16[1024,512]{1,0:T(8,128)(2,1)} %get-tuple-element.169.refs_0_, bf16[1024,512]{1,0:T(8,128)(2,1)} %get-tuple-element.170.refs_1_, bf16[512,4096]{1,0:T(8,128)(2,1)} %get-tuple-element.173.refs_2_, ...), custom_call_target="tpu_custom_call" | custom-call | flops 536870912 | bytes 16777216 | tf_op jit(solution)/shard_map/up_grad/pallas_call | solution.py:736
  381.2 5.7 all-to-all-start.7
  388.3 14.1 %down_grad.1.refs_4_ = bf16[32,4,32,2304]{3,2,1,0:T(8,128)(2,1)} custom-call(bf16[4096,512]{1,0:T(8,128)(2,1)} %get-tuple-element.179.refs_0_, bf16[4096,512]{1,0:T(8,128)(2,1)} %get-tuple-element.180.refs_1_, bf16[512,1024]{1,0:T(8,128)(2,1)} %get-tuple-element.183.refs_2_, bf16[512,1024]{1,0:T(8,128)(2,1)} %get-tuple-element.184.refs_3_), custom_call_target="tpu_custom_call" | custom-call | flops 536870912 | bytes 8388608 | tf_op jit(solution)/shard_map/down_grad/pallas_call | solution.py:790
  402.4 10.4 %all-to-all-done.7.grad_ref = bf16[8,128,512]{2,1,0:T(8,128)(2,1)S(1)} async-done(((bf16[8,128,512]{2,1,0:T(8,128)(2,1)}), bf16[8,128,512]{2,1,0:T(8,128)(2,1)S(1)}, u32[]{:S(2)}, u32[]{:S(2)}) %all-to-all-start.7) | async-done | bytes 1048608 | tf_op jit(solution)/shard_map/all_to_all | solution.py:940
  412.8 13.5 %gate_grad.1.refs_4_ = bf16[32,4,32,2304]{3,2,1,0:T(8,128)(2,1)} custom-call(bf16[1024,512]{1,0:T(8,128)(2,1)} %get-tuple-element.169.refs_0_, bf16[1024,512]{1,0:T(8,128)(2,1)} %get-tuple-element.170.refs_1_, bf16[512,4096]{1,0:T(8,128)(2,1)} %get-tuple-element.177.refs_2_, ...), custom_call_target="tpu_custom_call", output_to_operand_aliasing={{}: (4, {})} | custom-call | flops 536870912 | bytes 8388608 | tf_op jit(solution)/shard_map/gate_grad/pallas_call | solution.py:790
  426.3 6.0 out_grad.1
  432.4 5.5 add_convert_fusion
  437.9 5.4 collective-permute-start.8
  444.2 18.1 %attend_backward.4 = (bf16[8,192,512]{2,1,0:T(8,128)(2,1)}, f32[8,128]{1,0:T(8,128)}) custom-call(s32[1]{0:T(128)} %bitcast.9.len_ref, f32[1,2]{1,0:T(1,128)} %copy.48.bias_ref, bf16[8,192,512]{2,1,0:T(8,128)(2,1)} %copy-done.9, f32[8,1,512]{2,1,0:T(1,128)} %get-tuple-element.266.ids_ref, bf16[8,128,512]{2,1,0:T(8,128)(2,1)} %all-to-all-done.6.grad_ref, ...), custom_call_target="tpu_custom_call" | custom-call | flops 5368709120 | bytes 4718592 | tf_op jit(solution)/shard_map/attend_backward/pallas_call | solution.py:309
  462.2 4.8 all-to-all-start.8
  467.0 21.2 %collective-permute-done.8 = bf16[256,4096]{1,0:T(8,128)(2,1)} collective-permute-done((bf16[256,4096]{1,0:T(8,128)(2,1)}, bf16[256,4096]{1,0:T(8,128)(2,1)}, u32[]{:S(2)}, u32[]{:S(2)}) %collective-permute-start.8) | collective-permute-done | bytes 2097184 | tf_op jit(solution)/shard_map/ppermute | solution.py:950
  488.3 3.3 add_convert_fusion.2
  491.6 1.6 collective-permute-start.11
  493.2 13.7 %attend_backward.5 = (bf16[8,192,512]{2,1,0:T(8,128)(2,1)}, f32[8,128]{1,0:T(8,128)}) custom-call(s32[1]{0:T(128)} %bitcast.7.len_ref, f32[1,2]{1,0:T(1,128)} %copy.48.bias_ref, bf16[8,192,512]{2,1,0:T(8,128)(2,1)} %collective-permute-done.2.x_ref, f32[8,1,512]{2,1,0:T(1,128)} %get-tuple-element.268.ids_ref, ...), custom_call_target="tpu_custom_call" | custom-call | flops 5368709120 | bytes 4718592 | tf_op jit(solution)/shard_map/attend_backward/pallas_call | solution.py:309
  506.9 2.3 collective-permute-start.10
  509.3 17.9 %collective-permute-done.11 = bf16[128,4096]{1,0:T(8,128)(2,1)} collective-permute-done((bf16[128,4096]{1,0:T(8,128)(2,1)}, bf16[128,4096]{1,0:T(8,128)(2,1)}, u32[]{:S(2)}, u32[]{:S(2)}) %collective-permute-start.11) | collective-permute-done | bytes 1048608 | tf_op jit(solution)/shard_map/ppermute | solution.py:950
  527.2 2.6 add_convert_fusion.4
  531.0 7.1 all-to-all-start.9
  538.0 2.0 collective-permute-start.12
  540.1 24.6 %attend_backward.6 = (bf16[8,192,512]{2,1,0:T(8,128)(2,1)}, f32[8,128]{1,0:T(8,128)}) custom-call(s32[1]{0:T(128)} %bitcast.len_ref, f32[1,2]{1,0:T(1,128)} %copy.48.bias_ref, bf16[8,192,512]{2,1,0:T(8,128)(2,1)} %copy-done.8, f32[8,1,512]{2,1,0:T(1,128)} %get-tuple-element.265.ids_ref, bf16[8,128,512]{2,1,0:T(8,128)(2,1)} %copy-done.7, ...), custom_call_target="tpu_custom_call" | custom-call | flops 5368709120 | bytes 4718592 | tf_op jit(solution)/shard_map/attend_backward/pallas_call | solution.py:309
  564.6 26.1 %collective-permute-done.12 = bf16[64,4096]{1,0:T(8,128)(2,1)} collective-permute-done((bf16[64,4096]{1,0:T(8,128)(2,1)}, bf16[64,4096]{1,0:T(8,128)(2,1)}, u32[]{:S(2)}, u32[]{:S(2)}) %collective-permute-start.12) | collective-permute-done | bytes 524320 | tf_op jit(solution)/shard_map/ppermute | solution.py:950
  590.7 2.0 add_convert_fusion.6
  592.8 4.3 all-to-all-start.10
  597.1 41.3 %attend_backward.7 = (bf16[8,192,512]{2,1,0:T(8,128)(2,1)}, f32[8,128]{1,0:T(8,128)}) custom-call(s32[1]{0:T(128)} %bitcast.11.len_ref, f32[1,2]{1,0:T(1,128)} %copy.48.bias_ref, bf16[8,192,512]{2,1,0:T(8,128)(2,1)} %collective-permute-done.3.x_ref, f32[8,1,512]{2,1,0:T(1,128)} %get-tuple-element.267.ids_ref, ...), custom_call_target="tpu_custom_call" | custom-call | flops 5368709120 | bytes 4718592 | tf_op jit(solution)/shard_map/attend_backward/pallas_call | solution.py:309
  638.5 3.6 collective-permute-done.13
  642.1 17.1 %all-to-all-done.10.rest_0_ = bf16[8,192,512]{2,1,0:T(8,128)(2,1)} async-done(((bf16[8,192,512]{2,1,0:T(8,128)(2,1)}), bf16[8,192,512]{2,1,0:T(8,128)(2,1)}, u32[]{:S(2)}, u32[]{:S(2)}) %all-to-all-start.10) | async-done | bytes 1572896 | tf_op jit(solution)/shard_map/all_to_all | solution.py:940
  659.3 3.6 all-to-all-start.11
  663.6 3.0 collective-permute-start.14
  667.0 11.9 %final_part.2 = (bf16[2,1,512,1024]{3,2,1,0:T(8,128)(2,1)}, bf16[1024,512]{1,0:T(8,128)(2,1)}, bf16[1024,512]{1,0:T(8,128)(2,1)}, bf16[1024,512]{1,0:T(8,128)(2,1)}, f32[1,1024]{1,0:T(1,128)}) custom-call(s32[1]{0:T(128)} %bitcast.2.core_ref, bf16[2,1,512,1024]{3,2,1,0:T(8,128)(2,1)} %tokens_ref.11, f32[512,1024]{1,0:T(8,128)} %get-tuple-element.205.grad_res_ref, ...), custom_call_target="tpu_custom_call" | custom-call | flops 201326592 | bytes 12582912 | tf_op jit(solution)/shard_map/final_part/pallas_call | solution.py:679
  678.8 40.7 %all-to-all-done.11.rest_1_ = bf16[8,192,512]{2,1,0:T(8,128)(2,1)S(1)} async-done(((bf16[8,192,512]{2,1,0:T(8,128)(2,1)}), bf16[8,192,512]{2,1,0:T(8,128)(2,1)S(1)}, u32[]{:S(2)}, u32[]{:S(2)}) %all-to-all-start.11) | async-done | bytes 1572896 | tf_op jit(solution)/shard_map/all_to_all | solution.py:940
  720.7 11.5 %final_part.3 = (bf16[2,1,512,1024]{3,2,1,0:T(8,128)(2,1)}, bf16[1024,512]{1,0:T(8,128)(2,1)}, bf16[1024,512]{1,0:T(8,128)(2,1)}, bf16[1024,512]{1,0:T(8,128)(2,1)}, f32[1,1024]{1,0:T(1,128)}) custom-call(s32[1]{0:T(128)} %bitcast.2.core_ref, bf16[2,1,512,1024]{3,2,1,0:T(8,128)(2,1)} %tokens_ref.11, ...), custom_call_target="tpu_custom_call", output_to_operand_aliasing={{0}: (11, {})} | custom-call | flops 201326592 | bytes 12582912 | tf_op jit(solution)/shard_map/final_part/pallas_call | solution.py:679
  732.9 1.8 convert_add_fusion
  734.7 11.9 %attn_grads.1 = (bf16[1024,1024]{1,0:T(8,128)(2,1)}, bf16[1024,1024]{1,0:T(8,128)(2,1)}, bf16[1024,1024]{1,0:T(8,128)(2,1)}) custom-call(s32[96]{0:T(128)} %pad_add_fusion.table_ref, bf16[1024,512]{1,0:T(8,128)(2,1)} %get-tuple-element.217.refs_0_, bf16[1024,512]{1,0:T(8,128)(2,1)} %get-tuple-element.130.refs_1_, ...), custom_call_target="tpu_custom_call" | custom-call | flops 402653184 | bytes 12582912 | tf_op jit(solution)/shard_map/attn_grads/pallas_call | solution.py:736
  747.2 46.0 %reduce_rows.1 = (f32[32,1024]{1,0:T(8,128)}, f32[32,1024]{1,0:T(8,128)}, f32[32,1024]{1,0:T(8,128)}, f32[24,128]{1,0:T(8,128)}) custom-call(bf16[1024,1024]{1,0:T(8,128)(2,1)} %get-tuple-element.224.refs_0_, bf16[1024,1024]{1,0:T(8,128)(2,1)} %get-tuple-element.225.refs_1_, bf16[1024,1024]{1,0:T(8,128)(2,1)} %get-tuple-element.226.refs_2_, ...), custom_call_target="tpu_custom_call" | custom-call | tf_op jit(solution)/shard_map/reduce_rows/pallas_call | solution.py:893
  793.2 1.4 slice.160
  795.3 1.3 slice_bitcast_fusion
  796.6 1.9 slice_convert_fusion
  (140 shorter events, 26.7 us)
Async XLA Ops:
  7.2 111.2 %copy-start = (f32[16,2]{0,1:T(2,128)S(1)}, f32[16,2]{0,1:T(2,128)}, u32[]{:S(2)}) copy-start(f32[16,2]{0,1:T(2,128)} %param.29) | copy-start | bytes 388
  7.2 52.3 %all-gather.16.cloned.1.call-start = ((), (), s32[]{:S(2)}) async-start(), calls=%async_computation.18 | async-start | bytes 7864320 | tf_op jit(solution)/shard_map/all_gather | solution.py:946
  10.2 263.4 %all-gather.8.cloned.1.call-start = ((), (), s32[]{:S(2)}) async-start(), calls=%async_computation.13 | async-start | bytes 2621440 | tf_op jit(solution)/shard_map/all_gather | solution.py:937
  11.0 1.3 copy-start.17
  11.0 33.7 %copy-start.25 = (s32[2,1,512]{2,1,0:T(1,128)S(1)}, s32[2,1,512]{2,1,0:T(1,128)}, u32[]{:S(2)}) copy-start(s32[2,1,512]{2,1,0:T(1,128)} %param.23) | copy-start | bytes 12292
  11.0 262.6 %all-gather.10.cloned.1.call-start = ((), (), s32[]{:S(2)}) async-start(), calls=%async_computation.14 | async-start | bytes 10485760 | tf_op jit(solution)/shard_map/all_gather | solution.py:937
  11.7 261.8 %all-gather.12.cloned.1.call-start = ((), (), s32[]{:S(2)}) async-start(), calls=%async_computation.15 | async-start | bytes 10485760 | tf_op jit(solution)/shard_map/all_gather | solution.py:937
  44.6 1.3 collective-permute-start
  70.1 42.9 %all-to-all-start = ((bf16[8,192,512]{2,1,0:T(8,128)(2,1)}), bf16[8,192,512]{2,1,0:T(8,128)(2,1)S(1)}, u32[]{:S(2)}, u32[]{:S(2)}) async-start(bf16[8,192,512]{2,1,0:T(8,128)(2,1)} %get-tuple-element.129), calls=%async_computation | async-start | bytes 3145728 | tf_op jit(solution)/shard_map/all_to_all | solution.py:940
  75.6 198.0 %all-gather.14.cloned.1.call-start = ((), (), s32[]{:S(2)}) async-start(), calls=%async_computation.16 | async-start | bytes 10485760 | tf_op jit(solution)/shard_map/all_gather | solution.py:937
  86.8 31.1 %copy-start.26 = (s32[2,1]{0,1:T(1,128)S(1)}, s32[2,1]{0,1:T(1,128)}, u32[]{:S(2)}) copy-start(s32[2,1]{0,1:T(1,128)} %param.21) | copy-start | bytes 28
  113.0 1.2 copy-start.10
  114.2 40.8 %all-to-all-start.1 = ((bf16[8,192,512]{2,1,0:T(8,128)(2,1)}), bf16[8,192,512]{2,1,0:T(8,128)(2,1)S(1)}, u32[]{:S(2)}, u32[]{:S(2)}) async-start(bf16[8,192,512]{2,1,0:T(8,128)(2,1)} %get-tuple-element.131), calls=%async_computation.1 | async-start | bytes 3145728 | tf_op jit(solution)/shard_map/all_to_all | solution.py:940
  117.8 4.3 collective-permute-start.2
  117.9 3.0 collective-permute-start.1
  155.0 5.7 copy-start.9
  155.0 40.9 %all-to-all-start.2 = ((bf16[8,192,512]{2,1,0:T(8,128)(2,1)}), bf16[8,192,512]{2,1,0:T(8,128)(2,1)}, u32[]{:S(2)}, u32[]{:S(2)}) async-start(bf16[8,192,512]{2,1,0:T(8,128)(2,1)} %get-tuple-element.135), calls=%async_computation.2 | async-start | bytes 3145728 | tf_op jit(solution)/shard_map/all_to_all | solution.py:940
  172.2 31.4 %copy-start.13 = (bf16[8,64,512]{2,1,0:T(8,128)(2,1)S(1)}, bf16[8,64,512]{2,1,0:T(8,128)(2,1)}, u32[]{:S(2)}) copy-start(bf16[8,64,512]{2,1,0:T(8,128)(2,1)} %get-tuple-element.147.mixed_ref) | copy-start | bytes 1572868
  195.9 40.8 %all-to-all-start.3 = ((bf16[8,192,512]{2,1,0:T(8,128)(2,1)}), bf16[8,192,512]{2,1,0:T(8,128)(2,1)S(1)}, u32[]{:S(2)}, u32[]{:S(2)}) async-start(bf16[8,192,512]{2,1,0:T(8,128)(2,1)} %get-tuple-element.139), calls=%async_computation.3 | async-start | bytes 3145728 | tf_op jit(solution)/shard_map/all_to_all | solution.py:940
  199.6 5.1 collective-permute-start.3
  199.6 4.0 collective-permute-start.5
  236.7 1.2 copy-start.8
  237.9 29.8 %all-to-all-start.4 = ((bf16[8,128,512]{2,1,0:T(8,128)(2,1)}), bf16[8,128,512]{2,1,0:T(8,128)(2,1)S(1)}, u32[]{:S(2)}, u32[]{:S(2)}) async-start(bf16[8,128,512]{2,1,0:T(8,128)(2,1)} %pad_maximum_fusion.1), calls=%async_computation.4 | async-start | bytes 2097152 | tf_op jit(solution)/shard_map/all_to_all | solution.py:940
  241.8 14.7 %collective-permute-start.4 = (bf16[8,64,512]{2,1,0:T(8,128)(2,1)}, bf16[8,64,512]{2,1,0:T(8,128)(2,1)S(1)}, u32[]{:S(2)}, u32[]{:S(2)}) collective-permute-start(bf16[8,64,512]{2,1,0:T(8,128)(2,1)} %get-tuple-element.146.mixed_ref), channel_id=1, source_target_pairs={{0,8},{1,9},{2,10},{3,11},{4,12},{5,13},{6,14},{7,15},{8,0},{9,1},... | collective-permute-start | bytes 1572872 | tf_op jit(solution)/shard_map/ppermute | solution.py:950
  268.7 47.2 %all-to-all-start.5 = ((bf16[8,128,512]{2,1,0:T(8,128)(2,1)}), bf16[8,128,512]{2,1,0:T(8,128)(2,1)S(1)}, u32[]{:S(2)}, u32[]{:S(2)}) async-start(bf16[8,128,512]{2,1,0:T(8,128)(2,1)} %pad_maximum_fusion), calls=%async_computation.5 | async-start | bytes 2097152 | tf_op jit(solution)/shard_map/all_to_all | solution.py:940
  315.9 7.8 copy-start.30
  315.9 8.4 %copy-start.5 = (bf16[8,128,512]{2,1,0:T(8,128)(2,1)}, bf16[8,128,512]{2,1,0:T(8,128)(2,1)S(1)}, u32[]{:S(2)}) copy-start(bf16[8,128,512]{2,1,0:T(8,128)(2,1)S(1)} %all-to-all-done.5) | copy-start | bytes 3145732
  315.9 50.7 %all-to-all-start.6 = ((bf16[8,128,512]{2,1,0:T(8,128)(2,1)}), bf16[8,128,512]{2,1,0:T(8,128)(2,1)}, u32[]{:S(2)}, u32[]{:S(2)}) async-start(bf16[8,128,512]{2,1,0:T(8,128)(2,1)} %bitcast.60), calls=%async_computation.6 | async-start | bytes 2097152 | tf_op jit(solution)/shard_map/all_to_all | solution.py:940
  380.3 32.5 %collective-permute-start.6 = (bf16[512,4096]{1,0:T(8,128)(2,1)}, bf16[512,4096]{1,0:T(8,128)(2,1)}, u32[]{:S(2)}, u32[]{:S(2)}) collective-permute-start(bf16[512,4096]{1,0:T(8,128)(2,1)} %get-tuple-element.175), channel_id=1, source_target_pairs={{0,8},{1,9},{2,10},{3,11},{4,12},{5,13},{6,14},{7,15},{8,0},{9,1},... | collective-permute-start | bytes 12582920 | tf_op jit(solution)/shard_map/ppermute | solution.py:950
  381.2 31.7 %all-to-all-start.7 = ((bf16[8,128,512]{2,1,0:T(8,128)(2,1)}), bf16[8,128,512]{2,1,0:T(8,128)(2,1)S(1)}, u32[]{:S(2)}, u32[]{:S(2)}) async-start(bf16[8,128,512]{2,1,0:T(8,128)(2,1)} %bitcast.61), calls=%async_computation.7 | async-start | bytes 2097152 | tf_op jit(solution)/shard_map/all_to_all | solution.py:940
  386.9 409.8 %reduce-scatter.2.cloned.1.call-start = ((), (), s32[]{:S(2)}) async-start(), calls=%async_computation.17 | async-start | bytes 19464192 | tf_op jit(solution)/shard_map/reduce_scatter | solution.py:1095
  388.2 14.2 %collective-permute-start.7 = (bf16[8,64,512]{2,1,0:T(8,128)(2,1)S(1)}, bf16[8,64,512]{2,1,0:T(8,128)(2,1)}, u32[]{:S(2)}, u32[]{:S(2)}) collective-permute-start(bf16[8,64,512]{2,1,0:T(8,128)(2,1)S(1)} %slice.137), channel_id=1, source_target_pairs={{0,8},{1,9},{2,10},{3,11},{4,12},{5,13},{6,14},{7,15},{8,0},{9,1},... | collective-permute-start | bytes 1572872 | tf_op jit(solution)/shard_map/ppermute | solution.py:950
  412.8 30.5 %copy-start.7 = (bf16[8,128,512]{2,1,0:T(8,128)(2,1)}, bf16[8,128,512]{2,1,0:T(8,128)(2,1)S(1)}, u32[]{:S(2)}) copy-start(bf16[8,128,512]{2,1,0:T(8,128)(2,1)S(1)} %all-to-all-done.7.grad_ref) | copy-start | bytes 3145732
  437.9 50.4 %collective-permute-start.8 = (bf16[256,4096]{1,0:T(8,128)(2,1)}, bf16[256,4096]{1,0:T(8,128)(2,1)}, u32[]{:S(2)}, u32[]{:S(2)}) collective-permute-start(bf16[256,4096]{1,0:T(8,128)(2,1)} %get-tuple-element.256), channel_id=1, source_target_pairs={{0,16},{1,17},{2,18},{3,19},{4,20},{5,21},{6,22},{7,23},{8,24},{9,... | collective-permute-start | bytes 6291464 | tf_op jit(solution)/shard_map/ppermute | solution.py:950
  444.2 49.1 %collective-permute-start.9 = (bf16[8,64,512]{2,1,0:T(8,128)(2,1)}, bf16[8,64,512]{2,1,0:T(8,128)(2,1)}, u32[]{:S(2)}, u32[]{:S(2)}) collective-permute-start(bf16[8,64,512]{2,1,0:T(8,128)(2,1)} %slice.146), channel_id=1, source_target_pairs={{0,8},{1,9},{2,10},{3,11},{4,12},{5,13},{6,14},{7,15},{8,0},{9,1},... | collective-permute-start | bytes 1572872 | tf_op jit(solution)/shard_map/ppermute | solution.py:950
  462.2 26.1 %copy-start.2 = (bf16[256,4096]{1,0:T(8,128)(2,1)S(1)}, bf16[256,4096]{1,0:T(8,128)(2,1)}, u32[]{:S(2)}) copy-start(bf16[256,4096]{1,0:T(8,128)(2,1)} %get-tuple-element.188) | copy-start | bytes 6291460
  462.2 67.5 %all-to-all-start.8 = ((bf16[8,192,512]{2,1,0:T(8,128)(2,1)}), bf16[8,192,512]{2,1,0:T(8,128)(2,1)}, u32[]{:S(2)}, u32[]{:S(2)}) async-start(bf16[8,192,512]{2,1,0:T(8,128)(2,1)} %get-tuple-element.192), calls=%async_computation.8 | async-start | bytes 3145728 | tf_op jit(solution)/shard_map/all_to_all | solution.py:940
  491.6 35.6 %collective-permute-start.11 = (bf16[128,4096]{1,0:T(8,128)(2,1)}, bf16[128,4096]{1,0:T(8,128)(2,1)}, u32[]{:S(2)}, u32[]{:S(2)}) collective-permute-start(bf16[128,4096]{1,0:T(8,128)(2,1)} %get-tuple-element.258), channel_id=1, source_target_pairs={{0,1},{1,0},{2,3},{3,2},{4,5},{5,4},{6,7},{7,6},{8,9},{9,8},{10,11... | collective-permute-start | bytes 3145736 | tf_op jit(solution)/shard_map/ppermute | solution.py:950
  506.9 22.9 %collective-permute-start.10 = (bf16[8,192,512]{2,1,0:T(8,128)(2,1)}, bf16[8,192,512]{2,1,0:T(8,128)(2,1)S(1)}, u32[]{:S(2)}, u32[]{:S(2)}) collective-permute-start(bf16[8,192,512]{2,1,0:T(8,128)(2,1)} %get-tuple-element.191), channel_id=1, source_target_pairs={{0,8},{1,9},{2,10},{3,11},{4,12},{5,13},{6,14},{7,15},{8,0},{9,1},... | collective-permute-start | bytes 4718600 | tf_op jit(solution)/shard_map/ppermute | solution.py:950
  529.8 1.2 copy-start.12
  531.0 61.8 %all-to-all-start.9 = ((bf16[8,192,512]{2,1,0:T(8,128)(2,1)}), bf16[8,192,512]{2,1,0:T(8,128)(2,1)S(1)}, u32[]{:S(2)}, u32[]{:S(2)}) async-start(bf16[8,192,512]{2,1,0:T(8,128)(2,1)} %copy-done.12), calls=%async_computation.9 | async-start | bytes 3145728 | tf_op jit(solution)/shard_map/all_to_all | solution.py:940
  538.0 52.7 %collective-permute-start.12 = (bf16[64,4096]{1,0:T(8,128)(2,1)}, bf16[64,4096]{1,0:T(8,128)(2,1)}, u32[]{:S(2)}, u32[]{:S(2)}) collective-permute-start(bf16[64,4096]{1,0:T(8,128)(2,1)} %get-tuple-element.260), channel_id=1, source_target_pairs={{0,2},{1,3},{2,0},{3,1},{4,6},{5,7},{6,4},{7,5},{8,10},{9,11},{10,... | collective-permute-start | bytes 1572872 | tf_op jit(solution)/shard_map/ppermute | solution.py:950
  592.8 45.6 %copy-start.3 = (bf16[8,192,512]{2,1,0:T(8,128)(2,1)}, bf16[8,192,512]{2,1,0:T(8,128)(2,1)S(1)}, u32[]{:S(2)}) copy-start(bf16[8,192,512]{2,1,0:T(8,128)(2,1)S(1)} %all-to-all-done.9.rest_1_) | copy-start | bytes 4718596
  592.8 66.5 %all-to-all-start.10 = ((bf16[8,192,512]{2,1,0:T(8,128)(2,1)}), bf16[8,192,512]{2,1,0:T(8,128)(2,1)}, u32[]{:S(2)}, u32[]{:S(2)}) async-start(bf16[8,192,512]{2,1,0:T(8,128)(2,1)} %get-tuple-element.202), calls=%async_computation.10 | async-start | bytes 3145728 | tf_op jit(solution)/shard_map/all_to_all | solution.py:940
  638.4 24.5 %copy-start.28 = (s32[32]{0:T(128)S(1)}, s32[32]{0:T(128)}, u32[]{:S(2)}) copy-start(s32[32]{0:T(128)} %constant.43.clone) | copy-start | bytes 388
  638.4 24.5 %copy-start.29 = (s32[32]{0:T(128)S(1)}, s32[32]{0:T(128)}, u32[]{:S(2)}) copy-start(s32[32]{0:T(128)} %constant.44.clone) | copy-start | bytes 388
  638.4 24.6 %copy-start.27 = (s32[32]{0:T(128)S(1)}, s32[32]{0:T(128)}, u32[]{:S(2)}) copy-start(s32[32]{0:T(128)} %broadcast_xor_fusion.2.table_ref) | copy-start | bytes 388
  638.4 25.1 %copy-start.18 = (f32[1,1024]{1,0:T(1,128)S(1)}, f32[1,1024]{1,0:T(1,128)}, u32[]{:S(2)}) copy-start(f32[1,1024]{1,0:T(1,128)} %get-tuple-element.154) | copy-start | bytes 12292
  638.4 25.1 %copy-start.19 = (f32[1,1024]{1,0:T(1,128)S(1)}, f32[1,1024]{1,0:T(1,128)}, u32[]{:S(2)}) copy-start(f32[1,1024]{1,0:T(1,128)} %get-tuple-element.163) | copy-start | bytes 12292
  638.4 25.1 %copy-start.20 = (f32[8,128]{1,0:T(8,128)S(1)}, f32[8,128]{1,0:T(8,128)}, u32[]{:S(2)}) copy-start(f32[8,128]{1,0:T(8,128)} %get-tuple-element.187) | copy-start | bytes 12292
  638.4 25.1 %copy-start.22 = (f32[8,128]{1,0:T(8,128)S(1)}, f32[8,128]{1,0:T(8,128)}, u32[]{:S(2)}) copy-start(f32[8,128]{1,0:T(8,128)} %get-tuple-element.197) | copy-start | bytes 12292
  638.4 28.1 %copy-start.21 = (f32[8,128]{1,0:T(8,128)S(1)}, f32[8,128]{1,0:T(8,128)}, u32[]{:S(2)}) copy-start(f32[8,128]{1,0:T(8,128)} %get-tuple-element.193) | copy-start | bytes 12292
  638.4 28.1 %copy-start.23 = (f32[8,128]{1,0:T(8,128)S(1)}, f32[8,128]{1,0:T(8,128)}, u32[]{:S(2)}) copy-start(f32[8,128]{1,0:T(8,128)} %get-tuple-element.203) | copy-start | bytes 12292
  638.4 3.7 collective-permute-start.13
  642.1 17.1 %copy-start.11 = (bf16[8,192,512]{2,1,0:T(8,128)(2,1)}, bf16[8,192,512]{2,1,0:T(8,128)(2,1)S(1)}, u32[]{:S(2)}) copy-start(bf16[8,192,512]{2,1,0:T(8,128)(2,1)S(1)} %collective-permute-done.13) | copy-start | bytes 4718596
  659.3 60.3 %all-to-all-start.11 = ((bf16[8,192,512]{2,1,0:T(8,128)(2,1)}), bf16[8,192,512]{2,1,0:T(8,128)(2,1)S(1)}, u32[]{:S(2)}, u32[]{:S(2)}) async-start(bf16[8,192,512]{2,1,0:T(8,128)(2,1)} %copy-done.11), calls=%async_computation.11 | async-start | bytes 3145728 | tf_op jit(solution)/shard_map/all_to_all | solution.py:940
  663.6 69.3 %collective-permute-start.14 = (bf16[32,4096]{1,0:T(8,128)(2,1)}, bf16[32,4096]{1,0:T(8,128)(2,1)}, u32[]{:S(2)}, u32[]{:S(2)}) collective-permute-start(bf16[32,4096]{1,0:T(8,128)(2,1)} %get-tuple-element.262), channel_id=1, source_target_pairs={{0,4},{1,5},{2,6},{3,7},{4,0},{5,1},{6,2},{7,3},{8,12},{9,13},{10,... | collective-permute-start | bytes 786440 | tf_op jit(solution)/shard_map/ppermute | solution.py:950
  719.6 1.2 copy-start.4
  720.7 11.5 %copy-start.24 = (f32[1,1024]{1,0:T(1,128)S(1)}, f32[1,1024]{1,0:T(1,128)}, u32[]{:S(2)}) copy-start(f32[1,1024]{1,0:T(1,128)} %get-tuple-element.209) | copy-start | bytes 12292
  794.7 5.5 copy-start.16
  794.7 6.1 copy-start.15
  795.3 6.8 copy-start.1
  796.6 4.8 copy-start.14
  796.6 2.8 slice-start
  (1 other events, 1.0 us)
Sparse Core Ops, SparseCore 0:
  10.3 49.0 all-gather.15
  61.0 22.5 all-gather.7
  85.2 58.2 all-gather.9
  145.0 58.9 all-gather.11
  205.4 58.3 all-gather.13
  432.5 283.0 reduce-scatter.1

commit v5 on v4

--- a/solution.py
+++ b/solution.py
@@ -1092,7 +1092,7 @@
         mixed_all = [mixed_tok[u] for u in range(len(units))]
         terms = weight_grad(mixed_all, column(6), False, struct, out, fold, terms, "out_grad")
         terms = terms.reshape(ffn, spare)
-        holder["owned"] = lax.psum_scatter(terms, ("shard", "seq"), scatter_dimension=0, tiled=True)
+        holder["half"] = lax.psum_scatter(terms, "shard", scatter_dimension=0, tiled=True)
         return terms
 
     def wide_sum(a, b):
@@ -1206,6 +1206,9 @@
                 ahead = leaving
             elif task not in late:
                 token = token + leaving
+        if "half" in holder and index == len(steps) - 2:
+            half = after(holder["half"], *token)
+            holder["owned"] = lax.psum_scatter(half, "seq", scatter_dimension=0, tiled=True)
         if send is not None:
             moved = exchange(after(send[0](), *token))
             done = (moved,)

time: 822 us -> 845 us (1.028)
  Pallas kernels: 393 us -> 457 us
  waiting for transfers between devices: 251 us -> 192 us
  starting transfers between devices: 73.5 us -> 95.8 us
    ppermute x15, waiting for transfers between devices: 74.1 us -> 28.1 us  [permute(): lax.ppermute(value, ('shard', 'seq'), [(i, i ^ mask) for i in range(devic...]
    pallas_call x4, Pallas kernels: 97.6 us -> 138 us  [attend_backward(): pl.pallas_call(functools.partial(backward_kernel, (local, head_dim, block...]
    ppermute x15, starting transfers between devices: 16.5 us -> 36 us  [permute(): lax.ppermute(value, ('shard', 'seq'), [(i, i ^ mask) for i in range(devic...]
    pallas_call x4, Pallas kernels: 57.8 us -> 77.1 us  [attend_forward(): pl.pallas_call(functools.partial(forward_kernel, (local, head_dim, block,...]
    all_to_all x12, waiting for transfers between devices: 161 us -> 148 us  [exchange(): lax.all_to_all(values, 'seq', split_axis=0, concat_axis=0, tiled=True)]
  transfers between devices with their start and end apart: 33 -> 34, of which waited for: 15 -> 12; matrix products, arithmetic and copies ran while one was open for 4% -> 4% of each run, Pallas kernels for 44% -> 50%
where the time goes in v5:
time: 845 us; the launch traced here: 839 us
  Pallas kernels  457 us (54%)
  waiting for transfers between devices  192 us (23%)
  starting transfers between devices  95.8 us (11%)
  blocking collectives  32.2 us (4%)
  other arithmetic  28.1 us (3%)
  local copies, waits for them, and re-layouts  18.4 us (2%)
  between operations  15.1 us (2%)
    all_to_all x12, waiting for transfers between devices, exchange(): lax.all_to_all(values, 'seq', split_axis=0, concat_axis=0, tiled=True)  148 us
    pallas_call x4, Pallas kernels, attend_backward(): pl.pallas_call(functools.partial(backward_kernel, (local, head_dim, block...  138 us
    pallas_call x2, Pallas kernels, middle_part(): pl.pallas_call(functools.partial(middle_kernel, (head_dim, output is not...  84.6 us
    pallas_call x4, Pallas kernels, attend_forward(): pl.pallas_call(functools.partial(forward_kernel, (local, head_dim, block,...  77.1 us
    all_to_all x12, starting transfers between devices, exchange(): lax.all_to_all(values, 'seq', split_axis=0, concat_axis=0, tiled=True)  59.4 us
    pallas_call x1, Pallas kernels, reduce_rows(): pl.pallas_call(functools.partial(reduce_kernel, orders, count), in_specs=...  50.5 us
    ppermute x15, starting transfers between devices, permute(): lax.ppermute(value, ('shard', 'seq'), [(i, i ^ mask) for i in range(devic...  36 us
    pallas_call x3, Pallas kernels, weight_grad(): pl.pallas_call(functools.partial(weights_kernel, units), grid=(steps,), i...  33.7 us
  transfers between devices with their start and end apart: 34, of which 12 were waited for; matrix products, arithmetic and copies ran while one was open for 4% of the time, Pallas kernels for 50%

profile of v5, /device:TPU:0, one launch (start us, length us, event | category | flops | bytes accessed | tf_op | source)
XLA Modules:
  0.0 838.5 jit_solution(7680036982762238368)
XLA Ops:
  7.2 3.0 turn_weights.1
  12.3 32.2 %all-gather.1 = s32[16,1,512]{2,1,0:T(1,128)S(1)} all-gather(s32[2,1,512]{2,1,0:T(1,128)S(1)} %copy-done.16), channel_id=3, replica_groups=mesh['shard'=4,'seq'=8] {'seq'}, dimensions={0}, use_global_device_ids=true | all-gather | bytes 36864 | tf_op jit(solution)/shard_map/all_gather | solution.py:956
  44.7 1.2 multiply_sine_fusion
  45.9 13.5 %all-gather.16.cloned.1.call-done = bf16[12288,256]{1,0:T(8,128)(2,1)} async-done(((bf16[3072,256]{1,0:T(8,128)(2,1)}), bf16[12288,256]{1,0:T(8,128)(2,1)}) %all-gather.16.cloned.1.call-update) | async-done | bytes 6291472 | tf_op jit(solution)/shard_map/all_gather | solution.py:946
  59.5 10.7 %project.2 = (bf16[1024,512]{1,0:T(8,128)(2,1)}, bf16[8,192,512]{2,1,0:T(8,128)(2,1)}, bf16[8,192,512]{2,1,0:T(8,128)(2,1)}) custom-call(s32[1]{0:T(128)} %bitcast.2.core_ref, bf16[2,1,512,1024]{3,2,1,0:T(8,128)(2,1)} %tokens_ref.11, f32[1,1024]{1,0:T(1,128)} %bitcast.65, bf16[4,3072,256]{2,1,0:T(8,128)(2,1)} %bitcast.44, bf16[4,3072,256]{2,1,0:T(8,128)(2,1)} %bitcast.45, ...), custom_call_target="tpu_custom_call" | custom-call | flops 201326592 | bytes 12582912 | tf_op jit(solution)/shard_map/project/pallas_call | solution.py:442
  70.1 5.5 all-to-all-start
  76.2 10.6 %project.3 = (bf16[1024,512]{1,0:T(8,128)(2,1)}, bf16[8,192,512]{2,1,0:T(8,128)(2,1)}, bf16[8,192,512]{2,1,0:T(8,128)(2,1)}) custom-call(s32[1]{0:T(128)} %bitcast.2.core_ref, bf16[2,1,512,1024]{3,2,1,0:T(8,128)(2,1)} %tokens_ref.11, f32[1,1024]{1,0:T(1,128)} %bitcast.66, bf16[4,3072,256]{2,1,0:T(8,128)(2,1)} %bitcast.47, bf16[4,3072,256]{2,1,0:T(8,128)(2,1)} %bitcast.48, ...), custom_call_target="tpu_custom_call" | custom-call | flops 201326592 | bytes 12582912 | tf_op jit(solution)/shard_map/project/pallas_call | solution.py:442
  86.8 26.2 %all-to-all-done = bf16[8,192,512]{2,1,0:T(8,128)(2,1)S(1)} async-done(((bf16[8,192,512]{2,1,0:T(8,128)(2,1)}), bf16[8,192,512]{2,1,0:T(8,128)(2,1)S(1)}, u32[]{:S(2)}, u32[]{:S(2)}) %all-to-all-start) | async-done | bytes 1572896 | tf_op jit(solution)/shard_map/all_to_all | solution.py:940
  114.2 3.6 all-to-all-start.1
  119.1 1.8 collective-permute-done.1
  122.2 9.1 %attend_forward.4 = (bf16[8,64,512]{2,1,0:T(8,128)(2,1)}, f32[8,1,512]{2,1,0:T(1,128)}) custom-call(s32[1]{0:T(128)} %bitcast.7.len_ref, f32[1,2]{1,0:T(1,128)} %copy.48.bias_ref, bf16[8,192,512]{2,1,0:T(8,128)(2,1)} %collective-permute-done.2.x_ref, f32[8,1,512]{2,1,0:T(1,128)} %get-tuple-element.270.ids_ref), custom_call_target="tpu_custom_call" | custom-call | flops 2147483648 | bytes 3145728 | tf_op jit(solution)/shard_map/attend_forward/pallas_call | solution.py:170
  131.3 23.7 %all-to-all-done.1.x_ref = bf16[8,192,512]{2,1,0:T(8,128)(2,1)S(1)} async-done(((bf16[8,192,512]{2,1,0:T(8,128)(2,1)}), bf16[8,192,512]{2,1,0:T(8,128)(2,1)S(1)}, u32[]{:S(2)}, u32[]{:S(2)}) %all-to-all-start.1) | async-done | bytes 1572896 | tf_op jit(solution)/shard_map/all_to_all | solution.py:940
  155.0 4.3 all-to-all-start.2
  160.7 22.5 %attend_forward.5 = (bf16[8,64,512]{2,1,0:T(8,128)(2,1)}, f32[8,1,512]{2,1,0:T(1,128)}) custom-call(s32[1]{0:T(128)} %bitcast.9.len_ref, f32[1,2]{1,0:T(1,128)} %copy.48.bias_ref, bf16[8,192,512]{2,1,0:T(8,128)(2,1)} %copy-done.9, f32[8,1,512]{2,1,0:T(1,128)} %get-tuple-element.268.ids_ref), custom_call_target="tpu_custom_call" | custom-call | flops 2147483648 | bytes 3145728 | tf_op jit(solution)/shard_map/attend_forward/pallas_call | solution.py:170
  183.2 12.8 %all-to-all-done.2 = bf16[8,192,512]{2,1,0:T(8,128)(2,1)} async-done(((bf16[8,192,512]{2,1,0:T(8,128)(2,1)}), bf16[8,192,512]{2,1,0:T(8,128)(2,1)}, u32[]{:S(2)}, u32[]{:S(2)}) %all-to-all-start.2) | async-done | bytes 1572896 | tf_op jit(solution)/shard_map/all_to_all | solution.py:940
  196.0 3.6 all-to-all-start.3
  200.2 3.9 collective-permute-done.5
  205.1 18.1 %attend_forward.6 = (bf16[8,64,512]{2,1,0:T(8,128)(2,1)}, f32[8,1,512]{2,1,0:T(1,128)}) custom-call(s32[1]{0:T(128)} %bitcast.11.len_ref, f32[1,2]{1,0:T(1,128)} %copy.48.bias_ref, bf16[8,192,512]{2,1,0:T(8,128)(2,1)} %collective-permute-done.3.x_ref, f32[8,1,512]{2,1,0:T(1,128)} %get-tuple-element.269.ids_ref), custom_call_target="tpu_custom_call" | custom-call | flops 2147483648 | bytes 3145728 | tf_op jit(solution)/shard_map/attend_forward/pallas_call | solution.py:170
  223.2 13.6 %all-to-all-done.3.x_ref = bf16[8,192,512]{2,1,0:T(8,128)(2,1)S(1)} async-done(((bf16[8,192,512]{2,1,0:T(8,128)(2,1)}), bf16[8,192,512]{2,1,0:T(8,128)(2,1)S(1)}, u32[]{:S(2)}, u32[]{:S(2)}) %all-to-all-start.3) | async-done | bytes 1572896 | tf_op jit(solution)/shard_map/all_to_all | solution.py:940
  238.0 3.9 all-to-all-start.4
  241.9 27.4 %attend_forward.7 = (bf16[8,64,512]{2,1,0:T(8,128)(2,1)}, f32[8,1,512]{2,1,0:T(1,128)}) custom-call(s32[1]{0:T(128)} %bitcast.len_ref, f32[1,2]{1,0:T(1,128)} %copy.48.bias_ref, bf16[8,192,512]{2,1,0:T(8,128)(2,1)} %copy-done.8, f32[8,1,512]{2,1,0:T(1,128)} %get-tuple-element.267.ids_ref), custom_call_target="tpu_custom_call" | custom-call | flops 2147483648 | bytes 3145728 | tf_op jit(solution)/shard_map/attend_forward/pallas_call | solution.py:170
  269.3 2.1 pad_maximum_fusion
  272.4 6.0 all-to-all-start.5
  278.5 1.3 add_add_fusion.1.info_ref
  279.8 42.3 %middle_part.2 = (bf16[2,1,512,1024]{3,2,1,0:T(8,128)(2,1)}, bf16[1024,512]{1,0:T(8,128)(2,1)}, bf16[1024,512]{1,0:T(8,128)(2,1)}, bf16[4096,512]{1,0:T(8,128)(2...) custom-call(s32[3]{0:T(128)} %add_add_fusion.1.info_ref, ...), custom_call_target="tpu_custom_call" | custom-call | flops 1610612736 | bytes 33554432 | tf_op jit(solution)/shard_map/middle_part/pallas_call | solution.py:565
  322.1 6.5 all-to-all-start.6
  328.6 1.3 add_add_fusion.info_ref
  330.5 42.3 %middle_part.3 = (bf16[2,1,512,1024]{3,2,1,0:T(8,128)(2,1)}, bf16[1024,512]{1,0:T(8,128)(2,1)}, bf16[1024,512]{1,0:T(8,128)(2,1)}, bf16[4096,512]{1,0:T(8,128)(2...) custom-call(s32[3]{0:T(128)} %add_add_fusion.info_ref, ...), custom_call_target="tpu_custom_call", output_to_operand_aliasing={{0}: (9, {})} | custom-call | flops 1610612736 | bytes 33554432 | tf_op jit(solution)/shard_map/middle_part/pallas_call | solution.py:565
  372.8 13.7 %up_grad.1 = (bf16[512,4096]{1,0:T(8,128)(2,1)}, bf16[512,4096]{1,0:T(8,128)(2,1)}) custom-call(s32[32]{0:T(128)} %broadcast_xor_fusion.2.table_ref, bf16[1024,512]{1,0:T(8,128)(2,1)} %get-tuple-element.170.refs_0_, bf16[1024,512]{1,0:T(8,128)(2,1)} %get-tuple-element.171.refs_1_, bf16[512,4096]{1,0:T(8,128)(2,1)} %get-tuple-element.174.refs_2_, ...), custom_call_target="tpu_custom_call" | custom-call | flops 536870912 | bytes 16777216 | tf_op jit(solution)/shard_map/up_grad/pallas_call | solution.py:736
  386.5 6.0 all-to-all-start.7
  394.1 14.1 %down_grad.1.refs_4_ = bf16[32,4,32,2304]{3,2,1,0:T(8,128)(2,1)} custom-call(bf16[4096,512]{1,0:T(8,128)(2,1)} %get-tuple-element.180.refs_0_, bf16[4096,512]{1,0:T(8,128)(2,1)} %get-tuple-element.181.refs_1_, bf16[512,1024]{1,0:T(8,128)(2,1)} %get-tuple-element.184.refs_2_, bf16[512,1024]{1,0:T(8,128)(2,1)} %get-tuple-element.185.refs_3_), custom_call_target="tpu_custom_call" | custom-call | flops 536870912 | bytes 8388608 | tf_op jit(solution)/shard_map/down_grad/pallas_call | solution.py:790
  408.2 10.7 %all-to-all-done.7.grad_ref = bf16[8,128,512]{2,1,0:T(8,128)(2,1)S(1)} async-done(((bf16[8,128,512]{2,1,0:T(8,128)(2,1)}), bf16[8,128,512]{2,1,0:T(8,128)(2,1)S(1)}, u32[]{:S(2)}, u32[]{:S(2)}) %all-to-all-start.7) | async-done | bytes 1048608 | tf_op jit(solution)/shard_map/all_to_all | solution.py:940
  419.0 13.5 %gate_grad.1.refs_4_ = bf16[32,4,32,2304]{3,2,1,0:T(8,128)(2,1)} custom-call(bf16[1024,512]{1,0:T(8,128)(2,1)} %get-tuple-element.170.refs_0_, bf16[1024,512]{1,0:T(8,128)(2,1)} %get-tuple-element.171.refs_1_, bf16[512,4096]{1,0:T(8,128)(2,1)} %get-tuple-element.178.refs_2_, ...), custom_call_target="tpu_custom_call", output_to_operand_aliasing={{}: (4, {})} | custom-call | flops 536870912 | bytes 8388608 | tf_op jit(solution)/shard_map/gate_grad/pallas_call | solution.py:790
  432.5 6.0 out_grad.1
  438.6 5.6 add_convert_fusion
  445.0 41.9 %attend_backward.4 = (bf16[8,192,512]{2,1,0:T(8,128)(2,1)}, f32[8,128]{1,0:T(8,128)}) custom-call(s32[1]{0:T(128)} %bitcast.9.len_ref, f32[1,2]{1,0:T(1,128)} %copy.48.bias_ref, bf16[8,192,512]{2,1,0:T(8,128)(2,1)} %copy-done.9, f32[8,1,512]{2,1,0:T(1,128)} %get-tuple-element.268.ids_ref, bf16[8,128,512]{2,1,0:T(8,128)(2,1)} %all-to-all-done.6.grad_ref, ...), custom_call_target="tpu_custom_call" | custom-call | flops 5368709120 | bytes 4718592 | tf_op jit(solution)/shard_map/attend_backward/pallas_call | solution.py:309
  486.9 4.6 all-to-all-start.8
  491.6 18.5 %collective-permute-done.8 = bf16[256,4096]{1,0:T(8,128)(2,1)} collective-permute-done((bf16[256,4096]{1,0:T(8,128)(2,1)}, bf16[256,4096]{1,0:T(8,128)(2,1)}, u32[]{:S(2)}, u32[]{:S(2)}) %collective-permute-start.8) | collective-permute-done | bytes 2097184 | tf_op jit(solution)/shard_map/ppermute | solution.py:950
  510.1 3.3 add_convert_fusion.2
  513.4 1.4 collective-permute-start.11
  514.8 13.1 %attend_backward.5 = (bf16[8,192,512]{2,1,0:T(8,128)(2,1)}, f32[8,128]{1,0:T(8,128)}) custom-call(s32[1]{0:T(128)} %bitcast.7.len_ref, f32[1,2]{1,0:T(1,128)} %copy.48.bias_ref, bf16[8,192,512]{2,1,0:T(8,128)(2,1)} %collective-permute-done.2.x_ref, f32[8,1,512]{2,1,0:T(1,128)} %get-tuple-element.270.ids_ref, ...), custom_call_target="tpu_custom_call" | custom-call | flops 5368709120 | bytes 4718592 | tf_op jit(solution)/shard_map/attend_backward/pallas_call | solution.py:309
  527.9 23.4 %collective-permute-start.10 = (bf16[8,192,512]{2,1,0:T(8,128)(2,1)}, bf16[8,192,512]{2,1,0:T(8,128)(2,1)S(1)}, u32[]{:S(2)}, u32[]{:S(2)}) collective-permute-start(bf16[8,192,512]{2,1,0:T(8,128)(2,1)} %get-tuple-element.192), channel_id=1, source_target_pairs={{0,8},{1,9},{2,10},{3,11},{4,12},{5,13},{6,14},{7,15},{8,0},{9,1},... | collective-permute-start | bytes 4718600 | tf_op jit(solution)/shard_map/ppermute | solution.py:950
  551.2 2.6 add_convert_fusion.4
  555.6 5.0 all-to-all-start.9
  560.6 2.0 collective-permute-start.12
  562.7 51.3 %attend_backward.6 = (bf16[8,192,512]{2,1,0:T(8,128)(2,1)}, f32[8,128]{1,0:T(8,128)}) custom-call(s32[1]{0:T(128)} %bitcast.len_ref, f32[1,2]{1,0:T(1,128)} %copy.48.bias_ref, bf16[8,192,512]{2,1,0:T(8,128)(2,1)} %copy-done.8, f32[8,1,512]{2,1,0:T(1,128)} %get-tuple-element.267.ids_ref, bf16[8,128,512]{2,1,0:T(8,128)(2,1)} %copy-done.7, ...), custom_call_target="tpu_custom_call" | custom-call | flops 5368709120 | bytes 4718592 | tf_op jit(solution)/shard_map/attend_backward/pallas_call | solution.py:309
  614.0 2.0 add_convert_fusion.6
  616.0 4.5 all-to-all-start.10
  620.6 31.9 %attend_backward.7 = (bf16[8,192,512]{2,1,0:T(8,128)(2,1)}, f32[8,128]{1,0:T(8,128)}) custom-call(s32[1]{0:T(128)} %bitcast.11.len_ref, f32[1,2]{1,0:T(1,128)} %copy.48.bias_ref, bf16[8,192,512]{2,1,0:T(8,128)(2,1)} %collective-permute-done.3.x_ref, f32[8,1,512]{2,1,0:T(1,128)} %get-tuple-element.269.ids_ref, ...), custom_call_target="tpu_custom_call" | custom-call | flops 5368709120 | bytes 4718592 | tf_op jit(solution)/shard_map/attend_backward/pallas_call | solution.py:309
  652.7 1.3 copy-done.29
  653.9 4.7 collective-permute-start.13
  658.7 3.2 collective-permute-done.13
  661.9 5.7 all-to-all-start.11
  668.2 3.0 collective-permute-start.14
  671.6 11.5 %final_part.2 = (bf16[2,1,512,1024]{3,2,1,0:T(8,128)(2,1)}, bf16[1024,512]{1,0:T(8,128)(2,1)}, bf16[1024,512]{1,0:T(8,128)(2,1)}, bf16[1024,512]{1,0:T(8,128)(2,1)}, f32[1,1024]{1,0:T(1,128)}) custom-call(s32[1]{0:T(128)} %bitcast.2.core_ref, bf16[2,1,512,1024]{3,2,1,0:T(8,128)(2,1)} %tokens_ref.11, f32[512,1024]{1,0:T(8,128)} %get-tuple-element.206.grad_res_ref, ...), custom_call_target="tpu_custom_call" | custom-call | flops 201326592 | bytes 12582912 | tf_op jit(solution)/shard_map/final_part/pallas_call | solution.py:679
  683.1 60.9 %all-to-all-done.11.rest_1_ = bf16[8,192,512]{2,1,0:T(8,128)(2,1)S(1)} async-done(((bf16[8,192,512]{2,1,0:T(8,128)(2,1)}), bf16[8,192,512]{2,1,0:T(8,128)(2,1)S(1)}, u32[]{:S(2)}, u32[]{:S(2)}) %all-to-all-start.11) | async-done | bytes 1572896 | tf_op jit(solution)/shard_map/all_to_all | solution.py:940
  744.0 1.2 copy-done.4
  745.3 11.6 %final_part.3 = (bf16[2,1,512,1024]{3,2,1,0:T(8,128)(2,1)}, bf16[1024,512]{1,0:T(8,128)(2,1)}, bf16[1024,512]{1,0:T(8,128)(2,1)}, bf16[1024,512]{1,0:T(8,128)(2,1)}, f32[1,1024]{1,0:T(1,128)}) custom-call(s32[1]{0:T(128)} %bitcast.2.core_ref, bf16[2,1,512,1024]{3,2,1,0:T(8,128)(2,1)} %tokens_ref.11, ...), custom_call_target="tpu_custom_call", output_to_operand_aliasing={{0}: (11, {})} | custom-call | flops 201326592 | bytes 12582912 | tf_op jit(solution)/shard_map/final_part/pallas_call | solution.py:679
  757.5 1.8 convert_add_fusion
  759.4 11.8 %attn_grads.1 = (bf16[1024,1024]{1,0:T(8,128)(2,1)}, bf16[1024,1024]{1,0:T(8,128)(2,1)}, bf16[1024,1024]{1,0:T(8,128)(2,1)}) custom-call(s32[96]{0:T(128)} %pad_add_fusion.table_ref, bf16[1024,512]{1,0:T(8,128)(2,1)} %get-tuple-element.218.refs_0_, bf16[1024,512]{1,0:T(8,128)(2,1)} %get-tuple-element.131.refs_1_, ...), custom_call_target="tpu_custom_call" | custom-call | flops 402653184 | bytes 12582912 | tf_op jit(solution)/shard_map/attn_grads/pallas_call | solution.py:736
  771.8 50.5 %reduce_rows.1 = (f32[32,1024]{1,0:T(8,128)}, f32[32,1024]{1,0:T(8,128)}, f32[32,1024]{1,0:T(8,128)}, f32[24,128]{1,0:T(8,128)}) custom-call(bf16[1024,1024]{1,0:T(8,128)(2,1)} %get-tuple-element.225.refs_0_, bf16[1024,1024]{1,0:T(8,128)(2,1)} %get-tuple-element.226.refs_1_, bf16[1024,1024]{1,0:T(8,128)(2,1)} %get-tuple-element.227.refs_2_, ...), custom_call_target="tpu_custom_call" | custom-call | tf_op jit(solution)/shard_map/reduce_rows/pallas_call | solution.py:893
  822.3 1.4 slice.160
  824.5 1.3 slice_bitcast_fusion
  825.8 1.9 slice_convert_fusion
  (143 shorter events, 23.3 us)
Async XLA Ops:
  7.2 111.2 %copy-start = (f32[16,2]{0,1:T(2,128)S(1)}, f32[16,2]{0,1:T(2,128)}, u32[]{:S(2)}) copy-start(f32[16,2]{0,1:T(2,128)} %param.29) | copy-start | bytes 388
  7.2 52.3 %all-gather.16.cloned.1.call-start = ((), (), s32[]{:S(2)}) async-start(), calls=%async_computation.20 | async-start | bytes 7864320 | tf_op jit(solution)/shard_map/all_gather | solution.py:946
  10.2 269.5 %all-gather.8.cloned.1.call-start = ((), (), s32[]{:S(2)}) async-start(), calls=%async_computation.14 | async-start | bytes 2621440 | tf_op jit(solution)/shard_map/all_gather | solution.py:937
  11.0 1.3 copy-start.16
  11.0 33.7 %copy-start.24 = (s32[2,1,512]{2,1,0:T(1,128)S(1)}, s32[2,1,512]{2,1,0:T(1,128)}, u32[]{:S(2)}) copy-start(s32[2,1,512]{2,1,0:T(1,128)} %param.23) | copy-start | bytes 12292
  11.0 268.8 %all-gather.10.cloned.1.call-start = ((), (), s32[]{:S(2)}) async-start(), calls=%async_computation.15 | async-start | bytes 10485760 | tf_op jit(solution)/shard_map/all_gather | solution.py:937
  11.7 268.0 %all-gather.12.cloned.1.call-start = ((), (), s32[]{:S(2)}) async-start(), calls=%async_computation.16 | async-start | bytes 10485760 | tf_op jit(solution)/shard_map/all_gather | solution.py:937
  44.6 1.3 collective-permute-start
  70.1 42.9 %all-to-all-start = ((bf16[8,192,512]{2,1,0:T(8,128)(2,1)}), bf16[8,192,512]{2,1,0:T(8,128)(2,1)S(1)}, u32[]{:S(2)}, u32[]{:S(2)}) async-start(bf16[8,192,512]{2,1,0:T(8,128)(2,1)} %get-tuple-element.130), calls=%async_computation | async-start | bytes 3145728 | tf_op jit(solution)/shard_map/all_to_all | solution.py:940
  75.6 204.2 %all-gather.14.cloned.1.call-start = ((), (), s32[]{:S(2)}) async-start(), calls=%async_computation.17 | async-start | bytes 10485760 | tf_op jit(solution)/shard_map/all_gather | solution.py:937
  86.8 31.1 %copy-start.25 = (s32[2,1]{0,1:T(1,128)S(1)}, s32[2,1]{0,1:T(1,128)}, u32[]{:S(2)}) copy-start(s32[2,1]{0,1:T(1,128)} %param.21) | copy-start | bytes 28
  113.0 1.2 copy-start.10
  114.2 40.8 %all-to-all-start.1 = ((bf16[8,192,512]{2,1,0:T(8,128)(2,1)}), bf16[8,192,512]{2,1,0:T(8,128)(2,1)S(1)}, u32[]{:S(2)}, u32[]{:S(2)}) async-start(bf16[8,192,512]{2,1,0:T(8,128)(2,1)} %get-tuple-element.132), calls=%async_computation.1 | async-start | bytes 3145728 | tf_op jit(solution)/shard_map/all_to_all | solution.py:940
  117.8 4.3 collective-permute-start.2
  117.9 3.0 collective-permute-start.1
  155.0 5.7 copy-start.9
  155.0 40.9 %all-to-all-start.2 = ((bf16[8,192,512]{2,1,0:T(8,128)(2,1)}), bf16[8,192,512]{2,1,0:T(8,128)(2,1)}, u32[]{:S(2)}, u32[]{:S(2)}) async-start(bf16[8,192,512]{2,1,0:T(8,128)(2,1)} %get-tuple-element.136), calls=%async_computation.2 | async-start | bytes 3145728 | tf_op jit(solution)/shard_map/all_to_all | solution.py:940
  183.2 20.8 %copy-start.12 = (bf16[8,64,512]{2,1,0:T(8,128)(2,1)S(1)}, bf16[8,64,512]{2,1,0:T(8,128)(2,1)}, u32[]{:S(2)}) copy-start(bf16[8,64,512]{2,1,0:T(8,128)(2,1)} %get-tuple-element.148.mixed_ref) | copy-start | bytes 1572868
  196.0 40.8 %all-to-all-start.3 = ((bf16[8,192,512]{2,1,0:T(8,128)(2,1)}), bf16[8,192,512]{2,1,0:T(8,128)(2,1)S(1)}, u32[]{:S(2)}, u32[]{:S(2)}) async-start(bf16[8,192,512]{2,1,0:T(8,128)(2,1)} %get-tuple-element.140), calls=%async_computation.3 | async-start | bytes 3145728 | tf_op jit(solution)/shard_map/all_to_all | solution.py:940
  199.6 5.5 collective-permute-start.3
  199.7 4.4 collective-permute-start.5
  236.8 1.2 copy-start.8
  238.0 33.4 %all-to-all-start.4 = ((bf16[8,128,512]{2,1,0:T(8,128)(2,1)}), bf16[8,128,512]{2,1,0:T(8,128)(2,1)S(1)}, u32[]{:S(2)}, u32[]{:S(2)}) async-start(bf16[8,128,512]{2,1,0:T(8,128)(2,1)} %pad_maximum_fusion.1), calls=%async_computation.4 | async-start | bytes 2097152 | tf_op jit(solution)/shard_map/all_to_all | solution.py:940
  241.9 27.4 %collective-permute-start.4 = (bf16[8,64,512]{2,1,0:T(8,128)(2,1)}, bf16[8,64,512]{2,1,0:T(8,128)(2,1)S(1)}, u32[]{:S(2)}, u32[]{:S(2)}) collective-permute-start(bf16[8,64,512]{2,1,0:T(8,128)(2,1)} %get-tuple-element.147.mixed_ref), channel_id=1, source_target_pairs={{0,8},{1,9},{2,10},{3,11},{4,12},{5,13},{6,14},{7,15},{8,0},{9,1},... | collective-permute-start | bytes 1572872 | tf_op jit(solution)/shard_map/ppermute | solution.py:950
  272.4 49.7 %all-to-all-start.5 = ((bf16[8,128,512]{2,1,0:T(8,128)(2,1)}), bf16[8,128,512]{2,1,0:T(8,128)(2,1)S(1)}, u32[]{:S(2)}, u32[]{:S(2)}) async-start(bf16[8,128,512]{2,1,0:T(8,128)(2,1)} %pad_maximum_fusion), calls=%async_computation.5 | async-start | bytes 2097152 | tf_op jit(solution)/shard_map/all_to_all | solution.py:940
  322.1 7.9 copy-start.30
  322.1 8.4 %copy-start.5 = (bf16[8,128,512]{2,1,0:T(8,128)(2,1)}, bf16[8,128,512]{2,1,0:T(8,128)(2,1)S(1)}, u32[]{:S(2)}) copy-start(bf16[8,128,512]{2,1,0:T(8,128)(2,1)S(1)} %all-to-all-done.5) | copy-start | bytes 3145732
  322.1 50.7 %all-to-all-start.6 = ((bf16[8,128,512]{2,1,0:T(8,128)(2,1)}), bf16[8,128,512]{2,1,0:T(8,128)(2,1)}, u32[]{:S(2)}, u32[]{:S(2)}) async-start(bf16[8,128,512]{2,1,0:T(8,128)(2,1)} %bitcast.60), calls=%async_computation.6 | async-start | bytes 2097152 | tf_op jit(solution)/shard_map/all_to_all | solution.py:940
  386.5 32.4 %collective-permute-start.6 = (bf16[512,4096]{1,0:T(8,128)(2,1)}, bf16[512,4096]{1,0:T(8,128)(2,1)}, u32[]{:S(2)}, u32[]{:S(2)}) collective-permute-start(bf16[512,4096]{1,0:T(8,128)(2,1)} %get-tuple-element.176), channel_id=1, source_target_pairs={{0,8},{1,9},{2,10},{3,11},{4,12},{5,13},{6,14},{7,15},{8,0},{9,1},... | collective-permute-start | bytes 12582920 | tf_op jit(solution)/shard_map/ppermute | solution.py:950
  386.5 32.4 %all-to-all-start.7 = ((bf16[8,128,512]{2,1,0:T(8,128)(2,1)}), bf16[8,128,512]{2,1,0:T(8,128)(2,1)S(1)}, u32[]{:S(2)}, u32[]{:S(2)}) async-start(bf16[8,128,512]{2,1,0:T(8,128)(2,1)} %bitcast.61), calls=%async_computation.7 | async-start | bytes 2097152 | tf_op jit(solution)/shard_map/all_to_all | solution.py:940
  392.5 260.0 %reduce-scatter.3.cloned.1.call-start = ((), (), s32[]{:S(2)}) async-start(), calls=%async_computation.18 | async-start | bytes 23592960 | tf_op jit(solution)/shard_map/reduce_scatter | solution.py:1095
  393.8 14.4 %collective-permute-start.7 = (bf16[8,64,512]{2,1,0:T(8,128)(2,1)S(1)}, bf16[8,64,512]{2,1,0:T(8,128)(2,1)}, u32[]{:S(2)}, u32[]{:S(2)}) collective-permute-start(bf16[8,64,512]{2,1,0:T(8,128)(2,1)S(1)} %slice.137), channel_id=1, source_target_pairs={{0,8},{1,9},{2,10},{3,11},{4,12},{5,13},{6,14},{7,15},{8,0},{9,1},... | collective-permute-start | bytes 1572872 | tf_op jit(solution)/shard_map/ppermute | solution.py:950
  419.0 25.2 %copy-start.7 = (bf16[8,128,512]{2,1,0:T(8,128)(2,1)}, bf16[8,128,512]{2,1,0:T(8,128)(2,1)S(1)}, u32[]{:S(2)}) copy-start(bf16[8,128,512]{2,1,0:T(8,128)(2,1)S(1)} %all-to-all-done.7.grad_ref) | copy-start | bytes 3145732
  444.1 66.0 %collective-permute-start.8 = (bf16[256,4096]{1,0:T(8,128)(2,1)}, bf16[256,4096]{1,0:T(8,128)(2,1)}, u32[]{:S(2)}, u32[]{:S(2)}) collective-permute-start(bf16[256,4096]{1,0:T(8,128)(2,1)} %get-tuple-element.258), channel_id=1, source_target_pairs={{0,16},{1,17},{2,18},{3,19},{4,20},{5,21},{6,22},{7,23},{8,24},{9,... | collective-permute-start | bytes 6291464 | tf_op jit(solution)/shard_map/ppermute | solution.py:950
  445.0 69.8 %collective-permute-start.9 = (bf16[8,64,512]{2,1,0:T(8,128)(2,1)}, bf16[8,64,512]{2,1,0:T(8,128)(2,1)}, u32[]{:S(2)}, u32[]{:S(2)}) collective-permute-start(bf16[8,64,512]{2,1,0:T(8,128)(2,1)} %slice.146), channel_id=1, source_target_pairs={{0,8},{1,9},{2,10},{3,11},{4,12},{5,13},{6,14},{7,15},{8,0},{9,1},... | collective-permute-start | bytes 1572872 | tf_op jit(solution)/shard_map/ppermute | solution.py:950
  486.9 23.2 %copy-start.2 = (bf16[256,4096]{1,0:T(8,128)(2,1)S(1)}, bf16[256,4096]{1,0:T(8,128)(2,1)}, u32[]{:S(2)}) copy-start(bf16[256,4096]{1,0:T(8,128)(2,1)} %get-tuple-element.189) | copy-start | bytes 6291460
  486.9 66.8 %all-to-all-start.8 = ((bf16[8,192,512]{2,1,0:T(8,128)(2,1)}), bf16[8,192,512]{2,1,0:T(8,128)(2,1)}, u32[]{:S(2)}, u32[]{:S(2)}) async-start(bf16[8,192,512]{2,1,0:T(8,128)(2,1)} %get-tuple-element.193), calls=%async_computation.8 | async-start | bytes 3145728 | tf_op jit(solution)/shard_map/all_to_all | solution.py:940
  513.4 37.8 %collective-permute-start.11 = (bf16[128,4096]{1,0:T(8,128)(2,1)}, bf16[128,4096]{1,0:T(8,128)(2,1)}, u32[]{:S(2)}, u32[]{:S(2)}) collective-permute-start(bf16[128,4096]{1,0:T(8,128)(2,1)} %get-tuple-element.260), channel_id=1, source_target_pairs={{0,1},{1,0},{2,3},{3,2},{4,5},{5,4},{6,7},{7,6},{8,9},{9,8},{10,11... | collective-permute-start | bytes 3145736 | tf_op jit(solution)/shard_map/ppermute | solution.py:950
  527.9 26.6 %collective-permute-start.10 = (bf16[8,192,512]{2,1,0:T(8,128)(2,1)}, bf16[8,192,512]{2,1,0:T(8,128)(2,1)S(1)}, u32[]{:S(2)}, u32[]{:S(2)}) collective-permute-start(bf16[8,192,512]{2,1,0:T(8,128)(2,1)} %get-tuple-element.192), channel_id=1, source_target_pairs={{0,8},{1,9},{2,10},{3,11},{4,12},{5,13},{6,14},{7,15},{8,0},{9,1},... | collective-permute-start | bytes 4718600 | tf_op jit(solution)/shard_map/ppermute | solution.py:950
  555.6 60.4 %all-to-all-start.9 = ((bf16[8,192,512]{2,1,0:T(8,128)(2,1)}), bf16[8,192,512]{2,1,0:T(8,128)(2,1)S(1)}, u32[]{:S(2)}, u32[]{:S(2)}) async-start(bf16[8,192,512]{2,1,0:T(8,128)(2,1)} %copy-done.11), calls=%async_computation.9 | async-start | bytes 3145728 | tf_op jit(solution)/shard_map/all_to_all | solution.py:940
  560.6 53.4 %collective-permute-start.12 = (bf16[64,4096]{1,0:T(8,128)(2,1)}, bf16[64,4096]{1,0:T(8,128)(2,1)}, u32[]{:S(2)}, u32[]{:S(2)}) collective-permute-start(bf16[64,4096]{1,0:T(8,128)(2,1)} %get-tuple-element.262), channel_id=1, source_target_pairs={{0,2},{1,3},{2,0},{3,1},{4,6},{5,7},{6,4},{7,5},{8,10},{9,11},{10,... | collective-permute-start | bytes 1572872 | tf_op jit(solution)/shard_map/ppermute | solution.py:950
  616.0 36.5 %copy-start.3 = (bf16[8,192,512]{2,1,0:T(8,128)(2,1)}, bf16[8,192,512]{2,1,0:T(8,128)(2,1)S(1)}, u32[]{:S(2)}) copy-start(bf16[8,192,512]{2,1,0:T(8,128)(2,1)S(1)} %all-to-all-done.9.rest_1_) | copy-start | bytes 4718596
  616.0 36.5 %all-to-all-start.10 = ((bf16[8,192,512]{2,1,0:T(8,128)(2,1)}), bf16[8,192,512]{2,1,0:T(8,128)(2,1)}, u32[]{:S(2)}, u32[]{:S(2)}) async-start(bf16[8,192,512]{2,1,0:T(8,128)(2,1)} %get-tuple-element.203), calls=%async_computation.10 | async-start | bytes 3145728 | tf_op jit(solution)/shard_map/all_to_all | solution.py:940
  620.6 205.2 %reduce-scatter.5.cloned.1.call-start = ((), (), s32[]{:S(2)}) async-start(), calls=%async_computation.19 | async-start | bytes 5308416 | tf_op jit(solution)/shard_map/reduce_scatter | solution.py:1211
  652.5 1.4 copy-start.29
  652.6 15.0 %copy-start.27 = (s32[32]{0:T(128)S(1)}, s32[32]{0:T(128)}, u32[]{:S(2)}) copy-start(s32[32]{0:T(128)} %constant.43.clone) | copy-start | bytes 388
  652.6 15.0 %copy-start.28 = (s32[32]{0:T(128)S(1)}, s32[32]{0:T(128)}, u32[]{:S(2)}) copy-start(s32[32]{0:T(128)} %constant.44.clone) | copy-start | bytes 388
  652.6 15.0 %copy-start.26 = (s32[32]{0:T(128)S(1)}, s32[32]{0:T(128)}, u32[]{:S(2)}) copy-start(s32[32]{0:T(128)} %broadcast_xor_fusion.2.table_ref) | copy-start | bytes 388
  652.6 15.6 %copy-start.17 = (f32[1,1024]{1,0:T(1,128)S(1)}, f32[1,1024]{1,0:T(1,128)}, u32[]{:S(2)}) copy-start(f32[1,1024]{1,0:T(1,128)} %get-tuple-element.155) | copy-start | bytes 12292
  652.6 15.6 %copy-start.18 = (f32[1,1024]{1,0:T(1,128)S(1)}, f32[1,1024]{1,0:T(1,128)}, u32[]{:S(2)}) copy-start(f32[1,1024]{1,0:T(1,128)} %get-tuple-element.164) | copy-start | bytes 12292
  652.6 15.6 %copy-start.19 = (f32[8,128]{1,0:T(8,128)S(1)}, f32[8,128]{1,0:T(8,128)}, u32[]{:S(2)}) copy-start(f32[8,128]{1,0:T(8,128)} %get-tuple-element.188) | copy-start | bytes 12292
  652.6 15.6 %copy-start.21 = (f32[8,128]{1,0:T(8,128)S(1)}, f32[8,128]{1,0:T(8,128)}, u32[]{:S(2)}) copy-start(f32[8,128]{1,0:T(8,128)} %get-tuple-element.198) | copy-start | bytes 12292
  652.7 18.6 %copy-start.20 = (f32[8,128]{1,0:T(8,128)S(1)}, f32[8,128]{1,0:T(8,128)}, u32[]{:S(2)}) copy-start(f32[8,128]{1,0:T(8,128)} %get-tuple-element.194) | copy-start | bytes 12292
  652.7 18.6 %copy-start.22 = (f32[8,128]{1,0:T(8,128)S(1)}, f32[8,128]{1,0:T(8,128)}, u32[]{:S(2)}) copy-start(f32[8,128]{1,0:T(8,128)} %get-tuple-element.204) | copy-start | bytes 12292
  653.9 7.9 collective-permute-start.13
  661.9 82.2 %all-to-all-start.11 = ((bf16[8,192,512]{2,1,0:T(8,128)(2,1)}), bf16[8,192,512]{2,1,0:T(8,128)(2,1)S(1)}, u32[]{:S(2)}, u32[]{:S(2)}) async-start(bf16[8,192,512]{2,1,0:T(8,128)(2,1)} %collective-permute-done.13), calls=%async_computation.11 | async-start | bytes 3145728 | tf_op jit(solution)/shard_map/all_to_all | solution.py:940
  668.2 89.3 %collective-permute-start.14 = (bf16[32,4096]{1,0:T(8,128)(2,1)}, bf16[32,4096]{1,0:T(8,128)(2,1)}, u32[]{:S(2)}, u32[]{:S(2)}) collective-permute-start(bf16[32,4096]{1,0:T(8,128)(2,1)} %get-tuple-element.264), channel_id=1, source_target_pairs={{0,4},{1,5},{2,6},{3,7},{4,0},{5,1},{6,2},{7,3},{8,12},{9,13},{10,... | collective-permute-start | bytes 786440 | tf_op jit(solution)/shard_map/ppermute | solution.py:950
  744.0 1.2 copy-start.4
  745.2 11.6 %copy-start.23 = (f32[1,1024]{1,0:T(1,128)S(1)}, f32[1,1024]{1,0:T(1,128)}, u32[]{:S(2)}) copy-start(f32[1,1024]{1,0:T(1,128)} %get-tuple-element.210) | copy-start | bytes 12292
  823.8 5.5 copy-start.15
  823.8 6.1 copy-start.14
  824.5 6.8 copy-start.1
  825.8 4.8 copy-start.13
  825.8 2.8 slice-start
  (2 other events, 2.2 us)
Sparse Core Ops, SparseCore 0:
  10.3 49.0 all-gather.15
  61.0 22.5 all-gather.7
  85.2 58.2 all-gather.9
  145.0 58.9 all-gather.11
  205.4 58.4 all-gather.13
  438.7 155.1 reduce-scatter.2
  652.7 141.2 reduce-scatter.4
